TPU v7x, 256 devices: a whole 4x4x8 slice. The times are simulated.
256 devices in a mesh: height: 8 (over x, core), dom: 32 (over z, y).
Axes of the slice: x: 4, y: 4, z: 8, core: 2. Of those that a mesh axis runs over, the one named last changes fastest.
Arguments:
- modes_now: float32 [64, 256, 4096], P('height', 'dom'), may hold values from -6 to 6
- modes_prev: float32 [64, 256, 4096], P('height', 'dom'), may hold values from -6 to 6
- partition_boxes: int32 [256, 2], P('dom'), may hold values from 16 to 64, as said below
- face_table: int32 [1024, 8], P('dom'), may hold values from 0 to 64, as said below
Outputs:
- new_modes: float32 [64, 256, 4096], P('height', 'dom')
- pressure: float32 [64, 256, 4096], P('height', 'dom')
Inputs may be any that keep to these rules, and one draw needn't show every extreme that they name: `partition_boxes`: column 0 is a partition's extent along x, column 1 along y. `face_table`: row r belongs to dom index r // 32. Columns: 0 the local number of the source partition on that index, 1 its side (0 low x, 1 high x, 2 low y, 3 high y), 2 the first cell of the face along that side, 3 the face's length in cells (0 marks an unused row), 4 the dom index holding the target partition, 5 the target's local number, 6 its side, 7 the first cell along it. Sides 0 and 1 run along y, sides 2 and 3 along x; start plus length never passes either side's extent. Among the rows of one dom index at most 2 name the same dom index in column 4, and that many is reached in every draw.
All inputs are finite; a program needn't handle non-finite values.
Results may differ from a plain program's by a relative error of at most 0.0002.
Values sent between devices are 32-bit elements; how exact they have to be, the bound alone decides.
No kernel may reach another device: no remote copies, remote signals or barrier semaphores. Data moves between devices by JAX's collectives and lax.ppermute only.
A program may use at most 64 MiB of HBM per device.

v0:
```python
import functools

import jax
import jax.numpy as jnp
import numpy as np
from jax import lax
from jax.experimental import pallas as pl
from jax.experimental.pallas import tpu as pltpu
from jax.sharding import PartitionSpec as P


B = 64
LANES = 128
UNROLL_A = 1
UNROLL_B = 1
RIM = 8

COUPLING = 32.0
STENCIL = (COUPLING * 270.0 / 180.0, COUPLING * -27.0 / 180.0, COUPLING * 2.0 / 180.0)
TIME_STEP = 0.4


bf16 = jnp.bfloat16
f32 = jnp.float32


def cosine(length, wave, place):
    angle = wave * (2 * place + 1)
    period = 4 * length
    turns = jnp.floor((angle.astype(f32) + 0.5) / period.astype(f32)).astype(jnp.int32)
    angle = angle - turns * period
    angle = jnp.minimum(angle, period - angle)
    x = (length - angle).astype(f32) * ((np.pi / 2) / length.astype(f32))
    y = x * x
    s = f32(-2.50521084e-8)
    for c in (2.75573192e-6, -1.98412698e-4, 8.33333333e-3, -1.66666667e-1):
        s = s * y + f32(c)
    s = x + x * y * s
    scale = jnp.sqrt(jnp.where(wave == 0, 1.0, 2.0) / length.astype(f32))
    inside = (wave < length) & (place < length) & (place >= 0)
    return jnp.where(inside, scale * s, 0.0)


def iota(shape, axis):
    return lax.broadcasted_iota(jnp.int32, shape, axis)


def rim_cell(index, extent):
    return jnp.where(index < 3, index, jnp.where(index < 6, extent + 2 - index, -1))


def split(x):
    hi = x.astype(bf16)
    lo = (x - hi.astype(f32)).astype(bf16)
    return hi, lo


def dot(a, b):
    return jnp.dot(a, b, preferred_element_type=f32)


def backward_tables(extent_rows, extent_cols):
    count = extent_rows.shape[0]
    ex = extent_rows[:, None, None]
    ey = extent_cols[:, None, None]
    shape = (count, B, LANES)
    col_back = cosine(ey, iota(shape, 2) % B, iota(shape, 1))
    row = iota(shape, 1)
    lane = iota(shape, 2)
    row_back = jnp.where(lane < B, cosine(ex, 2 * (row % 32) + row // 32, lane), 0.0)

    def edge(extent, wave, index):
        layer = index % 3
        total = jnp.zeros(wave.shape, f32)
        for i in range(3):
            cell = jnp.where(index < 3, i, extent - 1 - i)
            weight = jnp.where(
                i + layer == 0,
                STENCIL[0],
                jnp.where(i + layer == 1, STENCIL[1], jnp.where(i + layer == 2, STENCIL[2], 0.0)),
            )
            total = total + weight * cosine(extent, wave, cell)
        return jnp.where(index < 6, total, 0.0)

    shape = (count, 32, LANES)
    lane = iota(shape, 2)
    edge_rows = edge(ex, 2 * iota(shape, 1) + (lane // 8) % 2, lane % 8)
    shape = (count, 16, LANES)
    row = iota(shape, 1)
    lane = iota(shape, 2)
    edge_cols = jnp.where(row // 8 == lane // B, edge(ey, lane % B, row % 8), 0.0)
    return col_back, row_back, edge_rows, edge_cols


def cosine_tile(length, wave, place):
    size = jnp.full((1, LANES), length, jnp.int32).astype(f32)
    unit = 1.0 / size
    angle = wave * (2.0 * place + 1.0)
    angle = angle - jnp.floor((angle + 0.5) * (0.25 * unit)) * (4.0 * size)
    angle = jnp.minimum(angle, 4.0 * size - angle)
    x = (size - angle) * (f32(np.pi / 2) * unit)
    y = x * x
    s = f32(-2.50521084e-8)
    for c in (2.75573192e-6, -1.98412698e-4, 8.33333333e-3, -1.66666667e-1):
        s = s * y + f32(c)
    s = x + x * y * s
    s = s * jnp.where(wave == 0.0, jnp.sqrt(unit), jnp.sqrt(2.0 * unit))
    return jnp.where((wave < size) & (place < size) & (place >= 0.0), s, 0.0)


def cells_kernel(
    planes, mine_ref, box_ref, face_ref, x_ref, piece_ref, rim_ref, pay_ref, used_ref, table_ref
):
    mine = mine_ref[0]
    holders = box_ref.shape[0]
    lane = iota((B, LANES), 1)
    low = lane < B
    low32 = iota((32, LANES), 1) < B
    low8 = iota((8, LANES), 1) < B
    row64 = iota((B, LANES), 0).astype(f32)
    x_wave = 2 * (lane % 32) + (lane // 32) % 2
    x_wave64 = x_wave.astype(f32)
    x_wave8 = x_wave[:8].astype(f32)

    def one(p, carry):
        x = jnp.concatenate(
            [x_ref[pl.ds(kz * 256 + p, 32, stride=8), :] for kz in range(planes)], 0
        )
        ex = box_ref[p, 0]
        ey = box_ref[p, 1]
        c = cosine_tile(
            ey, row64, jnp.where(low, lane, rim_cell(lane - B, ey)).astype(f32)
        )
        spot = pl.multiple_of(p * B, B)
        g = cosine_tile(ex, x_wave64, row64)
        table_ref[pl.ds(spot, B), :] = g
        edge = cosine_tile(ex, x_wave8, rim_cell(iota((8, LANES), 0), ex).astype(f32))
        rows = jnp.concatenate(
            [
                table_ref[pl.ds(spot, 32, stride=2), :],
                pltpu.roll(table_ref[pl.ds(spot + 1, 32, stride=2), :], 32, 1),
                edge,
                jnp.zeros((8, LANES), f32),
                g,
                jnp.zeros((B, LANES), f32),
            ],
            0,
        )
        turned = pltpu.roll(c, B, 1)
        c = jnp.concatenate(
            [
                jnp.concatenate([jnp.where(low, c, 0.0), jnp.where(low, turned, 0.0)], 1),
                jnp.concatenate([jnp.where(low, 0.0, turned), jnp.where(low, 0.0, c)], 1),
            ],
            0,
        )
        c_hi, c_lo = split(c)
        x_hi, x_lo = split(x)
        t = dot(
            jnp.concatenate([x_hi, x_hi, x_lo], 1), jnp.concatenate([c_hi, c_lo, c_hi], 0)
        )
        main = [t[kz * 32 : (kz + 1) * 32, :LANES] for kz in range(planes)]
        rims = t[0:32, LANES:]
        for kz in range(1, planes):
            rims = rims + pltpu.roll(t[kz * 32 : (kz + 1) * 32, LANES:], kz * RIM, 1)
        main.append(rims)
        upper = jnp.concatenate(main, 1)
        lower = jnp.concatenate([pltpu.roll(m, B, 1) for m in main], 1)
        r_hi, r_lo = split(jnp.concatenate([upper, lower], 0))
        right = jnp.concatenate([r_hi, r_lo, r_hi, r_lo], 0)
        l_hi, l_lo = split(rows)
        l_lo = jnp.where(iota((208, LANES), 1) < B, l_lo, jnp.zeros_like(l_lo))
        left = jnp.concatenate([l_hi, l_lo], 1)
        y = dot(left[:80], right[:, : planes * LANES])
        z = dot(left[80:], right[:, planes * LANES :])
        for kz in range(planes):
            tile = y[:, kz * LANES : (kz + 1) * LANES]
            out = jnp.where(low32, tile[:32], tile[32:64])
            for g in range(8):
                spot = (mine ^ g) * 256 + kz * 32 + p
                piece_ref[pl.ds(spot, 4, stride=8), :] = out[g * 4 : (g + 1) * 4]
            rim_ref[pl.ds(pl.multiple_of(p * 128 + kz * RIM, RIM), RIM), :] = jnp.where(
                low8, tile[64:72], 0.0
            )
        rim_ref[pl.ds(pl.multiple_of(p * 128 + 64, 64), 64), :] = z.T[:64]
        return carry

    lax.fori_loop(0, holders, one, 0, unroll=UNROLL_A)

    pay_ref[...] = jnp.zeros_like(pay_ref)
    targets = pay_ref.shape[0] // 32

    def clear(t, carry):
        used_ref[t] = 0
        return carry

    lax.fori_loop(0, targets, clear, 0)

    def face(r, carry):
        length = face_ref[r, 3]

        @pl.when(length > 0)
        def _():
            side = face_ref[r, 1]
            start = face_ref[r, 2]
            target = face_ref[r, 4]
            code = face_ref[r, 5] * 4 + face_ref[r, 6] + 1
            slot = used_ref[target]
            used_ref[target] = slot + 1
            first = slot * B + face_ref[r, 7]
            turn = (first - start + LANES) & (LANES - 1)
            base = face_ref[r, 0] * 128 + (side >> 1) * 64 + (side & 1) * 3
            lane = iota((RIM, LANES), 1)
            here = (lane >= first) & (lane < first + length)
            for j in range(3):
                values = rim_ref[pl.ds(base + j, planes, stride=RIM), :]
                values = jnp.where(here, pltpu.roll(values, turn, 1), 0.0)
                rows = pl.ds(pl.multiple_of(target * 32 + j * 8, 8), 8)
                pay_ref[rows, :] = pay_ref[rows, :] + values
            rows = pl.ds(pl.multiple_of(target * 32 + 24, 8), 8)
            pay_ref[rows, :] = pay_ref[rows, :] + jnp.where(here, code, 0).astype(f32)

        return carry

    lax.fori_loop(0, face_ref.shape[0], face, 0)


def depth_kernel(planes, table_ref, *refs):
    blocks, out_ref = refs[:-1], refs[-1]
    count = len(blocks)
    total = count * planes
    t_hi, t_lo = split(table_ref[...])
    t_lo = jnp.where(iota((total, LANES), 1) < total, t_lo, jnp.zeros_like(t_lo))
    left = jnp.concatenate([t_hi, t_lo], 1)
    for q in range(4):
        right = jnp.concatenate(
            [
                jnp.concatenate(
                    [b[pl.ds(q * 8 + p, planes, stride=32), :] for b in blocks], 0
                )
                for p in range(8)
            ],
            1,
        )
        r_hi, r_lo = split(right)
        mixed = dot(left, jnp.concatenate([r_hi, r_lo, r_hi, r_lo], 0))
        for p in range(8):
            for s in range(count):
                out_ref[pl.ds(s * 256 + q * 8 + p, planes, stride=32), :] = mixed[
                    s * planes : (s + 1) * planes, p * LANES : (p + 1) * LANES
                ]


def advance_kernel(
    planes,
    total,
    code_ref,
    mine_ref,
    box_ref,
    got_ref,
    rim_ref,
    now_ref,
    prev_ref,
    col_ref,
    row_ref,
    edge_row_ref,
    edge_col_ref,
    out_ref,
    sum_ref,
    times_ref,
):
    holders = col_ref.shape[0]
    sum_ref[...] = jnp.zeros_like(sum_ref)
    times_ref[...] = jnp.zeros_like(times_ref)

    def gather(k, carry):
        code = code_ref[k]

        @pl.when(code > 0)
        def _():
            source = k >> 1
            turn = (k & 1) * B
            which = code - 1
            tile = which >> 1
            first = (which & 1) * 3
            marks = pltpu.roll(got_ref[pl.ds(pl.multiple_of(source * 32 + 24, 8), 8), :], turn, 1)
            here = (marks == code.astype(f32)) & (iota((RIM, LANES), 1) < B)
            for j in range(3):
                values = got_ref[pl.ds(pl.multiple_of(source * 32 + j * 8, 8), 8), :]
                values = jnp.where(here, pltpu.roll(values, turn, 1), 0.0)
                rows = pl.ds(tile * 64 + first + j, planes, stride=RIM)
                sum_ref[rows, :] = sum_ref[rows, :] + values
            row = iota((RIM, LANES), 0)
            hit = here & (row >= first) & (row < first + 3)
            rows = pl.ds(pl.multiple_of(tile * RIM, RIM), RIM)
            times_ref[rows, :] = times_ref[rows, :] + jnp.where(hit, 1.0, 0.0)

        return carry

    lax.fori_loop(0, code_ref.shape[0], gather, 0)
    first_plane = mine_ref[0] * planes

    def one(p, carry):
        jumps = []
        for axis in range(2):
            rows = pl.ds(pl.multiple_of((p * 2 + axis) * 64, 64), 64)
            times = times_ref[pl.ds(pl.multiple_of((p * 2 + axis) * RIM, RIM), RIM), :]
            times = jnp.concatenate([times] * planes, 0)
            jumps.append(split(sum_ref[rows, :] - times * rim_ref[rows, :]))
        j_hi, j_lo = jumps[0]
        c_hi, c_lo = split(jnp.concatenate([col_ref[p], jnp.zeros((B, LANES), f32)], 0))
        along_y = dot(
            jnp.concatenate([j_hi, j_hi, j_lo], 1), jnp.concatenate([c_hi, c_lo, c_hi], 0)
        )
        j_hi, j_lo = jumps[1]
        r_hi, r_lo = split(row_ref[p])
        along_x = lax.dot_general(
            jnp.concatenate([r_hi, r_lo, r_hi], 1),
            jnp.concatenate([j_hi, j_hi, j_lo], 1),
            (((1,), (1,)), ((), ())),
            preferred_element_type=f32,
        )
        along_x = jnp.concatenate([along_x, along_x], 1)
        even, odd = along_x[:32], along_x[32:]
        lane = iota((32, LANES), 1)
        edge = edge_row_ref[p]
        left = []
        for kz in range(planes):
            across = jnp.where(lane // 16 == kz, edge, 0.0)
            back = (LANES - kz * RIM) % LANES
            low = pltpu.roll(even, back, 1) if back else even
            high = pltpu.roll(odd, (back + RIM) % LANES, 1)
            down = jnp.where(lane < RIM, low, jnp.where(lane < 2 * RIM, high, 0.0))
            left.append(jnp.concatenate([across, down], 1))
        left = jnp.concatenate(left, 0)
        half = iota((RIM, LANES), 1) < B
        right = []
        for kz in range(planes):
            tile = along_y[kz * RIM : (kz + 1) * RIM]
            right += [jnp.where(half, tile, 0.0), jnp.where(half, 0.0, tile)]
        right += [edge_col_ref[p], jnp.zeros((LANES - 2 * RIM, LANES), f32)]
        right = jnp.concatenate(right, 0)
        l_hi, l_lo = split(left)
        r_hi, r_lo = split(right)
        force = dot(l_hi, r_hi) + dot(l_hi, r_lo) + dot(l_lo, r_hi)
        ex = box_ref[p, 0]
        ey = box_ref[p, 1]
        wave_x = 2 * iota((32, LANES), 0) + lane // B
        wave_y = lane % B
        inside = (wave_x < ex) & (wave_y < ey)
        unit = TIME_STEP * np.pi
        scale_x = unit / jnp.full((32, LANES), ex, jnp.int32).astype(f32)
        scale_y = unit / jnp.full((32, LANES), ey, jnp.int32).astype(f32)
        flat = (wave_x.astype(f32) * scale_x) ** 2 + (wave_y.astype(f32) * scale_y) ** 2
        for kz in range(planes):
            depth = (first_plane + kz).astype(f32) * (unit / total)
            u = flat + depth * depth
            s = f32(-2.0 / 6402373705728000.0)
            for c in (
                2.0 / 20922789888000.0,
                -2.0 / 87178291200.0,
                2.0 / 479001600.0,
                -2.0 / 3628800.0,
                2.0 / 40320.0,
                -2.0 / 720.0,
                2.0 / 24.0,
            ):
                s = s * u + f32(c)
            s = 1.0 - u * s
            rows = pl.ds(kz * 256 + p, 32, stride=8)
            new = (2.0 - u * s) * now_ref[rows, :] - prev_ref[rows, :]
            new = new + (TIME_STEP * TIME_STEP) * s * force[kz * 32 : (kz + 1) * 32]
            out_ref[rows, :] = jnp.where(inside, new, 0.0)
        return carry

    lax.fori_loop(0, holders, one, 0, unroll=UNROLL_B)


def join_kernel(planes, mine_ref, *refs):
    blocks, out_ref = refs[:-1], refs[-1]
    mine = mine_ref[0]
    for s, block in enumerate(blocks):
        for z in range(planes):
            spot = pl.multiple_of((mine ^ s) * 32 + z * 256, 32)
            out_ref[pl.ds(spot, 32), :] = block[z * 32 : (z + 1) * 32, :]


VM = pl.BlockSpec(memory_space=pltpu.VMEM)
SM = pl.BlockSpec(memory_space=pltpu.SMEM)


def call(kernel, args, spots, outs, scratch=(), flops=10**8):
    return pl.pallas_call(
        kernel,
        out_shape=outs,
        in_specs=spots,
        out_specs=jax.tree.map(lambda _: VM, outs),
        scratch_shapes=list(scratch),
        compiler_params=pltpu.CompilerParams(vmem_limit_bytes=40 * 2**20),
        cost_estimate=pl.CostEstimate(flops=flops, bytes_accessed=4 * 2**20, transcendentals=0),
    )(*args)


def swap(block, step):
    count = lax.axis_size("height")
    return lax.ppermute(block, "height", [(i, i ^ step) for i in range(count)])


def tiles(field):
    planes, holders, cells = field.shape
    split_up = field.reshape(planes, holders, cells // LANES, LANES).transpose(0, 2, 1, 3)
    return split_up.reshape(-1, LANES)


def untiles(rows, planes, holders):
    cells = rows.shape[0] // (planes * holders)
    folded = rows.reshape(planes, cells, holders, LANES).transpose(0, 2, 1, 3)
    return folded.reshape(planes, holders, cells * LANES)


def step(modes_now, modes_prev, partition_boxes, face_table):
    planes, holders, _ = modes_now.shape
    count = lax.axis_size("height")
    domains = lax.axis_size("dom")
    total = planes * count
    mine = lax.axis_index("height").astype(jnp.int32)
    extent_rows = partition_boxes[:, 0]
    extent_cols = partition_boxes[:, 1]
    now = tiles(modes_now)
    prev = tiles(modes_prev)
    mine_word = mine.reshape(1)

    def rows(n):
        return jax.ShapeDtypeStruct((n, LANES), f32)

    pieces, rim, pay = call(
        functools.partial(cells_kernel, planes),
        (mine_word, partition_boxes, face_table, now),
        [SM, SM, SM, VM],
        (rows(2048), rows(holders * 128), rows(domains * 32)),
        [pltpu.SMEM((domains,), jnp.int32), pltpu.VMEM((holders * B, LANES), f32)],
    )
    pieces = pieces.reshape(count, 256, LANES)
    got = [pieces[0]] + [swap(pieces[s], s) for s in range(1, count)]
    arrived = lax.all_to_all(pay.reshape(domains, 32, LANES), "dom", 0, 0, tiled=True)

    order = (mine ^ jnp.arange(count, dtype=jnp.int32))[:, None] * planes
    order = (order + jnp.arange(planes, dtype=jnp.int32)).reshape(-1)
    depth_table = cosine(jnp.full((), total, jnp.int32), order[None, :], order[:, None])
    depth_table = jnp.concatenate([depth_table, depth_table], 1)
    mixed = call(
        functools.partial(depth_kernel, planes), (depth_table, *got), [VM] * (1 + count), rows(2048)
    )
    mixed = mixed.reshape(count, 256, LANES)
    back = [mixed[0]] + [swap(mixed[s], s) for s in range(1, count)]

    codes = jnp.max(arrived[:, 24].reshape(domains * 2, B), 1).astype(jnp.int32)
    new = call(
        functools.partial(advance_kernel, planes, total),
        (codes, mine_word, partition_boxes, arrived.reshape(-1, LANES), rim, now, prev)
        + tuple(backward_tables(extent_rows, extent_cols)),
        [SM] * 3 + [VM] * 8,
        rows(2048),
        [pltpu.VMEM((holders * 128, LANES), f32), pltpu.VMEM((holders * 2 * RIM, LANES), f32)],
    )
    pressure = call(
        functools.partial(join_kernel, planes), (mine_word, *back), [SM] + [VM] * count, rows(2048)
    )
    pressure = untiles(pressure, planes, holders)
    return untiles(new, planes, holders), pressure


def solution(mesh):
    placed = (P("height", "dom", None), P("height", "dom", None), P("dom", None), P("dom", None))
    return jax.shard_map(
        step,
        mesh=mesh,
        in_specs=placed,
        out_specs=(P("height", "dom", None), P("height", "dom", None)),
        check_vma=False,
    )
```

profile of v0, /device:TPU:1, one launch (start us, length us, event | category | flops | bytes accessed | tf_op | source)
XLA Modules:
  0.0 71.3 jit_solution(15846830697260154020)
XLA Ops:
  0.6 0.0 copy-start.5
  0.6 0.0 copy-start.6
  0.7 0.7 copy-done.5
  1.3 0.1 copy.6.box_ref
  1.4 0.0 copy-done.6
  1.4 0.1 copy.7.face_ref
  1.5 0.0 copy-start
  1.5 1.2 %copy-done = f32[8,8,4096]{2,1,0:T(8,128)S(1)} copy-done((f32[8,8,4096]{2,1,0:T(8,128)S(1)}, f32[8,8,4096]{2,1,0:T(8,128)}, u32[]{:S(2)}) %copy-start) | copy-done | bytes 1048600
  2.7 9.9 %shard_map.59 = (f32[2048,128]{1,0:T(8,128)S(1)}, f32[1024,128]{1,0:T(8,128)S(1)}, f32[1024,128]{1,0:T(8,128)}) custom-call(s32[1]{0:T(128)} %bitcast.mine_ref, s32[8,2]{1,0:T(8,128)S(1)} %copy.6.box_ref, s32[32,8]{1,0:T(8,128)S(1)} %copy.7.face_ref, f32[2048,128]{1,0:T(8,128)S(1)} %bitcast.55), custom_call_target="tpu_custom_call" | custom-call | flops 100000000 | bytes 4194304 | tf_op jit(solution)/shard_map/pallas_call | solution.py:393
  12.6 0.0 copy-start.3
  12.6 0.1 fusion.204
  12.7 0.7 %copy-done.3 = f32[1024,128]{1,0:T(8,128)} copy-done((f32[1024,128]{1,0:T(8,128)}, f32[1024,128]{1,0:T(8,128)S(1)}, u32[]{:S(2)}) %copy-start.3) | copy-done | bytes 524312
  13.4 3.2 %collective-permute-start = (f32[256,128]{1,0:T(8,128)S(1)}, f32[256,128]{1,0:T(8,128)S(1)}, u32[]{:S(2)}, u32[]{:S(2)}) collective-permute-start(f32[256,128]{1,0:T(8,128)S(1)} %get-tuple-element.22), channel_id=1, source_target_pairs={{0,32},{32,0},{64,96},{96,64},{128,160},{160,128},{192,224},{224,1... | collective-permute-start | bytes 393224 | tf_op jit(solution)/shard_map/ppermute | solution.py:406
  16.6 0.0 collective-permute-start.1
  16.6 1.6 %collective-permute-start.2 = (f32[256,128]{1,0:T(8,128)S(1)}, f32[256,128]{1,0:T(8,128)S(1)}, u32[]{:S(2)}, u32[]{:S(2)}) collective-permute-start(f32[256,128]{1,0:T(8,128)S(1)} %get-tuple-element.20), channel_id=1, source_target_pairs={{0,96},{32,64},{64,32},{96,0},{128,224},{160,192},{192,160},{224,1... | collective-permute-start | bytes 393224 | tf_op jit(solution)/shard_map/ppermute | solution.py:406
  18.2 1.0 %collective-permute-start.3 = (f32[256,128]{1,0:T(8,128)S(1)}, f32[256,128]{1,0:T(8,128)S(1)}, u32[]{:S(2)}, u32[]{:S(2)}) collective-permute-start(f32[256,128]{1,0:T(8,128)S(1)} %get-tuple-element.19), channel_id=1, source_target_pairs={{0,128},{32,160},{64,192},{96,224},{128,0},{160,32},{192,64},{224,... | collective-permute-start | bytes 393224 | tf_op jit(solution)/shard_map/ppermute | solution.py:406
  19.3 2.3 %collective-permute-start.4 = (f32[256,128]{1,0:T(8,128)S(1)}, f32[256,128]{1,0:T(8,128)S(1)}, u32[]{:S(2)}, u32[]{:S(2)}) collective-permute-start(f32[256,128]{1,0:T(8,128)S(1)} %get-tuple-element.18), channel_id=1, source_target_pairs={{0,160},{32,128},{64,224},{96,192},{128,32},{160,0},{192,96},{224,... | collective-permute-start | bytes 393224 | tf_op jit(solution)/shard_map/ppermute | solution.py:406
  21.6 9.5 %all-to-all-start = ((f32[32,32,128]{2,1,0:T(8,128)}), f32[32,32,128]{2,1,0:T(8,128)S(1)}, u32[]{:S(2)}, u32[]{:S(2)}) async-start(f32[32,32,128]{2,1,0:T(8,128)} %bitcast.4), calls=%async_computation | async-start | bytes 1048576 | tf_op jit(solution)/shard_map/all_to_all | solution.py:445
  31.1 0.1 iota_add_fusion
  31.2 0.1 add.544
  31.5 0.3 fusion.5.col_ref
  31.8 0.4 fusion.14.row_ref
  32.3 0.7 fusion.45.edge_row_ref
  32.9 0.1 fusion.184
  33.1 0.0 collective-permute-done.refs_1_
  33.1 2.6 %collective-permute-start.5 = (f32[256,128]{1,0:T(8,128)S(1)}, f32[256,128]{1,0:T(8,128)S(1)}, u32[]{:S(2)}, u32[]{:S(2)}) collective-permute-start(f32[256,128]{1,0:T(8,128)S(1)} %get-tuple-element.17), channel_id=1, source_target_pairs={{0,192},{32,224},{64,128},{96,160},{128,64},{160,96},{192,0},{224,... | collective-permute-start | bytes 393224 | tf_op jit(solution)/shard_map/ppermute | solution.py:406
  35.6 0.0 collective-permute-done.1.refs_2_
  35.6 0.7 collective-permute-start.6
  36.3 0.1 pad_maximum_fusion.table_ref
  36.4 0.0 collective-permute-done.2.refs_3_
  36.4 0.0 collective-permute-done.3.refs_4_
  36.4 0.0 collective-permute-done.4.refs_5_
  36.4 2.8 %collective-permute-done.5.refs_6_ = f32[256,128]{1,0:T(8,128)S(1)} collective-permute-done((f32[256,128]{1,0:T(8,128)S(1)}, f32[256,128]{1,0:T(8,128)S(1)}, u32[]{:S(2)}, u32[]{:S(2)}) %collective-permute-start.5) | collective-permute-done | bytes 131104 | tf_op jit(solution)/shard_map/ppermute | solution.py:406
  39.1 3.7 %collective-permute-done.6.refs_7_ = f32[256,128]{1,0:T(8,128)S(1)} collective-permute-done((f32[256,128]{1,0:T(8,128)S(1)}, f32[256,128]{1,0:T(8,128)S(1)}, u32[]{:S(2)}, u32[]{:S(2)}) %collective-permute-start.6) | collective-permute-done | bytes 131104 | tf_op jit(solution)/shard_map/ppermute | solution.py:406
  42.8 1.3 %shard_map.61 = f32[2048,128]{1,0:T(8,128)S(1)} custom-call(f32[64,128]{1,0:T(8,128)S(1)} %pad_maximum_fusion.table_ref, f32[256,128]{1,0:T(8,128)S(1)} %get-tuple-element.23.refs_0_, f32[256,128]{1,0:T(8,128)S(1)} %collective-permute-done.refs_1_, f32[256,128]{1,0:T(8,128)S(1)} %collective-permute-done.1.refs_2_, ...), custom_call_target="tpu_custom_call" | custom-call | flops 100000000 | bytes 4194304 | tf_op jit(solution)/shard_map/pallas_call | solution.py:393
  44.1 0.1 fusion.203
  44.2 1.5 %collective-permute-start.10 = (f32[256,128]{1,0:T(8,128)S(1)}, f32[256,128]{1,0:T(8,128)S(1)}, u32[]{:S(2)}, u32[]{:S(2)}) collective-permute-start(f32[256,128]{1,0:T(8,128)S(1)} %get-tuple-element.11), channel_id=1, source_target_pairs={{0,128},{32,160},{64,192},{96,224},{128,0},{160,32},{192,64},{224,... | collective-permute-start | bytes 393224 | tf_op jit(solution)/shard_map/ppermute | solution.py:406
  45.7 2.0 %collective-permute-start.11 = (f32[256,128]{1,0:T(8,128)S(1)}, f32[256,128]{1,0:T(8,128)S(1)}, u32[]{:S(2)}, u32[]{:S(2)}) collective-permute-start(f32[256,128]{1,0:T(8,128)S(1)} %get-tuple-element.10), channel_id=1, source_target_pairs={{0,160},{32,128},{64,224},{96,192},{128,32},{160,0},{192,96},{224,... | collective-permute-start | bytes 393224 | tf_op jit(solution)/shard_map/ppermute | solution.py:406
  47.7 1.7 %collective-permute-start.12 = (f32[256,128]{1,0:T(8,128)S(1)}, f32[256,128]{1,0:T(8,128)S(1)}, u32[]{:S(2)}, u32[]{:S(2)}) collective-permute-start(f32[256,128]{1,0:T(8,128)S(1)} %get-tuple-element.9), channel_id=1, source_target_pairs={{0,192},{32,224},{64,128},{96,160},{128,64},{160,96},{192,0},{224,... | collective-permute-start | bytes 393224 | tf_op jit(solution)/shard_map/ppermute | solution.py:406
  49.4 1.1 %collective-permute-start.13 = (f32[256,128]{1,0:T(8,128)S(1)}, f32[256,128]{1,0:T(8,128)S(1)}, u32[]{:S(2)}, u32[]{:S(2)}) collective-permute-start(f32[256,128]{1,0:T(8,128)S(1)} %get-tuple-element.8), channel_id=1, source_target_pairs={{0,224},{32,192},{64,160},{96,128},{128,96},{160,64},{192,32},{224... | collective-permute-start | bytes 393224 | tf_op jit(solution)/shard_map/ppermute | solution.py:406
  50.5 0.3 collective-permute-start.7
  50.7 0.0 collective-permute-done.10.refs_4_
  50.8 0.5 collective-permute-start.8
  51.2 2.7 %collective-permute-done.11.refs_5_ = f32[256,128]{1,0:T(8,128)S(1)} collective-permute-done((f32[256,128]{1,0:T(8,128)S(1)}, f32[256,128]{1,0:T(8,128)S(1)}, u32[]{:S(2)}, u32[]{:S(2)}) %collective-permute-start.11) | collective-permute-done | bytes 131104 | tf_op jit(solution)/shard_map/ppermute | solution.py:406
  53.9 0.2 collective-permute-start.9
  54.1 0.4 fusion.114.edge_col_ref
  54.5 2.4 %collective-permute-done.12.refs_6_ = f32[256,128]{1,0:T(8,128)S(1)} collective-permute-done((f32[256,128]{1,0:T(8,128)S(1)}, f32[256,128]{1,0:T(8,128)S(1)}, u32[]{:S(2)}, u32[]{:S(2)}) %collective-permute-start.12) | collective-permute-done | bytes 131104 | tf_op jit(solution)/shard_map/ppermute | solution.py:406
  56.9 2.8 %collective-permute-done.13.refs_7_ = f32[256,128]{1,0:T(8,128)S(1)} collective-permute-done((f32[256,128]{1,0:T(8,128)S(1)}, f32[256,128]{1,0:T(8,128)S(1)}, u32[]{:S(2)}, u32[]{:S(2)}) %collective-permute-start.13) | collective-permute-done | bytes 131104 | tf_op jit(solution)/shard_map/ppermute | solution.py:406
  59.7 0.0 collective-permute-done.7.refs_1_
  59.7 0.0 collective-permute-done.8.refs_2_
  59.7 0.0 collective-permute-done.9.refs_3_
  59.7 0.0 copy-start.1
  59.7 0.0 copy-start.2
  59.7 1.0 %shard_map.62 = f32[2048,128]{1,0:T(8,128)} custom-call(s32[1]{0:T(128)} %bitcast.mine_ref, f32[256,128]{1,0:T(8,128)S(1)} %get-tuple-element.15.refs_0_, f32[256,128]{1,0:T(8,128)S(1)} %collective-permute-done.7.refs_1_, f32[256,128]{1,0:T(8,128)S(1)} %collective-permute-done.8.refs_2_, f32[256,128]{1,0:T(8,128)S(1)} %collective-permute-done.9.refs_3_, ...), custom_call_target="tpu_custom_call" | custom-call | flops 100000000 | bytes 4194304 | tf_op jit(solution)/shard_map/pallas_call | solution.py:393
  60.8 0.0 all-to-all-done
  60.8 0.1 reshape_squeeze.3
  60.9 0.1 reduce_max.9
  61.0 0.3 copy-done.1
  61.3 0.3 copy-done.2
  61.6 0.0 copy-start.4
  61.6 1.0 %copy-done.4 = f32[1024,128]{1,0:T(8,128)S(1)} copy-done((f32[1024,128]{1,0:T(8,128)S(1)}, f32[1024,128]{1,0:T(8,128)}, u32[]{:S(2)}) %copy-start.4) | copy-done | bytes 524312
  62.7 8.7 %shard_map.60 = f32[2048,128]{1,0:T(8,128)} custom-call(s32[64]{0:T(128)S(1)} %convert_element_type.142.code_ref, s32[1]{0:T(128)} %bitcast.mine_ref, s32[8,2]{1,0:T(8,128)S(1)} %copy.6.box_ref, f32[1024,128]{1,0:T(8,128)S(1)} %bitcast.57, f32[1024,128]{1,0:T(8,128)S(1)} %copy-done.4, f32[2048,128]{1,0:T(8,128)S(1)} %bitcast.56, f32[2048,128]{1,0:T(8,128)S(1)} %bitcast.58, ...), custom_call_target="tpu_custom_call" | custom-call | flops 100000000 | bytes 4194304 | tf_op jit(solution)/shard_map/pallas_call | solution.py:393
  (25 shorter events, 0.2 us)
Async XLA Ops:
  0.6 0.7 copy-start.5
  0.6 0.8 %copy-start.6 = (s32[32,8]{0,1:T(8,128)S(1)}, s32[32,8]{0,1:T(8,128)}, u32[]{:S(2)}) copy-start(s32[32,8]{0,1:T(8,128)} %param.7) | copy-start | bytes 3076
  1.5 1.2 %copy-start = (f32[8,8,4096]{2,1,0:T(8,128)S(1)}, f32[8,8,4096]{2,1,0:T(8,128)}, u32[]{:S(2)}) copy-start(f32[8,8,4096]{2,1,0:T(8,128)} %param.4) | copy-start | bytes 3145732
  12.6 0.8 %copy-start.3 = (f32[1024,128]{1,0:T(8,128)}, f32[1024,128]{1,0:T(8,128)S(1)}, u32[]{:S(2)}) copy-start(f32[1024,128]{1,0:T(8,128)S(1)} %get-tuple-element.6.rim_ref) | copy-start | bytes 1572868
  13.4 19.7 %collective-permute-start = (f32[256,128]{1,0:T(8,128)S(1)}, f32[256,128]{1,0:T(8,128)S(1)}, u32[]{:S(2)}, u32[]{:S(2)}) collective-permute-start(f32[256,128]{1,0:T(8,128)S(1)} %get-tuple-element.22), channel_id=1, source_target_pairs={{0,32},{32,0},{64,96},{96,64},{128,160},{160,128},{192,224},{224,1... | collective-permute-start | bytes 393224 | tf_op jit(solution)/shard_map/ppermute | solution.py:406
  16.6 19.0 %collective-permute-start.1 = (f32[256,128]{1,0:T(8,128)S(1)}, f32[256,128]{1,0:T(8,128)S(1)}, u32[]{:S(2)}, u32[]{:S(2)}) collective-permute-start(f32[256,128]{1,0:T(8,128)S(1)} %get-tuple-element.21), channel_id=1, source_target_pairs={{0,64},{32,96},{64,0},{96,32},{128,192},{160,224},{192,128},{224,1... | collective-permute-start | bytes 393224 | tf_op jit(solution)/shard_map/ppermute | solution.py:406
  16.6 19.8 %collective-permute-start.2 = (f32[256,128]{1,0:T(8,128)S(1)}, f32[256,128]{1,0:T(8,128)S(1)}, u32[]{:S(2)}, u32[]{:S(2)}) collective-permute-start(f32[256,128]{1,0:T(8,128)S(1)} %get-tuple-element.20), channel_id=1, source_target_pairs={{0,96},{32,64},{64,32},{96,0},{128,224},{160,192},{192,160},{224,1... | collective-permute-start | bytes 393224 | tf_op jit(solution)/shard_map/ppermute | solution.py:406
  18.2 18.2 %collective-permute-start.3 = (f32[256,128]{1,0:T(8,128)S(1)}, f32[256,128]{1,0:T(8,128)S(1)}, u32[]{:S(2)}, u32[]{:S(2)}) collective-permute-start(f32[256,128]{1,0:T(8,128)S(1)} %get-tuple-element.19), channel_id=1, source_target_pairs={{0,128},{32,160},{64,192},{96,224},{128,0},{160,32},{192,64},{224,... | collective-permute-start | bytes 393224 | tf_op jit(solution)/shard_map/ppermute | solution.py:406
  19.3 17.1 %collective-permute-start.4 = (f32[256,128]{1,0:T(8,128)S(1)}, f32[256,128]{1,0:T(8,128)S(1)}, u32[]{:S(2)}, u32[]{:S(2)}) collective-permute-start(f32[256,128]{1,0:T(8,128)S(1)} %get-tuple-element.18), channel_id=1, source_target_pairs={{0,160},{32,128},{64,224},{96,192},{128,32},{160,0},{192,96},{224,... | collective-permute-start | bytes 393224 | tf_op jit(solution)/shard_map/ppermute | solution.py:406
  21.6 39.2 %all-to-all-start = ((f32[32,32,128]{2,1,0:T(8,128)}), f32[32,32,128]{2,1,0:T(8,128)S(1)}, u32[]{:S(2)}, u32[]{:S(2)}) async-start(f32[32,32,128]{2,1,0:T(8,128)} %bitcast.4), calls=%async_computation | async-start | bytes 1048576 | tf_op jit(solution)/shard_map/all_to_all | solution.py:445
  33.1 6.1 %collective-permute-start.5 = (f32[256,128]{1,0:T(8,128)S(1)}, f32[256,128]{1,0:T(8,128)S(1)}, u32[]{:S(2)}, u32[]{:S(2)}) collective-permute-start(f32[256,128]{1,0:T(8,128)S(1)} %get-tuple-element.17), channel_id=1, source_target_pairs={{0,192},{32,224},{64,128},{96,160},{128,64},{160,96},{192,0},{224,... | collective-permute-start | bytes 393224 | tf_op jit(solution)/shard_map/ppermute | solution.py:406
  35.6 7.2 %collective-permute-start.6 = (f32[256,128]{1,0:T(8,128)S(1)}, f32[256,128]{1,0:T(8,128)S(1)}, u32[]{:S(2)}, u32[]{:S(2)}) collective-permute-start(f32[256,128]{1,0:T(8,128)S(1)} %get-tuple-element.16), channel_id=1, source_target_pairs={{0,224},{32,192},{64,160},{96,128},{128,96},{160,64},{192,32},{224... | collective-permute-start | bytes 393224 | tf_op jit(solution)/shard_map/ppermute | solution.py:406
  44.2 6.6 %collective-permute-start.10 = (f32[256,128]{1,0:T(8,128)S(1)}, f32[256,128]{1,0:T(8,128)S(1)}, u32[]{:S(2)}, u32[]{:S(2)}) collective-permute-start(f32[256,128]{1,0:T(8,128)S(1)} %get-tuple-element.11), channel_id=1, source_target_pairs={{0,128},{32,160},{64,192},{96,224},{128,0},{160,32},{192,64},{224,... | collective-permute-start | bytes 393224 | tf_op jit(solution)/shard_map/ppermute | solution.py:406
  45.7 8.2 %collective-permute-start.11 = (f32[256,128]{1,0:T(8,128)S(1)}, f32[256,128]{1,0:T(8,128)S(1)}, u32[]{:S(2)}, u32[]{:S(2)}) collective-permute-start(f32[256,128]{1,0:T(8,128)S(1)} %get-tuple-element.10), channel_id=1, source_target_pairs={{0,160},{32,128},{64,224},{96,192},{128,32},{160,0},{192,96},{224,... | collective-permute-start | bytes 393224 | tf_op jit(solution)/shard_map/ppermute | solution.py:406
  47.7 9.2 %collective-permute-start.12 = (f32[256,128]{1,0:T(8,128)S(1)}, f32[256,128]{1,0:T(8,128)S(1)}, u32[]{:S(2)}, u32[]{:S(2)}) collective-permute-start(f32[256,128]{1,0:T(8,128)S(1)} %get-tuple-element.9), channel_id=1, source_target_pairs={{0,192},{32,224},{64,128},{96,160},{128,64},{160,96},{192,0},{224,... | collective-permute-start | bytes 393224 | tf_op jit(solution)/shard_map/ppermute | solution.py:406
  49.4 10.3 %collective-permute-start.13 = (f32[256,128]{1,0:T(8,128)S(1)}, f32[256,128]{1,0:T(8,128)S(1)}, u32[]{:S(2)}, u32[]{:S(2)}) collective-permute-start(f32[256,128]{1,0:T(8,128)S(1)} %get-tuple-element.8), channel_id=1, source_target_pairs={{0,224},{32,192},{64,160},{96,128},{128,96},{160,64},{192,32},{224... | collective-permute-start | bytes 393224 | tf_op jit(solution)/shard_map/ppermute | solution.py:406
  50.5 9.2 %collective-permute-start.7 = (f32[256,128]{1,0:T(8,128)S(1)}, f32[256,128]{1,0:T(8,128)S(1)}, u32[]{:S(2)}, u32[]{:S(2)}) collective-permute-start(f32[256,128]{1,0:T(8,128)S(1)} %get-tuple-element.14), channel_id=1, source_target_pairs={{0,32},{32,0},{64,96},{96,64},{128,160},{160,128},{192,224},{224,1... | collective-permute-start | bytes 393224 | tf_op jit(solution)/shard_map/ppermute | solution.py:406
  50.8 8.9 %collective-permute-start.8 = (f32[256,128]{1,0:T(8,128)S(1)}, f32[256,128]{1,0:T(8,128)S(1)}, u32[]{:S(2)}, u32[]{:S(2)}) collective-permute-start(f32[256,128]{1,0:T(8,128)S(1)} %get-tuple-element.13), channel_id=1, source_target_pairs={{0,64},{32,96},{64,0},{96,32},{128,192},{160,224},{192,128},{224,1... | collective-permute-start | bytes 393224 | tf_op jit(solution)/shard_map/ppermute | solution.py:406
  53.9 5.8 %collective-permute-start.9 = (f32[256,128]{1,0:T(8,128)S(1)}, f32[256,128]{1,0:T(8,128)S(1)}, u32[]{:S(2)}, u32[]{:S(2)}) collective-permute-start(f32[256,128]{1,0:T(8,128)S(1)} %get-tuple-element.12), channel_id=1, source_target_pairs={{0,96},{32,64},{64,32},{96,0},{128,224},{160,192},{192,160},{224,1... | collective-permute-start | bytes 393224 | tf_op jit(solution)/shard_map/ppermute | solution.py:406
  59.7 1.6 %copy-start.1 = (f32[8,8,4096]{2,1,0:T(8,128)S(1)}, f32[8,8,4096]{2,1,0:T(8,128)}, u32[]{:S(2)}) copy-start(f32[8,8,4096]{2,1,0:T(8,128)} %param.4) | copy-start | bytes 3145732
  59.7 1.9 %copy-start.2 = (f32[8,8,4096]{2,1,0:T(8,128)S(1)}, f32[8,8,4096]{2,1,0:T(8,128)}, u32[]{:S(2)}) copy-start(f32[8,8,4096]{2,1,0:T(8,128)} %param.5) | copy-start | bytes 3145732
  61.6 1.0 %copy-start.4 = (f32[1024,128]{1,0:T(8,128)S(1)}, f32[1024,128]{1,0:T(8,128)}, u32[]{:S(2)}) copy-start(f32[1024,128]{1,0:T(8,128)} %copy-done.3) | copy-start | bytes 1572868
where the time goes:
time: 71.7 us; the launch traced here: 71.3 us
  starting transfers between devices  28.1 us (39%)
  Pallas kernels  20.9 us (29%)
  waiting for transfers between devices  14.3 us (20%)
  local copies, waits for them, and re-layouts  4.77 us (7%)
  other arithmetic  2.33 us (3%)
  between operations  0.91 us (1%)
    pallas_call x4, Pallas kernels, call(): pl.pallas_call(kernel, out_shape=outs, in_specs=spots, out_specs=jax.tree...  20.9 us
    ppermute x14, starting transfers between devices, swap(): return lax.ppermute(block, 'height', [(i, i ^ step) for i in range(count)])  18.6 us
    ppermute x14, waiting for transfers between devices, swap(): return lax.ppermute(block, 'height', [(i, i ^ step) for i in range(count)])  14.3 us
    all_to_all x1, starting transfers between devices, step(): lax.all_to_all(pay.reshape(domains, 32, LANES), 'dom', 0, 0, tiled=True)  9.48 us
    unnamed x16, local copies, waits for them, and re-layouts  4.43 us
  transfers between devices with their start and end apart: 15, of which 5 were waited for; matrix products, arithmetic and copies ran while one was open for 3% of the time, Pallas kernels for 3%

commit v1 on v0

--- a/solution.py
+++ b/solution.py
@@ -11,13 +11,20 @@
 
 B = 64
 LANES = 128
-UNROLL_A = 1
-UNROLL_B = 1
+FACE_ROWS = 25
 RIM = 8
 
 COUPLING = 32.0
 STENCIL = (COUPLING * 270.0 / 180.0, COUPLING * -27.0 / 180.0, COUPLING * 2.0 / 180.0)
 TIME_STEP = 0.4
+WAVE = (
+    0.9999999998806415,
+    -0.08333333151883045,
+    0.002777773302928117,
+    -4.959913250130888e-05,
+    5.494915434656933e-07,
+    -3.861085658928547e-09,
+)
 
 
 bf16 = jnp.bfloat16
@@ -109,28 +116,51 @@
 
 
 def cells_kernel(
-    planes, mine_ref, box_ref, face_ref, x_ref, piece_ref, rim_ref, pay_ref, used_ref, table_ref
+    planes,
+    mine_ref,
+    box_ref,
+    x_hbm,
+    piece_ref,
+    rim_ref,
+    x_ref,
+    table_ref,
+    c_hi_ref,
+    c_lo_ref,
+    l_hi_ref,
+    l_lo_ref,
+    even_hi_ref,
+    even_lo_ref,
+    odd_hi_ref,
+    odd_lo_ref,
+    sem,
 ):
     mine = mine_ref[0]
     holders = box_ref.shape[0]
+    fetch = pltpu.make_async_copy(x_hbm, x_ref, sem)
+    fetch.start()
+    low32 = iota((32, LANES), 1) < B
+    low8 = iota((8, LANES), 1) < B
     lane = iota((B, LANES), 1)
     low = lane < B
-    low32 = iota((32, LANES), 1) < B
-    low8 = iota((8, LANES), 1) < B
     row64 = iota((B, LANES), 0).astype(f32)
     x_wave = 2 * (lane % 32) + (lane // 32) % 2
     x_wave64 = x_wave.astype(f32)
     x_wave8 = x_wave[:8].astype(f32)
-
-    def one(p, carry):
-        x = jnp.concatenate(
-            [x_ref[pl.ds(kz * 256 + p, 32, stride=8), :] for kz in range(planes)], 0
-        )
+    l_low = iota((144, LANES), 1) < B
+
+    def tables(p, carry):
         ex = box_ref[p, 0]
         ey = box_ref[p, 1]
-        c = cosine_tile(
-            ey, row64, jnp.where(low, lane, rim_cell(lane - B, ey)).astype(f32)
-        )
+        c = cosine_tile(ey, row64, jnp.where(low, lane, rim_cell(lane - B, ey)).astype(f32))
+        turned = pltpu.roll(c, B, 1)
+        c = jnp.concatenate(
+            [
+                jnp.concatenate([jnp.where(low, c, 0.0), jnp.where(low, turned, 0.0)], 1),
+                jnp.concatenate([jnp.where(low, 0.0, turned), jnp.where(low, 0.0, c)], 1),
+            ],
+            0,
+        )
+        c_hi_ref[p], c_lo_ref[p] = split(c)
         spot = pl.multiple_of(p * B, B)
         g = cosine_tile(ex, x_wave64, row64)
         table_ref[pl.ds(spot, B), :] = g
@@ -142,19 +172,22 @@
                 edge,
                 jnp.zeros((8, LANES), f32),
                 g,
-                jnp.zeros((B, LANES), f32),
             ],
             0,
         )
-        turned = pltpu.roll(c, B, 1)
-        c = jnp.concatenate(
-            [
-                jnp.concatenate([jnp.where(low, c, 0.0), jnp.where(low, turned, 0.0)], 1),
-                jnp.concatenate([jnp.where(low, 0.0, turned), jnp.where(low, 0.0, c)], 1),
-            ],
-            0,
-        )
-        c_hi, c_lo = split(c)
+        l_hi, l_lo = split(rows)
+        l_hi_ref[p] = l_hi
+        l_lo_ref[p] = jnp.where(l_low, l_lo, jnp.zeros_like(l_lo))
+        return carry
+
+    lax.fori_loop(0, holders, tables, 0)
+    fetch.wait()
+
+    def along_y(p, r_hi_ref, r_lo_ref):
+        x = jnp.concatenate(
+            [x_ref[pl.ds(kz * 256 + p, 32, stride=8), :] for kz in range(planes)], 0
+        )
+        c_hi, c_lo = c_hi_ref[p], c_lo_ref[p]
         x_hi, x_lo = split(x)
         t = dot(
             jnp.concatenate([x_hi, x_hi, x_lo], 1), jnp.concatenate([c_hi, c_lo, c_hi], 0)
@@ -164,13 +197,15 @@
         for kz in range(1, planes):
             rims = rims + pltpu.roll(t[kz * 32 : (kz + 1) * 32, LANES:], kz * RIM, 1)
         main.append(rims)
-        upper = jnp.concatenate(main, 1)
-        lower = jnp.concatenate([pltpu.roll(m, B, 1) for m in main], 1)
-        r_hi, r_lo = split(jnp.concatenate([upper, lower], 0))
+        for i, part in enumerate(main):
+            hi, lo = split(jnp.concatenate([part, pltpu.roll(part, B, 1)], 0))
+            r_hi_ref[:, i * LANES : (i + 1) * LANES] = hi
+            r_lo_ref[:, i * LANES : (i + 1) * LANES] = lo
+
+    def along_x(p, r_hi_ref, r_lo_ref):
+        r_hi, r_lo = r_hi_ref[...], r_lo_ref[...]
         right = jnp.concatenate([r_hi, r_lo, r_hi, r_lo], 0)
-        l_hi, l_lo = split(rows)
-        l_lo = jnp.where(iota((208, LANES), 1) < B, l_lo, jnp.zeros_like(l_lo))
-        left = jnp.concatenate([l_hi, l_lo], 1)
+        left = jnp.concatenate([l_hi_ref[p], l_lo_ref[p]], 1)
         y = dot(left[:80], right[:, : planes * LANES])
         z = dot(left[80:], right[:, planes * LANES :])
         for kz in range(planes):
@@ -182,13 +217,27 @@
             rim_ref[pl.ds(pl.multiple_of(p * 128 + kz * RIM, RIM), RIM), :] = jnp.where(
                 low8, tile[64:72], 0.0
             )
-        rim_ref[pl.ds(pl.multiple_of(p * 128 + 64, 64), 64), :] = z.T[:64]
+        rim_ref[pl.ds(pl.multiple_of(p * 128 + 64, 64), 64), :] = jnp.concatenate(
+            [z.T[:64], jnp.zeros((64, 64), f32)], 1
+        )
+
+    even = (even_hi_ref, even_lo_ref)
+    odd = (odd_hi_ref, odd_lo_ref)
+
+    def two(i, carry):
+        along_y(2 * i, *even)
+        along_x(jnp.maximum(2 * i - 1, 0), *odd)
+        along_y(2 * i + 1, *odd)
+        along_x(2 * i, *even)
         return carry
 
-    lax.fori_loop(0, holders, one, 0, unroll=UNROLL_A)
-
+    lax.fori_loop(0, holders // 2, two, 0)
+    along_x(holders - 1, *odd)
+
+
+def pack_kernel(planes, face_ref, rim_ref, pay_hbm, used_ref, pay_ref, sem):
     pay_ref[...] = jnp.zeros_like(pay_ref)
-    targets = pay_ref.shape[0] // 32
+    targets = pay_ref.shape[0] // FACE_ROWS
 
     def clear(t, carry):
         used_ref[t] = 0
@@ -215,19 +264,22 @@
             for j in range(3):
                 values = rim_ref[pl.ds(base + j, planes, stride=RIM), :]
                 values = jnp.where(here, pltpu.roll(values, turn, 1), 0.0)
-                rows = pl.ds(pl.multiple_of(target * 32 + j * 8, 8), 8)
+                rows = pl.ds(target * FACE_ROWS + j * planes, planes)
                 pay_ref[rows, :] = pay_ref[rows, :] + values
-            rows = pl.ds(pl.multiple_of(target * 32 + 24, 8), 8)
-            pay_ref[rows, :] = pay_ref[rows, :] + jnp.where(here, code, 0).astype(f32)
+            rows = pl.ds(target * FACE_ROWS + 3 * planes, 1)
+            pay_ref[rows, :] = pay_ref[rows, :] + jnp.where(here[:1], code, 0).astype(f32)
 
         return carry
 
     lax.fori_loop(0, face_ref.shape[0], face, 0)
+    send = pltpu.make_async_copy(pay_ref, pay_hbm, sem)
+    send.start()
+    send.wait()
 
 
 def depth_kernel(planes, table_ref, *refs):
-    blocks, out_ref = refs[:-1], refs[-1]
-    count = len(blocks)
+    count = len(refs) // 2
+    blocks, outs = refs[:count], refs[count:]
     total = count * planes
     t_hi, t_lo = split(table_ref[...])
     t_lo = jnp.where(iota((total, LANES), 1) < total, t_lo, jnp.zeros_like(t_lo))
@@ -246,7 +298,7 @@
         mixed = dot(left, jnp.concatenate([r_hi, r_lo, r_hi, r_lo], 0))
         for p in range(8):
             for s in range(count):
-                out_ref[pl.ds(s * 256 + q * 8 + p, planes, stride=32), :] = mixed[
+                outs[s][pl.ds(q * 8 + p, planes, stride=32), :] = mixed[
                     s * planes : (s + 1) * planes, p * LANES : (p + 1) * LANES
                 ]
 
@@ -254,13 +306,12 @@
 def advance_kernel(
     planes,
     total,
-    code_ref,
     mine_ref,
     box_ref,
     got_ref,
     rim_ref,
-    now_ref,
-    prev_ref,
+    now_hbm,
+    prev_hbm,
     col_ref,
     row_ref,
     edge_row_ref,
@@ -268,13 +319,40 @@
     out_ref,
     sum_ref,
     times_ref,
+    now_ref,
+    prev_ref,
+    label_ref,
+    code_ref,
+    even_down_ref,
+    even_hi_ref,
+    even_lo_ref,
+    odd_down_ref,
+    odd_hi_ref,
+    odd_lo_ref,
+    sems,
 ):
     holders = col_ref.shape[0]
+    fetches = [
+        pltpu.make_async_copy(now_hbm, now_ref, sems.at[0]),
+        pltpu.make_async_copy(prev_hbm, prev_ref, sems.at[1]),
+    ]
+    for copy in fetches:
+        copy.start()
+    sources = got_ref.shape[0] // FACE_ROWS
+    labels = got_ref[pl.ds(3 * planes, sources, stride=FACE_ROWS), :]
+    place = iota((sources, LANES), 1)
+    first = jnp.max(jnp.where(place < B, labels, 0.0), 1, keepdims=True)
+    second = jnp.max(jnp.where(place < B, 0.0, labels), 1, keepdims=True)
+    label_ref[...] = jnp.where(place == 0, first, second).astype(jnp.int32)
+    to_scalars = pltpu.make_async_copy(label_ref, code_ref, sems.at[2])
+    to_scalars.start()
     sum_ref[...] = jnp.zeros_like(sum_ref)
     times_ref[...] = jnp.zeros_like(times_ref)
 
+    to_scalars.wait()
+
     def gather(k, carry):
-        code = code_ref[k]
+        code = code_ref[k >> 1, k & 1]
 
         @pl.when(code > 0)
         def _():
@@ -283,10 +361,12 @@
             which = code - 1
             tile = which >> 1
             first = (which & 1) * 3
-            marks = pltpu.roll(got_ref[pl.ds(pl.multiple_of(source * 32 + 24, 8), 8), :], turn, 1)
+            base = source * FACE_ROWS
+            marks = got_ref[pl.ds(base + 3 * planes, 1), :]
+            marks = pltpu.roll(jnp.broadcast_to(marks, (RIM, LANES)), turn, 1)
             here = (marks == code.astype(f32)) & (iota((RIM, LANES), 1) < B)
             for j in range(3):
-                values = got_ref[pl.ds(pl.multiple_of(source * 32 + j * 8, 8), 8), :]
+                values = got_ref[pl.ds(base + j * planes, planes), :]
                 values = jnp.where(here, pltpu.roll(values, turn, 1), 0.0)
                 rows = pl.ds(tile * 64 + first + j, planes, stride=RIM)
                 sum_ref[rows, :] = sum_ref[rows, :] + values
@@ -297,10 +377,12 @@
 
         return carry
 
-    lax.fori_loop(0, code_ref.shape[0], gather, 0)
+    lax.fori_loop(0, 2 * sources, gather, 0)
     first_plane = mine_ref[0] * planes
-
-    def one(p, carry):
+    lane = iota((32, LANES), 1)
+    half = iota((RIM, LANES), 1) < B
+
+    def faces(p, down_ref, right_hi_ref, right_lo_ref):
         jumps = []
         for axis in range(2):
             rows = pl.ds(pl.multiple_of((p * 2 + axis) * 64, 64), 64)
@@ -320,84 +402,99 @@
             (((1,), (1,)), ((), ())),
             preferred_element_type=f32,
         )
-        along_x = jnp.concatenate([along_x, along_x], 1)
-        even, odd = along_x[:32], along_x[32:]
-        lane = iota((32, LANES), 1)
-        edge = edge_row_ref[p]
-        left = []
-        for kz in range(planes):
-            across = jnp.where(lane // 16 == kz, edge, 0.0)
-            back = (LANES - kz * RIM) % LANES
-            low = pltpu.roll(even, back, 1) if back else even
-            high = pltpu.roll(odd, (back + RIM) % LANES, 1)
-            down = jnp.where(lane < RIM, low, jnp.where(lane < 2 * RIM, high, 0.0))
-            left.append(jnp.concatenate([across, down], 1))
-        left = jnp.concatenate(left, 0)
-        half = iota((RIM, LANES), 1) < B
-        right = []
+        down_ref[...] = jnp.concatenate([along_x[:32], along_x[32:]], 1)
         for kz in range(planes):
             tile = along_y[kz * RIM : (kz + 1) * RIM]
-            right += [jnp.where(half, tile, 0.0), jnp.where(half, 0.0, tile)]
-        right += [edge_col_ref[p], jnp.zeros((LANES - 2 * RIM, LANES), f32)]
-        right = jnp.concatenate(right, 0)
-        l_hi, l_lo = split(left)
-        r_hi, r_lo = split(right)
-        force = dot(l_hi, r_hi) + dot(l_hi, r_lo) + dot(l_lo, r_hi)
+            both = jnp.concatenate([jnp.where(half, tile, 0.0), jnp.where(half, 0.0, tile)], 0)
+            spot = slice(kz * 2 * RIM, (kz + 1) * 2 * RIM)
+            right_hi_ref[spot], right_lo_ref[spot] = split(both)
+
+    def finish(p, down_ref, right_hi_ref, right_lo_ref):
+        edge_hi, edge_lo = split(edge_row_ref[p])
+        down_hi, down_lo = split(down_ref[...])
+        left_hi = []
+        left_lo = []
+        for kz in range(planes):
+            near = jnp.where(lane // 16 == kz, 1.0, 0.0).astype(bf16)
+            far = jnp.where((lane // RIM) % planes == kz, 1.0, 0.0).astype(bf16)
+            left_hi.append(jnp.concatenate([edge_hi * near, down_hi * far], 1))
+            left_lo.append(jnp.concatenate([edge_lo * near, down_lo * far], 1))
+        left_hi = jnp.concatenate(left_hi, 0)
+        left_lo = jnp.concatenate(left_lo, 0)
+        edges = edge_col_ref[p]
+        edges = jnp.concatenate([edges[:RIM]] * planes + [edges[RIM:]] * planes, 0)
+        edges_hi, edges_lo = split(edges)
+        right_hi = jnp.concatenate([right_hi_ref[...], edges_hi], 0)
+        right_lo = jnp.concatenate([right_lo_ref[...], edges_lo], 0)
+        force = dot(
+            jnp.concatenate([left_hi, left_hi, left_lo], 1),
+            jnp.concatenate([right_hi, right_lo, right_hi], 0),
+        )
         ex = box_ref[p, 0]
         ey = box_ref[p, 1]
         wave_x = 2 * iota((32, LANES), 0) + lane // B
         wave_y = lane % B
         inside = (wave_x < ex) & (wave_y < ey)
         unit = TIME_STEP * np.pi
-        scale_x = unit / jnp.full((32, LANES), ex, jnp.int32).astype(f32)
-        scale_y = unit / jnp.full((32, LANES), ey, jnp.int32).astype(f32)
+        scale_x = unit / jnp.full((1, LANES), ex, jnp.int32).astype(f32)
+        scale_y = unit / jnp.full((1, LANES), ey, jnp.int32).astype(f32)
         flat = (wave_x.astype(f32) * scale_x) ** 2 + (wave_y.astype(f32) * scale_y) ** 2
         for kz in range(planes):
             depth = (first_plane + kz).astype(f32) * (unit / total)
             u = flat + depth * depth
-            s = f32(-2.0 / 6402373705728000.0)
-            for c in (
-                2.0 / 20922789888000.0,
-                -2.0 / 87178291200.0,
-                2.0 / 479001600.0,
-                -2.0 / 3628800.0,
-                2.0 / 40320.0,
-                -2.0 / 720.0,
-                2.0 / 24.0,
-            ):
+            s = f32(WAVE[-1])
+            for c in WAVE[-2::-1]:
                 s = s * u + f32(c)
-            s = 1.0 - u * s
             rows = pl.ds(kz * 256 + p, 32, stride=8)
             new = (2.0 - u * s) * now_ref[rows, :] - prev_ref[rows, :]
-            new = new + (TIME_STEP * TIME_STEP) * s * force[kz * 32 : (kz + 1) * 32]
+            new = new + s * (force[kz * 32 : (kz + 1) * 32] * (TIME_STEP * TIME_STEP))
             out_ref[rows, :] = jnp.where(inside, new, 0.0)
+
+    def two(i, carry):
+        faces(2 * i, *even)
+        finish(jnp.maximum(2 * i - 1, 0), *odd)
+        faces(2 * i + 1, *odd)
+        finish(2 * i, *even)
         return carry
 
-    lax.fori_loop(0, holders, one, 0, unroll=UNROLL_B)
-
-
-def join_kernel(planes, mine_ref, *refs):
-    blocks, out_ref = refs[:-1], refs[-1]
+    for copy in fetches:
+        copy.wait()
+    even = (even_down_ref, even_hi_ref, even_lo_ref)
+    odd = (odd_down_ref, odd_hi_ref, odd_lo_ref)
+    for ref in odd:
+        ref[...] = jnp.zeros_like(ref)
+    lax.fori_loop(0, holders // 2, two, 0)
+    finish(holders - 1, *odd)
+
+
+def join_kernel(mine_ref, *refs):
+    count = (len(refs) - 2)
+    blocks, out_ref, sems = refs[:count], refs[count], refs[count + 1]
     mine = mine_ref[0]
+    copies = []
     for s, block in enumerate(blocks):
-        for z in range(planes):
-            spot = pl.multiple_of((mine ^ s) * 32 + z * 256, 32)
-            out_ref[pl.ds(spot, 32), :] = block[z * 32 : (z + 1) * 32, :]
-
-
+        spot = pl.multiple_of((mine ^ s) * 32, 32)
+        copies.append(pltpu.make_async_copy(block, out_ref.at[:, pl.ds(spot, 32), :], sems.at[s]))
+    for copy in copies:
+        copy.start()
+    for copy in copies:
+        copy.wait()
+
+
+HB = pl.BlockSpec(memory_space=pltpu.HBM)
 VM = pl.BlockSpec(memory_space=pltpu.VMEM)
 SM = pl.BlockSpec(memory_space=pltpu.SMEM)
 
 
-def call(kernel, args, spots, outs, scratch=(), flops=10**8):
+def call(kernel, args, spots, outs, scratch=(), spot=VM):
     return pl.pallas_call(
         kernel,
         out_shape=outs,
         in_specs=spots,
-        out_specs=jax.tree.map(lambda _: VM, outs),
+        out_specs=tuple(spot) if isinstance(spot, list) else jax.tree.map(lambda _: spot, outs),
         scratch_shapes=list(scratch),
-        compiler_params=pltpu.CompilerParams(vmem_limit_bytes=40 * 2**20),
-        cost_estimate=pl.CostEstimate(flops=flops, bytes_accessed=4 * 2**20, transcendentals=0),
+        compiler_params=pltpu.CompilerParams(vmem_limit_bytes=16 * 2**20),
+        cost_estimate=pl.CostEstimate(flops=10**8, bytes_accessed=4 * 2**20, transcendentals=0),
     )(*args)
 
 
@@ -426,47 +523,91 @@
     mine = lax.axis_index("height").astype(jnp.int32)
     extent_rows = partition_boxes[:, 0]
     extent_cols = partition_boxes[:, 1]
-    now = tiles(modes_now)
-    prev = tiles(modes_prev)
+    now = pltpu.with_memory_space_constraint(tiles(modes_now), pltpu.HBM)
+    prev = pltpu.with_memory_space_constraint(tiles(modes_prev), pltpu.HBM)
     mine_word = mine.reshape(1)
 
     def rows(n):
         return jax.ShapeDtypeStruct((n, LANES), f32)
 
-    pieces, rim, pay = call(
+    pieces, rim = call(
         functools.partial(cells_kernel, planes),
-        (mine_word, partition_boxes, face_table, now),
-        [SM, SM, SM, VM],
-        (rows(2048), rows(holders * 128), rows(domains * 32)),
-        [pltpu.SMEM((domains,), jnp.int32), pltpu.VMEM((holders * B, LANES), f32)],
+        (mine_word, partition_boxes, now),
+        [SM, SM, HB],
+        (rows(2048), rows(holders * 128)),
+        [
+            pltpu.VMEM((2048, LANES), f32),
+            pltpu.VMEM((holders * B, LANES), f32),
+            pltpu.VMEM((holders, LANES, 2 * LANES), bf16),
+            pltpu.VMEM((holders, LANES, 2 * LANES), bf16),
+            pltpu.VMEM((holders, 144, LANES), bf16),
+            pltpu.VMEM((holders, 144, LANES), bf16),
+            pltpu.VMEM((B, (planes + 1) * LANES), bf16),
+            pltpu.VMEM((B, (planes + 1) * LANES), bf16),
+            pltpu.VMEM((B, (planes + 1) * LANES), bf16),
+            pltpu.VMEM((B, (planes + 1) * LANES), bf16),
+            pltpu.SemaphoreType.DMA,
+        ],
+    )
+    pay = call(
+        functools.partial(pack_kernel, planes),
+        (face_table, rim),
+        [SM, VM],
+        rows(domains * FACE_ROWS),
+        [
+            pltpu.SMEM((domains,), jnp.int32),
+            pltpu.VMEM((domains * FACE_ROWS, LANES), f32),
+            pltpu.SemaphoreType.DMA,
+        ],
+        spot=HB,
     )
     pieces = pieces.reshape(count, 256, LANES)
     got = [pieces[0]] + [swap(pieces[s], s) for s in range(1, count)]
-    arrived = lax.all_to_all(pay.reshape(domains, 32, LANES), "dom", 0, 0, tiled=True)
+    arrived = lax.all_to_all(pay.reshape(-1, 1, LANES), "dom", 0, 0, tiled=True)
 
     order = (mine ^ jnp.arange(count, dtype=jnp.int32))[:, None] * planes
     order = (order + jnp.arange(planes, dtype=jnp.int32)).reshape(-1)
     depth_table = cosine(jnp.full((), total, jnp.int32), order[None, :], order[:, None])
     depth_table = jnp.concatenate([depth_table, depth_table], 1)
     mixed = call(
-        functools.partial(depth_kernel, planes), (depth_table, *got), [VM] * (1 + count), rows(2048)
+        functools.partial(depth_kernel, planes),
+        (depth_table, *got),
+        [VM] * (1 + count),
+        (rows(256),) * count,
     )
-    mixed = mixed.reshape(count, 256, LANES)
     back = [mixed[0]] + [swap(mixed[s], s) for s in range(1, count)]
 
-    codes = jnp.max(arrived[:, 24].reshape(domains * 2, B), 1).astype(jnp.int32)
     new = call(
         functools.partial(advance_kernel, planes, total),
-        (codes, mine_word, partition_boxes, arrived.reshape(-1, LANES), rim, now, prev)
+        (mine_word, partition_boxes, arrived.reshape(-1, LANES), rim, now, prev)
         + tuple(backward_tables(extent_rows, extent_cols)),
-        [SM] * 3 + [VM] * 8,
+        [SM] * 2 + [VM] * 2 + [HB] * 2 + [VM] * 4,
         rows(2048),
-        [pltpu.VMEM((holders * 128, LANES), f32), pltpu.VMEM((holders * 2 * RIM, LANES), f32)],
+        [
+            pltpu.VMEM((holders * 128, LANES), f32),
+            pltpu.VMEM((holders * 2 * RIM, LANES), f32),
+            pltpu.VMEM((2048, LANES), f32),
+            pltpu.VMEM((2048, LANES), f32),
+            pltpu.VMEM((domains, LANES), jnp.int32),
+            pltpu.SMEM((domains, LANES), jnp.int32),
+        ]
+        + [
+            pltpu.VMEM((32, LANES), f32),
+            pltpu.VMEM((LANES, LANES), bf16),
+            pltpu.VMEM((LANES, LANES), bf16),
+        ]
+        * 2
+        + [pltpu.SemaphoreType.DMA((3,))],
     )
     pressure = call(
-        functools.partial(join_kernel, planes), (mine_word, *back), [SM] + [VM] * count, rows(2048)
+        join_kernel,
+        (mine_word, *[b.reshape(planes, 32, LANES) for b in back]),
+        [SM] + [VM] * count,
+        jax.ShapeDtypeStruct((planes, 256, LANES), f32),
+        [pltpu.SemaphoreType.DMA((count,))],
+        spot=HB,
     )
-    pressure = untiles(pressure, planes, holders)
+    pressure = untiles(pressure.reshape(-1, LANES), planes, holders)
     return untiles(new, planes, holders), pressure
 
 

time: 71.7 us -> 67.8 us (0.946)
  local copies, waits for them, and re-layouts: 4.77 us -> 0.99 us
  starting transfers between devices: 28.1 us -> 31.2 us
  Pallas kernels: 20.9 us -> 18.6 us
    unnamed x16 -> x6, local copies, waits for them, and re-layouts: 4.43 us -> 0.83 us
    pallas_call x4 -> x5, Pallas kernels: 20.9 us -> 18.6 us  [call(): pl.pallas_call(kernel, out_shape=outs, in_specs=spots, out_specs=tuple(sp...]
    all_to_all x1, starting transfers between devices: 9.48 us -> 11.2 us  [step(): arrived = lax.all_to_all(pay.reshape(-1, 1, LANES), 'dom', 0, 0, tiled=True)]
    ppermute x14, starting transfers between devices: 18.6 us -> 20 us  [swap(): return lax.ppermute(block, 'height', [(i, i ^ step) for i in range(count)])]
  transfers between devices with their start and end apart: 15 -> 15, of which waited for: 5 -> 5; matrix products, arithmetic and copies ran while one was open for 3% -> 4% of each run, Pallas kernels for 3% -> 9%
where the time goes in v1:
time: 67.8 us; the launch traced here: 67.6 us
  starting transfers between devices  31.2 us (46%)
  Pallas kernels  18.6 us (27%)
  waiting for transfers between devices  13.7 us (20%)
  other arithmetic  2.21 us (3%)
  local copies, waits for them, and re-layouts  0.99 us (1%)
  between operations  0.91 us (1%)
    ppermute x14, starting transfers between devices, swap(): return lax.ppermute(block, 'height', [(i, i ^ step) for i in range(count)])  20 us
    pallas_call x5, Pallas kernels, call(): pl.pallas_call(kernel, out_shape=outs, in_specs=spots, out_specs=tuple(sp...  18.6 us
    ppermute x14, waiting for transfers between devices, swap(): return lax.ppermute(block, 'height', [(i, i ^ step) for i in range(count)])  13.7 us
    all_to_all x1, starting transfers between devices, step(): arrived = lax.all_to_all(pay.reshape(-1, 1, LANES), 'dom', 0, 0, tiled=True)  11.2 us
  transfers between devices with their start and end apart: 15, of which 5 were waited for; matrix products, arithmetic and copies ran while one was open for 4% of the time, Pallas kernels for 9%

profile of v1, /device:TPU:1, one launch (start us, length us, event | category | flops | bytes accessed | tf_op | source)
XLA Modules:
  0.0 67.6 jit_solution(14677694547055763707)
XLA Ops:
  0.6 0.0 copy-start
  0.6 0.7 copy-done
  1.3 0.1 copy.12.box_ref
  1.4 5.2 %shard_map.59 = (f32[2048,128]{1,0:T(8,128)S(1)}, f32[1024,128]{1,0:T(8,128)S(1)}) custom-call(s32[1]{0:T(128)} %bitcast.mine_ref, s32[8,2]{1,0:T(8,128)S(1)} %copy.12.box_ref, f32[2048,128]{1,0:T(8,128)} %bitcast.74), custom_call_target="tpu_custom_call" | custom-call | flops 100000000 | bytes 4194304 | tf_op jit(solution)/shard_map/pallas_call | solution.py:490
  6.6 0.1 fusion.203
  6.6 0.0 copy-start.1
  6.6 4.0 %collective-permute-start.6 = (f32[256,128]{1,0:T(8,128)S(1)}, f32[256,128]{1,0:T(8,128)S(1)}, u32[]{:S(2)}, u32[]{:S(2)}) collective-permute-start(f32[256,128]{1,0:T(8,128)S(1)} %get-tuple-element.22), channel_id=1, source_target_pairs={{0,224},{32,192},{64,160},{96,128},{128,96},{160,64},{192,32},{224... | collective-permute-start | bytes 393224 | tf_op jit(solution)/shard_map/ppermute | solution.py:503
  10.6 1.9 %collective-permute-start.5 = (f32[256,128]{1,0:T(8,128)S(1)}, f32[256,128]{1,0:T(8,128)S(1)}, u32[]{:S(2)}, u32[]{:S(2)}) collective-permute-start(f32[256,128]{1,0:T(8,128)S(1)} %get-tuple-element.23), channel_id=1, source_target_pairs={{0,192},{32,224},{64,128},{96,160},{128,64},{160,96},{192,0},{224,... | collective-permute-start | bytes 393224 | tf_op jit(solution)/shard_map/ppermute | solution.py:503
  12.5 0.0 collective-permute-start.4
  12.5 1.4 %collective-permute-start.3 = (f32[256,128]{1,0:T(8,128)S(1)}, f32[256,128]{1,0:T(8,128)S(1)}, u32[]{:S(2)}, u32[]{:S(2)}) collective-permute-start(f32[256,128]{1,0:T(8,128)S(1)} %get-tuple-element.25), channel_id=1, source_target_pairs={{0,128},{32,160},{64,192},{96,224},{128,0},{160,32},{192,64},{224,... | collective-permute-start | bytes 393224 | tf_op jit(solution)/shard_map/ppermute | solution.py:503
  14.0 0.4 collective-permute-start.2
  14.3 0.0 copy-done.1
  14.3 0.1 copy.10.face_ref
  14.4 3.7 %shard_map.60 = f32[800,128]{1,0:T(8,128)} custom-call(s32[32,8]{1,0:T(8,128)S(1)} %copy.10.face_ref, f32[1024,128]{1,0:T(8,128)S(1)} %get-tuple-element.12.rim_ref), custom_call_target="tpu_custom_call" | custom-call | flops 100000000 | bytes 4194304 | tf_op jit(solution)/shard_map/pallas_call | solution.py:490
  18.1 11.2 %all-to-all-start = ((f32[800,1,128]{2,1,0:T(1,128)}), f32[800,1,128]{2,1,0:T(1,128)S(1)}, u32[]{:S(2)}, u32[]{:S(2)}) async-start(f32[800,1,128]{2,1,0:T(1,128)} %bitcast.5), calls=%async_computation | async-start | bytes 819200 | tf_op jit(solution)/shard_map/all_to_all | solution.py:566
  29.5 0.1 iota_add_fusion
  29.6 0.1 add.544
  29.7 0.3 fusion.5.col_ref
  30.1 0.4 fusion.14.row_ref
  30.5 0.7 fusion.45.edge_row_ref
  31.2 0.1 fusion.184
  31.3 0.0 collective-permute-done.6.refs_7_
  31.3 1.6 %collective-permute-start.1 = (f32[256,128]{1,0:T(8,128)S(1)}, f32[256,128]{1,0:T(8,128)S(1)}, u32[]{:S(2)}, u32[]{:S(2)}) collective-permute-start(f32[256,128]{1,0:T(8,128)S(1)} %get-tuple-element.27), channel_id=1, source_target_pairs={{0,64},{32,96},{64,0},{96,32},{128,192},{160,224},{192,128},{224,1... | collective-permute-start | bytes 393224 | tf_op jit(solution)/shard_map/ppermute | solution.py:503
  32.9 0.0 collective-permute-done.5.refs_6_
  32.9 0.6 collective-permute-start
  33.5 0.1 pad_maximum_fusion.table_ref
  33.6 0.0 collective-permute-done.4.refs_5_
  33.6 0.0 collective-permute-done.3.refs_4_
  33.6 0.0 collective-permute-done.2.refs_3_
  33.6 2.5 %collective-permute-done.1.refs_2_ = f32[256,128]{1,0:T(8,128)S(1)} collective-permute-done((f32[256,128]{1,0:T(8,128)S(1)}, f32[256,128]{1,0:T(8,128)S(1)}, u32[]{:S(2)}, u32[]{:S(2)}) %collective-permute-start.1) | collective-permute-done | bytes 131104 | tf_op jit(solution)/shard_map/ppermute | solution.py:503
  36.1 0.0 collective-permute-done.refs_1_
  36.1 1.3 %shard_map.62 = (f32[256,128]{1,0:T(8,128)S(1)}, f32[256,128]{1,0:T(8,128)S(1)}, f32[256,128]{1,0:T(8,128)S(1)}, f32[256,128]{1,0:T(8,128)S(1)}, f32[256,128]{1,...) custom-call(f32[64,128]{1,0:T(8,128)S(1)} %pad_maximum_fusion.table_ref, ...), custom_call_target="tpu_custom_call" | custom-call | flops 100000000 | bytes 4194304 | tf_op jit(solution)/shard_map/pallas_call | solution.py:490
  37.4 1.3 %collective-permute-start.7 = (f32[256,128]{1,0:T(8,128)S(1)}, f32[256,128]{1,0:T(8,128)S(1)}, u32[]{:S(2)}, u32[]{:S(2)}) collective-permute-start(f32[256,128]{1,0:T(8,128)S(1)} %get-tuple-element.15), channel_id=1, source_target_pairs={{0,32},{32,0},{64,96},{96,64},{128,160},{160,128},{192,224},{224,1... | collective-permute-start | bytes 393224 | tf_op jit(solution)/shard_map/ppermute | solution.py:503
  38.7 1.5 %collective-permute-start.8 = (f32[256,128]{1,0:T(8,128)S(1)}, f32[256,128]{1,0:T(8,128)S(1)}, u32[]{:S(2)}, u32[]{:S(2)}) collective-permute-start(f32[256,128]{1,0:T(8,128)S(1)} %get-tuple-element.16), channel_id=1, source_target_pairs={{0,64},{32,96},{64,0},{96,32},{128,192},{160,224},{192,128},{224,1... | collective-permute-start | bytes 393224 | tf_op jit(solution)/shard_map/ppermute | solution.py:503
  40.2 0.4 collective-permute-start.9
  40.5 3.7 %collective-permute-start.10 = (f32[256,128]{1,0:T(8,128)S(1)}, f32[256,128]{1,0:T(8,128)S(1)}, u32[]{:S(2)}, u32[]{:S(2)}) collective-permute-start(f32[256,128]{1,0:T(8,128)S(1)} %get-tuple-element.18), channel_id=1, source_target_pairs={{0,128},{32,160},{64,192},{96,224},{128,0},{160,32},{192,64},{224,... | collective-permute-start | bytes 393224 | tf_op jit(solution)/shard_map/ppermute | solution.py:503
  44.2 0.0 collective-permute-start.11
  44.2 0.0 collective-permute-done.7
  44.2 2.2 %collective-permute-start.12 = (f32[256,128]{1,0:T(8,128)S(1)}, f32[256,128]{1,0:T(8,128)S(1)}, u32[]{:S(2)}, u32[]{:S(2)}) collective-permute-start(f32[256,128]{1,0:T(8,128)S(1)} %get-tuple-element.20), channel_id=1, source_target_pairs={{0,192},{32,224},{64,128},{96,160},{128,64},{160,96},{192,0},{224,... | collective-permute-start | bytes 393224 | tf_op jit(solution)/shard_map/ppermute | solution.py:503
  46.4 0.0 collective-permute-done.8
  46.4 1.2 %collective-permute-start.13 = (f32[256,128]{1,0:T(8,128)S(1)}, f32[256,128]{1,0:T(8,128)S(1)}, u32[]{:S(2)}, u32[]{:S(2)}) collective-permute-start(f32[256,128]{1,0:T(8,128)S(1)} %get-tuple-element.21), channel_id=1, source_target_pairs={{0,224},{32,192},{64,160},{96,128},{128,96},{160,64},{192,32},{224... | collective-permute-start | bytes 393224 | tf_op jit(solution)/shard_map/ppermute | solution.py:503
  47.6 0.4 fusion.114.edge_col_ref
  47.9 0.0 collective-permute-done.9
  47.9 3.6 %collective-permute-done.10 = f32[256,128]{1,0:T(8,128)S(1)} collective-permute-done((f32[256,128]{1,0:T(8,128)S(1)}, f32[256,128]{1,0:T(8,128)S(1)}, u32[]{:S(2)}, u32[]{:S(2)}) %collective-permute-start.10) | collective-permute-done | bytes 131104 | tf_op jit(solution)/shard_map/ppermute | solution.py:503
  51.5 3.1 %collective-permute-done.11 = f32[256,128]{1,0:T(8,128)S(1)} collective-permute-done((f32[256,128]{1,0:T(8,128)S(1)}, f32[256,128]{1,0:T(8,128)S(1)}, u32[]{:S(2)}, u32[]{:S(2)}) %collective-permute-start.11) | collective-permute-done | bytes 131104 | tf_op jit(solution)/shard_map/ppermute | solution.py:503
  54.7 1.2 %collective-permute-done.12 = f32[256,128]{1,0:T(8,128)S(1)} collective-permute-done((f32[256,128]{1,0:T(8,128)S(1)}, f32[256,128]{1,0:T(8,128)S(1)}, u32[]{:S(2)}, u32[]{:S(2)}) %collective-permute-start.12) | collective-permute-done | bytes 131104 | tf_op jit(solution)/shard_map/ppermute | solution.py:503
  55.9 3.2 %collective-permute-done.13 = f32[256,128]{1,0:T(8,128)S(1)} collective-permute-done((f32[256,128]{1,0:T(8,128)S(1)}, f32[256,128]{1,0:T(8,128)S(1)}, u32[]{:S(2)}, u32[]{:S(2)}) %collective-permute-start.13) | collective-permute-done | bytes 131104 | tf_op jit(solution)/shard_map/ppermute | solution.py:503
  59.1 1.0 %shard_map.63 = f32[8,256,128]{2,1,0:T(8,128)} custom-call(s32[1]{0:T(128)} %bitcast.mine_ref, f32[8,32,128]{2,1,0:T(8,128)S(1)} %bitcast.66, f32[8,32,128]{2,1,0:T(8,128)S(1)} %bitcast.67, f32[8,32,128]{2,1,0:T(8,128)S(1)} %bitcast.68, f32[8,32,128]{2,1,0:T(8,128)S(1)} %bitcast.69, f32[8,32,128]{2,1,0:T(8,128)S(1)} %bitcast.70, f32[8,32,128]{2,1,0:T(8,128)S(1)} %bitcast.71, ...), custom_call_target="tpu_custom_call" | custom-call | flops 100000000 | bytes 4194304 | tf_op jit(solution)/shard_map/pallas_call | solution.py:490
  60.1 0.0 all-to-all-done
  60.1 7.5 %shard_map.61 = f32[2048,128]{1,0:T(8,128)} custom-call(s32[1]{0:T(128)} %bitcast.mine_ref, s32[8,2]{1,0:T(8,128)S(1)} %copy.12.box_ref, f32[800,128]{1,0:T(8,128)S(1)} %bitcast.65, f32[1024,128]{1,0:T(8,128)S(1)} %get-tuple-element.12.rim_ref, f32[2048,128]{1,0:T(8,128)} %bitcast.75, f32[2048,128]{1,0:T(8,128)} %bitcast.77, ...), custom_call_target="tpu_custom_call" | custom-call | flops 100000000 | bytes 4194304 | tf_op jit(solution)/shard_map/pallas_call | solution.py:490
  (23 shorter events, 0.1 us)
Async XLA Ops:
  0.6 0.7 %copy-start = (s32[8,2]{0,1:T(2,128)S(1)}, s32[8,2]{0,1:T(2,128)}, u32[]{:S(2)}) copy-start(s32[8,2]{0,1:T(2,128)} %param.6) | copy-start | bytes 196
  6.6 7.7 %copy-start.1 = (s32[32,8]{0,1:T(8,128)S(1)}, s32[32,8]{0,1:T(8,128)}, u32[]{:S(2)}) copy-start(s32[32,8]{0,1:T(8,128)} %param.7) | copy-start | bytes 3076
  6.6 24.7 %collective-permute-start.6 = (f32[256,128]{1,0:T(8,128)S(1)}, f32[256,128]{1,0:T(8,128)S(1)}, u32[]{:S(2)}, u32[]{:S(2)}) collective-permute-start(f32[256,128]{1,0:T(8,128)S(1)} %get-tuple-element.22), channel_id=1, source_target_pairs={{0,224},{32,192},{64,160},{96,128},{128,96},{160,64},{192,32},{224... | collective-permute-start | bytes 393224 | tf_op jit(solution)/shard_map/ppermute | solution.py:503
  10.6 22.3 %collective-permute-start.5 = (f32[256,128]{1,0:T(8,128)S(1)}, f32[256,128]{1,0:T(8,128)S(1)}, u32[]{:S(2)}, u32[]{:S(2)}) collective-permute-start(f32[256,128]{1,0:T(8,128)S(1)} %get-tuple-element.23), channel_id=1, source_target_pairs={{0,192},{32,224},{64,128},{96,160},{128,64},{160,96},{192,0},{224,... | collective-permute-start | bytes 393224 | tf_op jit(solution)/shard_map/ppermute | solution.py:503
  12.5 21.0 %collective-permute-start.4 = (f32[256,128]{1,0:T(8,128)S(1)}, f32[256,128]{1,0:T(8,128)S(1)}, u32[]{:S(2)}, u32[]{:S(2)}) collective-permute-start(f32[256,128]{1,0:T(8,128)S(1)} %get-tuple-element.24), channel_id=1, source_target_pairs={{0,160},{32,128},{64,224},{96,192},{128,32},{160,0},{192,96},{224,... | collective-permute-start | bytes 393224 | tf_op jit(solution)/shard_map/ppermute | solution.py:503
  12.5 21.0 %collective-permute-start.3 = (f32[256,128]{1,0:T(8,128)S(1)}, f32[256,128]{1,0:T(8,128)S(1)}, u32[]{:S(2)}, u32[]{:S(2)}) collective-permute-start(f32[256,128]{1,0:T(8,128)S(1)} %get-tuple-element.25), channel_id=1, source_target_pairs={{0,128},{32,160},{64,192},{96,224},{128,0},{160,32},{192,64},{224,... | collective-permute-start | bytes 393224 | tf_op jit(solution)/shard_map/ppermute | solution.py:503
  14.0 19.6 %collective-permute-start.2 = (f32[256,128]{1,0:T(8,128)S(1)}, f32[256,128]{1,0:T(8,128)S(1)}, u32[]{:S(2)}, u32[]{:S(2)}) collective-permute-start(f32[256,128]{1,0:T(8,128)S(1)} %get-tuple-element.26), channel_id=1, source_target_pairs={{0,96},{32,64},{64,32},{96,0},{128,224},{160,192},{192,160},{224,1... | collective-permute-start | bytes 393224 | tf_op jit(solution)/shard_map/ppermute | solution.py:503
  18.1 42.0 %all-to-all-start = ((f32[800,1,128]{2,1,0:T(1,128)}), f32[800,1,128]{2,1,0:T(1,128)S(1)}, u32[]{:S(2)}, u32[]{:S(2)}) async-start(f32[800,1,128]{2,1,0:T(1,128)} %bitcast.5), calls=%async_computation | async-start | bytes 819200 | tf_op jit(solution)/shard_map/all_to_all | solution.py:566
  31.3 4.8 %collective-permute-start.1 = (f32[256,128]{1,0:T(8,128)S(1)}, f32[256,128]{1,0:T(8,128)S(1)}, u32[]{:S(2)}, u32[]{:S(2)}) collective-permute-start(f32[256,128]{1,0:T(8,128)S(1)} %get-tuple-element.27), channel_id=1, source_target_pairs={{0,64},{32,96},{64,0},{96,32},{128,192},{160,224},{192,128},{224,1... | collective-permute-start | bytes 393224 | tf_op jit(solution)/shard_map/ppermute | solution.py:503
  32.9 3.2 %collective-permute-start = (f32[256,128]{1,0:T(8,128)S(1)}, f32[256,128]{1,0:T(8,128)S(1)}, u32[]{:S(2)}, u32[]{:S(2)}) collective-permute-start(f32[256,128]{1,0:T(8,128)S(1)} %get-tuple-element.28), channel_id=1, source_target_pairs={{0,32},{32,0},{64,96},{96,64},{128,160},{160,128},{192,224},{224,1... | collective-permute-start | bytes 393224 | tf_op jit(solution)/shard_map/ppermute | solution.py:503
  37.4 6.8 %collective-permute-start.7 = (f32[256,128]{1,0:T(8,128)S(1)}, f32[256,128]{1,0:T(8,128)S(1)}, u32[]{:S(2)}, u32[]{:S(2)}) collective-permute-start(f32[256,128]{1,0:T(8,128)S(1)} %get-tuple-element.15), channel_id=1, source_target_pairs={{0,32},{32,0},{64,96},{96,64},{128,160},{160,128},{192,224},{224,1... | collective-permute-start | bytes 393224 | tf_op jit(solution)/shard_map/ppermute | solution.py:503
  38.7 7.7 %collective-permute-start.8 = (f32[256,128]{1,0:T(8,128)S(1)}, f32[256,128]{1,0:T(8,128)S(1)}, u32[]{:S(2)}, u32[]{:S(2)}) collective-permute-start(f32[256,128]{1,0:T(8,128)S(1)} %get-tuple-element.16), channel_id=1, source_target_pairs={{0,64},{32,96},{64,0},{96,32},{128,192},{160,224},{192,128},{224,1... | collective-permute-start | bytes 393224 | tf_op jit(solution)/shard_map/ppermute | solution.py:503
  40.2 7.7 %collective-permute-start.9 = (f32[256,128]{1,0:T(8,128)S(1)}, f32[256,128]{1,0:T(8,128)S(1)}, u32[]{:S(2)}, u32[]{:S(2)}) collective-permute-start(f32[256,128]{1,0:T(8,128)S(1)} %get-tuple-element.17), channel_id=1, source_target_pairs={{0,96},{32,64},{64,32},{96,0},{128,224},{160,192},{192,160},{224,1... | collective-permute-start | bytes 393224 | tf_op jit(solution)/shard_map/ppermute | solution.py:503
  40.5 11.0 %collective-permute-start.10 = (f32[256,128]{1,0:T(8,128)S(1)}, f32[256,128]{1,0:T(8,128)S(1)}, u32[]{:S(2)}, u32[]{:S(2)}) collective-permute-start(f32[256,128]{1,0:T(8,128)S(1)} %get-tuple-element.18), channel_id=1, source_target_pairs={{0,128},{32,160},{64,192},{96,224},{128,0},{160,32},{192,64},{224,... | collective-permute-start | bytes 393224 | tf_op jit(solution)/shard_map/ppermute | solution.py:503
  44.2 10.5 %collective-permute-start.11 = (f32[256,128]{1,0:T(8,128)S(1)}, f32[256,128]{1,0:T(8,128)S(1)}, u32[]{:S(2)}, u32[]{:S(2)}) collective-permute-start(f32[256,128]{1,0:T(8,128)S(1)} %get-tuple-element.19), channel_id=1, source_target_pairs={{0,160},{32,128},{64,224},{96,192},{128,32},{160,0},{192,96},{224,... | collective-permute-start | bytes 393224 | tf_op jit(solution)/shard_map/ppermute | solution.py:503
  44.2 11.6 %collective-permute-start.12 = (f32[256,128]{1,0:T(8,128)S(1)}, f32[256,128]{1,0:T(8,128)S(1)}, u32[]{:S(2)}, u32[]{:S(2)}) collective-permute-start(f32[256,128]{1,0:T(8,128)S(1)} %get-tuple-element.20), channel_id=1, source_target_pairs={{0,192},{32,224},{64,128},{96,160},{128,64},{160,96},{192,0},{224,... | collective-permute-start | bytes 393224 | tf_op jit(solution)/shard_map/ppermute | solution.py:503
  46.4 12.7 %collective-permute-start.13 = (f32[256,128]{1,0:T(8,128)S(1)}, f32[256,128]{1,0:T(8,128)S(1)}, u32[]{:S(2)}, u32[]{:S(2)}) collective-permute-start(f32[256,128]{1,0:T(8,128)S(1)} %get-tuple-element.21), channel_id=1, source_target_pairs={{0,224},{32,192},{64,160},{96,128},{128,96},{160,64},{192,32},{224... | collective-permute-start | bytes 393224 | tf_op jit(solution)/shard_map/ppermute | solution.py:503

commit v2 on v1

--- a/solution.py
+++ b/solution.py
@@ -66,39 +66,6 @@
     return jnp.dot(a, b, preferred_element_type=f32)
 
 
-def backward_tables(extent_rows, extent_cols):
-    count = extent_rows.shape[0]
-    ex = extent_rows[:, None, None]
-    ey = extent_cols[:, None, None]
-    shape = (count, B, LANES)
-    col_back = cosine(ey, iota(shape, 2) % B, iota(shape, 1))
-    row = iota(shape, 1)
-    lane = iota(shape, 2)
-    row_back = jnp.where(lane < B, cosine(ex, 2 * (row % 32) + row // 32, lane), 0.0)
-
-    def edge(extent, wave, index):
-        layer = index % 3
-        total = jnp.zeros(wave.shape, f32)
-        for i in range(3):
-            cell = jnp.where(index < 3, i, extent - 1 - i)
-            weight = jnp.where(
-                i + layer == 0,
-                STENCIL[0],
-                jnp.where(i + layer == 1, STENCIL[1], jnp.where(i + layer == 2, STENCIL[2], 0.0)),
-            )
-            total = total + weight * cosine(extent, wave, cell)
-        return jnp.where(index < 6, total, 0.0)
-
-    shape = (count, 32, LANES)
-    lane = iota(shape, 2)
-    edge_rows = edge(ex, 2 * iota(shape, 1) + (lane // 8) % 2, lane % 8)
-    shape = (count, 16, LANES)
-    row = iota(shape, 1)
-    lane = iota(shape, 2)
-    edge_cols = jnp.where(row // 8 == lane // B, edge(ey, lane % B, row % 8), 0.0)
-    return col_back, row_back, edge_rows, edge_cols
-
-
 def cosine_tile(length, wave, place):
     size = jnp.full((1, LANES), length, jnp.int32).astype(f32)
     unit = 1.0 / size
@@ -120,9 +87,12 @@
     mine_ref,
     box_ref,
     x_hbm,
-    piece_ref,
+    even_ref,
+    odd_ref,
     rim_ref,
     x_ref,
+    stage0_ref,
+    stage1_ref,
     table_ref,
     c_hi_ref,
     c_lo_ref,
@@ -135,7 +105,7 @@
     sem,
 ):
     mine = mine_ref[0]
-    holders = box_ref.shape[0]
+    holders = box_ref.shape[1]
     fetch = pltpu.make_async_copy(x_hbm, x_ref, sem)
     fetch.start()
     low32 = iota((32, LANES), 1) < B
@@ -149,8 +119,8 @@
     l_low = iota((144, LANES), 1) < B
 
     def tables(p, carry):
-        ex = box_ref[p, 0]
-        ey = box_ref[p, 1]
+        ex = box_ref[0, p]
+        ey = box_ref[1, p]
         c = cosine_tile(ey, row64, jnp.where(low, lane, rim_cell(lane - B, ey)).astype(f32))
         turned = pltpu.roll(c, B, 1)
         c = jnp.concatenate(
@@ -202,7 +172,7 @@
             r_hi_ref[:, i * LANES : (i + 1) * LANES] = hi
             r_lo_ref[:, i * LANES : (i + 1) * LANES] = lo
 
-    def along_x(p, r_hi_ref, r_lo_ref):
+    def along_x(p, r_hi_ref, r_lo_ref, stage_ref):
         r_hi, r_lo = r_hi_ref[...], r_lo_ref[...]
         right = jnp.concatenate([r_hi, r_lo, r_hi, r_lo], 0)
         left = jnp.concatenate([l_hi_ref[p], l_lo_ref[p]], 1)
@@ -211,9 +181,12 @@
         for kz in range(planes):
             tile = y[:, kz * LANES : (kz + 1) * LANES]
             out = jnp.where(low32, tile[:32], tile[32:64])
-            for g in range(8):
-                spot = (mine ^ g) * 256 + kz * 32 + p
-                piece_ref[pl.ds(spot, 4, stride=8), :] = out[g * 4 : (g + 1) * 4]
+            stage_ref[kz * 32 : (kz + 1) * 32, :] = out
+            for s in range(8):
+                spot = (s // 2) * 256 + kz * 32 + p
+                (even_ref, odd_ref)[s % 2][pl.ds(spot, 4, stride=8), :] = stage_ref[
+                    pl.ds(kz * 32 + (mine ^ s) * 4, 4), :
+                ]
             rim_ref[pl.ds(pl.multiple_of(p * 128 + kz * RIM, RIM), RIM), :] = jnp.where(
                 low8, tile[64:72], 0.0
             )
@@ -226,16 +199,18 @@
 
     def two(i, carry):
         along_y(2 * i, *even)
-        along_x(jnp.maximum(2 * i - 1, 0), *odd)
+        along_x(jnp.maximum(2 * i - 1, 0), *odd, stage1_ref)
         along_y(2 * i + 1, *odd)
-        along_x(2 * i, *even)
+        along_x(2 * i, *even, stage0_ref)
         return carry
 
     lax.fori_loop(0, holders // 2, two, 0)
-    along_x(holders - 1, *odd)
-
-
-def pack_kernel(planes, face_ref, rim_ref, pay_hbm, used_ref, pay_ref, sem):
+    along_x(holders - 1, *odd, stage1_ref)
+
+
+def pack_kernel(planes, face_ref, rim_ref, pay_hbm, rim_hbm, used_ref, pay_ref, sems):
+    keep = pltpu.make_async_copy(rim_ref, rim_hbm, sems.at[0])
+    keep.start()
     pay_ref[...] = jnp.zeros_like(pay_ref)
     targets = pay_ref.shape[0] // FACE_ROWS
 
@@ -245,41 +220,41 @@
 
     lax.fori_loop(0, targets, clear, 0)
 
+    lane = iota((planes, LANES), 1)
+
     def face(r, carry):
-        length = face_ref[r, 3]
-
-        @pl.when(length > 0)
-        def _():
-            side = face_ref[r, 1]
-            start = face_ref[r, 2]
-            target = face_ref[r, 4]
-            code = face_ref[r, 5] * 4 + face_ref[r, 6] + 1
-            slot = used_ref[target]
-            used_ref[target] = slot + 1
-            first = slot * B + face_ref[r, 7]
-            turn = (first - start + LANES) & (LANES - 1)
-            base = face_ref[r, 0] * 128 + (side >> 1) * 64 + (side & 1) * 3
-            lane = iota((RIM, LANES), 1)
-            here = (lane >= first) & (lane < first + length)
-            for j in range(3):
-                values = rim_ref[pl.ds(base + j, planes, stride=RIM), :]
-                values = jnp.where(here, pltpu.roll(values, turn, 1), 0.0)
-                rows = pl.ds(target * FACE_ROWS + j * planes, planes)
-                pay_ref[rows, :] = pay_ref[rows, :] + values
-            rows = pl.ds(target * FACE_ROWS + 3 * planes, 1)
-            pay_ref[rows, :] = pay_ref[rows, :] + jnp.where(here[:1], code, 0).astype(f32)
-
+        length = face_ref[3, r]
+        live = (length > 0).astype(jnp.int32)
+        side = face_ref[1, r]
+        target = face_ref[4, r] * live
+        code = face_ref[5, r] * 4 + face_ref[6, r] + 1
+        slot = used_ref[target] * live
+        used_ref[target] = used_ref[target] + live
+        first = slot * B + face_ref[7, r]
+        turn = (first - face_ref[2, r] + LANES) & (LANES - 1)
+        base = face_ref[0, r] * 128 + (side >> 1) * 64 + (side & 1) * 3
+        here = (lane >= first) & (lane < first + length)
+        for j in range(3):
+            values = pltpu.roll(rim_ref[pl.ds(base + j, planes, stride=RIM), :], turn, 1)
+            rows = pl.ds(target * FACE_ROWS + j * planes, planes)
+            pltpu.store(pay_ref.at[rows, :], values, mask=here)
+        rows = pl.ds(target * FACE_ROWS + 3 * planes, 1)
+        label = jnp.full((1, LANES), code, jnp.int32).astype(f32)
+        pltpu.store(pay_ref.at[rows, :], label, mask=here[:1])
         return carry
 
-    lax.fori_loop(0, face_ref.shape[0], face, 0)
-    send = pltpu.make_async_copy(pay_ref, pay_hbm, sem)
+    lax.fori_loop(0, face_ref.shape[1], face, 0, unroll=4)
+    send = pltpu.make_async_copy(pay_ref, pay_hbm, sems.at[1])
     send.start()
+    keep.wait()
     send.wait()
 
 
-def depth_kernel(planes, table_ref, *refs):
-    count = len(refs) // 2
-    blocks, outs = refs[:count], refs[count:]
+def depth_kernel(planes, table_ref, own_ref, near_ref, *refs):
+    far, outs = refs[:-2], refs[-2:]
+    count = 2 + 2 * len(far)
+    size = 32 * planes
+    blocks = [(own_ref, 0), (near_ref, 0)] + [(r, i * size) for r in far for i in range(2)]
     total = count * planes
     t_hi, t_lo = split(table_ref[...])
     t_lo = jnp.where(iota((total, LANES), 1) < total, t_lo, jnp.zeros_like(t_lo))
@@ -288,7 +263,7 @@
         right = jnp.concatenate(
             [
                 jnp.concatenate(
-                    [b[pl.ds(q * 8 + p, planes, stride=32), :] for b in blocks], 0
+                    [b[pl.ds(at + q * 8 + p, planes, stride=32), :] for b, at in blocks], 0
                 )
                 for p in range(8)
             ],
@@ -298,7 +273,8 @@
         mixed = dot(left, jnp.concatenate([r_hi, r_lo, r_hi, r_lo], 0))
         for p in range(8):
             for s in range(count):
-                outs[s][pl.ds(q * 8 + p, planes, stride=32), :] = mixed[
+                spot = (s // 2) * size + q * 8 + p
+                outs[s % 2][pl.ds(spot, planes, stride=32), :] = mixed[
                     s * planes : (s + 1) * planes, p * LANES : (p + 1) * LANES
                 ]
 
@@ -309,18 +285,23 @@
     mine_ref,
     box_ref,
     got_ref,
-    rim_ref,
+    rim_hbm,
     now_hbm,
     prev_hbm,
-    col_ref,
-    row_ref,
-    edge_row_ref,
-    edge_col_ref,
+    col_hbm,
+    row_hbm,
+    edge_row_hbm,
+    edge_col_hbm,
     out_ref,
     sum_ref,
     times_ref,
     now_ref,
     prev_ref,
+    rim_ref,
+    col_ref,
+    row_ref,
+    edge_row_ref,
+    edge_col_ref,
     label_ref,
     code_ref,
     even_down_ref,
@@ -331,10 +312,15 @@
     odd_lo_ref,
     sems,
 ):
-    holders = col_ref.shape[0]
+    holders = col_hbm.shape[0]
     fetches = [
-        pltpu.make_async_copy(now_hbm, now_ref, sems.at[0]),
-        pltpu.make_async_copy(prev_hbm, prev_ref, sems.at[1]),
+        pltpu.make_async_copy(rim_hbm, rim_ref, sems.at[0]),
+        pltpu.make_async_copy(col_hbm, col_ref, sems.at[1]),
+        pltpu.make_async_copy(row_hbm, row_ref, sems.at[2]),
+        pltpu.make_async_copy(edge_row_hbm, edge_row_ref, sems.at[3]),
+        pltpu.make_async_copy(edge_col_hbm, edge_col_ref, sems.at[4]),
+        pltpu.make_async_copy(now_hbm, now_ref, sems.at[5]),
+        pltpu.make_async_copy(prev_hbm, prev_ref, sems.at[6]),
     ]
     for copy in fetches:
         copy.start()
@@ -344,7 +330,7 @@
     first = jnp.max(jnp.where(place < B, labels, 0.0), 1, keepdims=True)
     second = jnp.max(jnp.where(place < B, 0.0, labels), 1, keepdims=True)
     label_ref[...] = jnp.where(place == 0, first, second).astype(jnp.int32)
-    to_scalars = pltpu.make_async_copy(label_ref, code_ref, sems.at[2])
+    to_scalars = pltpu.make_async_copy(label_ref, code_ref, sems.at[7])
     to_scalars.start()
     sum_ref[...] = jnp.zeros_like(sum_ref)
     times_ref[...] = jnp.zeros_like(times_ref)
@@ -430,8 +416,8 @@
             jnp.concatenate([left_hi, left_hi, left_lo], 1),
             jnp.concatenate([right_hi, right_lo, right_hi], 0),
         )
-        ex = box_ref[p, 0]
-        ey = box_ref[p, 1]
+        ex = box_ref[0, p]
+        ey = box_ref[1, p]
         wave_x = 2 * iota((32, LANES), 0) + lane // B
         wave_y = lane % B
         inside = (wave_x < ex) & (wave_y < ey)
@@ -467,10 +453,63 @@
     finish(holders - 1, *odd)
 
 
-def join_kernel(mine_ref, *refs):
-    count = (len(refs) - 2)
-    blocks, out_ref, sems = refs[:count], refs[count], refs[count + 1]
+def tables_kernel(box_ref, *refs):
+    outs, held, sems = refs[:4], refs[4:8], refs[8]
+    col_ref, row_ref, edge_row_ref, edge_col_ref = held
+    down = iota((B, LANES), 0)
+    lane = iota((B, LANES), 1)
+    col_wave = (lane % B).astype(f32)
+    row_wave = (2 * (down % 32) + down // 32).astype(f32)
+    across = lane.astype(f32)
+    below = down.astype(f32)
+    low = lane < B
+
+    def weights(index):
+        layer = index % 3
+        table = [jnp.zeros(index.shape, f32)] * 3
+        for i in range(3):
+            for j in range(3 - i):
+                table[i] = jnp.where((layer == j) & (index < 6), STENCIL[i + j], table[i])
+        return table
+
+    row_lane = lane[:32]
+    row_index = row_lane % 8
+    row_weights = weights(row_index)
+    edge_row_wave = (2 * down[:32] + (row_lane // 8) % 2).astype(f32)
+    col_index = down[:16] % 8
+    col_mine = down[:16] // 8 == lane[:16] // B
+    col_weights = [jnp.where(col_mine, w, 0.0) for w in weights(col_index)]
+    edge_col_wave = col_wave[:16]
+
+    def one(p, carry):
+        ex = box_ref[0, p]
+        ey = box_ref[1, p]
+        col_ref[p] = cosine_tile(ey, col_wave, below)
+        row_ref[p] = jnp.where(low, cosine_tile(ex, row_wave, across), 0.0)
+        for extent, wave, index, weight, ref in (
+            (ex, edge_row_wave, row_index, row_weights, edge_row_ref),
+            (ey, edge_col_wave, col_index, col_weights, edge_col_ref),
+        ):
+            total = jnp.zeros(wave.shape, f32)
+            for i in range(3):
+                cell = jnp.where(index < 3, i, extent - 1 - i).astype(f32)
+                total = total + weight[i] * cosine_tile(extent, wave, cell)
+            ref[p] = total
+        return carry
+
+    lax.fori_loop(0, box_ref.shape[1], one, 0, unroll=2)
+    copies = [pltpu.make_async_copy(h, o, sems.at[i]) for i, (h, o) in enumerate(zip(held, outs))]
+    for copy in copies:
+        copy.start()
+    for copy in copies:
+        copy.wait()
+
+
+def join_kernel(planes, mine_ref, own_ref, near_ref, *refs):
+    far, out_ref, sems = refs[:-2], refs[-2], refs[-1]
     mine = mine_ref[0]
+    blocks = [own_ref.at[:planes], near_ref.at[:planes]]
+    blocks += [r.at[pl.ds(i * planes, planes)] for r in far for i in range(2)]
     copies = []
     for s, block in enumerate(blocks):
         spot = pl.multiple_of((mine ^ s) * 32, 32)
@@ -503,6 +542,23 @@
     return lax.ppermute(block, "height", [(i, i ^ step) for i in range(count)])
 
 
+def across(blocks, near):
+    size = blocks.shape[0] // 4
+    return [
+        swap(
+            jnp.concatenate(
+                [blocks[t * size : (t + 1) * size], near[t * size : (t + 1) * size]], 0
+            ),
+            2 * t,
+        )
+        for t in range(1, 4)
+    ]
+
+
+def in_hbm(x):
+    return pltpu.with_memory_space_constraint(x, pltpu.HBM)
+
+
 def tiles(field):
     planes, holders, cells = field.shape
     split_up = field.reshape(planes, holders, cells // LANES, LANES).transpose(0, 2, 1, 3)
@@ -521,22 +577,25 @@
     domains = lax.axis_size("dom")
     total = planes * count
     mine = lax.axis_index("height").astype(jnp.int32)
-    extent_rows = partition_boxes[:, 0]
-    extent_cols = partition_boxes[:, 1]
-    now = pltpu.with_memory_space_constraint(tiles(modes_now), pltpu.HBM)
-    prev = pltpu.with_memory_space_constraint(tiles(modes_prev), pltpu.HBM)
+    now = in_hbm(tiles(modes_now))
+    prev = in_hbm(tiles(modes_prev))
     mine_word = mine.reshape(1)
+    boxes = in_hbm(partition_boxes.T)
+    face_rows = in_hbm(face_table.T)
 
     def rows(n):
         return jax.ShapeDtypeStruct((n, LANES), f32)
 
-    pieces, rim = call(
+    half = 1024
+    even, odd, rim = call(
         functools.partial(cells_kernel, planes),
-        (mine_word, partition_boxes, now),
+        (mine_word, boxes, now),
         [SM, SM, HB],
-        (rows(2048), rows(holders * 128)),
+        (rows(half), rows(half), rows(holders * 128)),
         [
             pltpu.VMEM((2048, LANES), f32),
+            pltpu.VMEM((32 * planes, LANES), f32),
+            pltpu.VMEM((32 * planes, LANES), f32),
             pltpu.VMEM((holders * B, LANES), f32),
             pltpu.VMEM((holders, LANES, 2 * LANES), bf16),
             pltpu.VMEM((holders, LANES, 2 * LANES), bf16),
@@ -549,20 +608,20 @@
             pltpu.SemaphoreType.DMA,
         ],
     )
-    pay = call(
+    pay, rim = call(
         functools.partial(pack_kernel, planes),
-        (face_table, rim),
+        (face_rows, rim),
         [SM, VM],
-        rows(domains * FACE_ROWS),
+        (rows(domains * FACE_ROWS), pltpu.HBM((holders * 128, LANES), f32)),
         [
             pltpu.SMEM((domains,), jnp.int32),
             pltpu.VMEM((domains * FACE_ROWS, LANES), f32),
-            pltpu.SemaphoreType.DMA,
+            pltpu.SemaphoreType.DMA((2,)),
         ],
         spot=HB,
     )
-    pieces = pieces.reshape(count, 256, LANES)
-    got = [pieces[0]] + [swap(pieces[s], s) for s in range(1, count)]
+    near = swap(odd, 1)
+    far = across(even, near)
     arrived = lax.all_to_all(pay.reshape(-1, 1, LANES), "dom", 0, 0, tiled=True)
 
     order = (mine ^ jnp.arange(count, dtype=jnp.int32))[:, None] * planes
@@ -571,23 +630,46 @@
     depth_table = jnp.concatenate([depth_table, depth_table], 1)
     mixed = call(
         functools.partial(depth_kernel, planes),
-        (depth_table, *got),
-        [VM] * (1 + count),
-        (rows(256),) * count,
+        (depth_table, even, near, *far),
+        [VM] * (3 + len(far)),
+        (rows(half),) * 2,
     )
-    back = [mixed[0]] + [swap(mixed[s], s) for s in range(1, count)]
-
+    back_near = swap(mixed[1], 1)
+    back_far = across(mixed[0], back_near)
+
+    later, _ = lax.optimization_barrier((boxes, mixed[0]))
+    tables = call(
+        tables_kernel,
+        (later,),
+        [SM],
+        tuple(
+            pltpu.HBM((holders, n, LANES), f32) for n in (B, B, 32, 2 * RIM)
+        ),
+        [
+            pltpu.VMEM((holders, B, LANES), f32),
+            pltpu.VMEM((holders, B, LANES), f32),
+            pltpu.VMEM((holders, 32, LANES), f32),
+            pltpu.VMEM((holders, 2 * RIM, LANES), f32),
+            pltpu.SemaphoreType.DMA((4,)),
+        ],
+        spot=HB,
+    )
     new = call(
         functools.partial(advance_kernel, planes, total),
-        (mine_word, partition_boxes, arrived.reshape(-1, LANES), rim, now, prev)
-        + tuple(backward_tables(extent_rows, extent_cols)),
-        [SM] * 2 + [VM] * 2 + [HB] * 2 + [VM] * 4,
+        (mine_word, boxes, arrived.reshape(-1, LANES), in_hbm(rim), now, prev)
+        + tuple(in_hbm(t) for t in tables),
+        [SM] * 2 + [VM] + [HB] * 7,
         rows(2048),
         [
             pltpu.VMEM((holders * 128, LANES), f32),
             pltpu.VMEM((holders * 2 * RIM, LANES), f32),
             pltpu.VMEM((2048, LANES), f32),
             pltpu.VMEM((2048, LANES), f32),
+            pltpu.VMEM((holders * 128, LANES), f32),
+            pltpu.VMEM((holders, B, LANES), f32),
+            pltpu.VMEM((holders, B, LANES), f32),
+            pltpu.VMEM((holders, 32, LANES), f32),
+            pltpu.VMEM((holders, 16, LANES), f32),
             pltpu.VMEM((domains, LANES), jnp.int32),
             pltpu.SMEM((domains, LANES), jnp.int32),
         ]
@@ -597,12 +679,12 @@
             pltpu.VMEM((LANES, LANES), bf16),
         ]
         * 2
-        + [pltpu.SemaphoreType.DMA((3,))],
+        + [pltpu.SemaphoreType.DMA((8,))],
     )
     pressure = call(
-        join_kernel,
-        (mine_word, *[b.reshape(planes, 32, LANES) for b in back]),
-        [SM] + [VM] * count,
+        functools.partial(join_kernel, planes),
+        (mine_word, *[b.reshape(-1, 32, LANES) for b in (mixed[0], back_near, *back_far)]),
+        [SM] + [VM] * (2 + len(back_far)),
         jax.ShapeDtypeStruct((planes, 256, LANES), f32),
         [pltpu.SemaphoreType.DMA((count,))],
         spot=HB,

time: 67.8 us -> 64.8 us (0.956)
  starting transfers between devices: 31.2 us -> 21.4 us
  waiting for transfers between devices: 13.7 us -> 20.6 us
  Pallas kernels: 18.6 us -> 20.6 us
  other arithmetic: 2.21 us -> 0.39 us
  local copies, waits for them, and re-layouts: 0.99 us -> 0.19 us
    all_to_all x1, waiting for transfers between devices: 0.01 us -> 8.15 us  [step(): arrived = lax.all_to_all(pay.reshape(-1, 1, LANES), 'dom', 0, 0, tiled=True)]
    ppermute x14 -> x8, starting transfers between devices: 20 us -> 11.9 us  [swap(): return lax.ppermute(block, 'height', [(i, i ^ step) for i in range(count)])]
    pallas_call x5 -> x6, Pallas kernels: 18.6 us -> 20.6 us  [call(): pl.pallas_call(kernel, out_shape=outs, in_specs=spots, out_specs=tuple(sp...]
    all_to_all x1, starting transfers between devices: 11.2 us -> 9.51 us  [step(): arrived = lax.all_to_all(pay.reshape(-1, 1, LANES), 'dom', 0, 0, tiled=True)]
    select_n x3 -> x0, other arithmetic: 1.48 us -> none  [the longest x1 0.66 us: edge(): return jnp.where(index < 6, total, 0.0)]
    ppermute x14 -> x8, waiting for transfers between devices: 13.7 us -> 12.5 us  [swap(): return lax.ppermute(block, 'height', [(i, i ^ step) for i in range(count)])]
    unnamed x6 -> x0, local copies, waits for them, and re-layouts: 0.83 us -> none
  transfers between devices with their start and end apart: 15 -> 9, of which waited for: 5 -> 4; matrix products, arithmetic and copies ran while one was open for 4% -> 1% of each run, Pallas kernels for 9% -> 20%
where the time goes in v2:
time: 64.8 us; the launch traced here: 64 us
  starting transfers between devices  21.4 us (33%)
  Pallas kernels  20.6 us (32%)
  waiting for transfers between devices  20.6 us (32%)
  between operations  0.79 us (1%)
    pallas_call x6, Pallas kernels, call(): pl.pallas_call(kernel, out_shape=outs, in_specs=spots, out_specs=tuple(sp...  20.6 us
    ppermute x8, waiting for transfers between devices, swap(): return lax.ppermute(block, 'height', [(i, i ^ step) for i in range(count)])  12.5 us
    ppermute x8, starting transfers between devices, swap(): return lax.ppermute(block, 'height', [(i, i ^ step) for i in range(count)])  11.9 us
    all_to_all x1, starting transfers between devices, step(): arrived = lax.all_to_all(pay.reshape(-1, 1, LANES), 'dom', 0, 0, tiled=True)  9.51 us
    all_to_all x1, waiting for transfers between devices, step(): arrived = lax.all_to_all(pay.reshape(-1, 1, LANES), 'dom', 0, 0, tiled=True)  8.15 us
  transfers between devices with their start and end apart: 9, of which 4 were waited for; matrix products, arithmetic and copies ran while one was open for 1% of the time, Pallas kernels for 20%

profile of v2, /device:TPU:1, one launch (start us, length us, event | category | flops | bytes accessed | tf_op | source)
XLA Modules:
  0.0 64.0 jit_solution(8542920138120860674)
XLA Ops:
  0.6 5.2 %shard_map.59 = (f32[1024,128]{1,0:T(8,128)S(1)}, f32[1024,128]{1,0:T(8,128)S(1)}, f32[1024,128]{1,0:T(8,128)S(1)}) custom-call(s32[1]{0:T(128)} %bitcast.mine_ref, s32[2,8]{1,0:T(2,128)} %bitcast.44, f32[2048,128]{1,0:T(8,128)} %bitcast.38), custom_call_target="tpu_custom_call" | custom-call | flops 100000000 | bytes 4194304 | tf_op jit(solution)/shard_map/pallas_call | solution.py:529
  5.9 3.3 %collective-permute-start = (f32[1024,128]{1,0:T(8,128)S(1)}, f32[1024,128]{1,0:T(8,128)S(1)}, u32[]{:S(2)}, u32[]{:S(2)}) collective-permute-start(f32[1024,128]{1,0:T(8,128)S(1)} %get-tuple-element.18), channel_id=1, source_target_pairs={{0,32},{32,0},{64,96},{96,64},{128,160},{160,128},{192,224},{224,1... | collective-permute-start | bytes 1572872 | tf_op jit(solution)/shard_map/ppermute | solution.py:542
  9.2 0.1 iota_add_fusion
  9.2 0.1 add.88
  9.4 1.3 %collective-permute-done.near_ref = f32[1024,128]{1,0:T(8,128)S(1)} collective-permute-done((f32[1024,128]{1,0:T(8,128)S(1)}, f32[1024,128]{1,0:T(8,128)S(1)}, u32[]{:S(2)}, u32[]{:S(2)}) %collective-permute-start) | collective-permute-done | bytes 524320 | tf_op jit(solution)/shard_map/ppermute | solution.py:542
  10.8 0.9 %collective-permute-start.3 = (f32[512,128]{1,0:T(8,128)S(1)}, f32[512,128]{1,0:T(8,128)S(1)}, u32[]{:S(2)}, u32[]{:S(2)}) collective-permute-start(f32[512,128]{1,0:T(8,128)S(1)} %pad_maximum_fusion.2), channel_id=1, source_target_pairs={{0,192},{32,224},{64,128},{96,160},{128,64},{160,96},{192,0},{224,... | collective-permute-start | bytes 786440 | tf_op jit(solution)/shard_map/ppermute | solution.py:542
  11.7 0.5 collective-permute-start.2
  12.3 2.0 %collective-permute-start.1 = (f32[512,128]{1,0:T(8,128)S(1)}, f32[512,128]{1,0:T(8,128)S(1)}, u32[]{:S(2)}, u32[]{:S(2)}) collective-permute-start(f32[512,128]{1,0:T(8,128)S(1)} %pad_maximum_fusion), channel_id=1, source_target_pairs={{0,64},{32,96},{64,0},{96,32},{128,192},{160,224},{192,128},{224,1... | collective-permute-start | bytes 786440 | tf_op jit(solution)/shard_map/ppermute | solution.py:542
  14.3 0.1 fusion.3
  14.4 0.1 pad_maximum_fusion.6.table_ref
  14.5 10.7 %collective-permute-done.3.refs_2_ = f32[512,128]{1,0:T(8,128)S(1)} collective-permute-done((f32[512,128]{1,0:T(8,128)S(1)}, f32[512,128]{1,0:T(8,128)S(1)}, u32[]{:S(2)}, u32[]{:S(2)}) %collective-permute-start.3) | collective-permute-done | bytes 262176 | tf_op jit(solution)/shard_map/ppermute | solution.py:542
  25.2 0.0 collective-permute-done.2.refs_1_
  25.2 0.5 collective-permute-done.1.refs_0_
  25.7 1.3 %shard_map.61 = (f32[1024,128]{1,0:T(8,128)S(1)}, f32[1024,128]{1,0:T(8,128)S(1)}) custom-call(f32[64,128]{1,0:T(8,128)S(1)} %pad_maximum_fusion.6.table_ref, f32[1024,128]{1,0:T(8,128)S(1)} %get-tuple-element.17.own_ref, f32[1024,128]{1,0:T(8,128)S(1)} %collective-permute-done.near_ref, f32[512,128]{1,0:T(8,128)S(1)} %collective-permute-done.1.refs_0_, ...), custom_call_target="tpu_custom_call" | custom-call | flops 100000000 | bytes 4194304 | tf_op jit(solution)/shard_map/pallas_call | solution.py:529
  27.0 1.6 %collective-permute-start.4 = (f32[1024,128]{1,0:T(8,128)S(1)}, f32[1024,128]{1,0:T(8,128)S(1)}, u32[]{:S(2)}, u32[]{:S(2)}) collective-permute-start(f32[1024,128]{1,0:T(8,128)S(1)} %get-tuple-element.25), channel_id=1, source_target_pairs={{0,32},{32,0},{64,96},{96,64},{128,160},{160,128},{192,224},{224,1... | collective-permute-start | bytes 1572872 | tf_op jit(solution)/shard_map/ppermute | solution.py:542
  28.5 2.6 %shard_map.60 = (f32[800,128]{1,0:T(8,128)}, f32[1024,128]{1,0:T(8,128)}) custom-call(s32[8,32]{1,0:T(8,128)} %bitcast.43, f32[1024,128]{1,0:T(8,128)S(1)} %get-tuple-element.14.rim_ref), custom_call_target="tpu_custom_call" | custom-call | flops 100000000 | bytes 4194304 | tf_op jit(solution)/shard_map/pallas_call | solution.py:529
  31.1 9.5 %all-to-all-start = ((f32[800,1,128]{2,1,0:T(1,128)}), f32[800,1,128]{2,1,0:T(1,128)S(1)}, u32[]{:S(2)}, u32[]{:S(2)}) async-start(f32[800,1,128]{2,1,0:T(1,128)} %bitcast.7), calls=%async_computation | async-start | bytes 819200 | tf_op jit(solution)/shard_map/all_to_all | solution.py:625
  40.6 0.0 collective-permute-done.4
  40.7 2.6 %collective-permute-start.7 = (f32[512,128]{1,0:T(8,128)S(1)}, f32[512,128]{1,0:T(8,128)S(1)}, u32[]{:S(2)}, u32[]{:S(2)}) collective-permute-start(f32[512,128]{1,0:T(8,128)S(1)} %pad_maximum_fusion.5), channel_id=1, source_target_pairs={{0,192},{32,224},{64,128},{96,160},{128,64},{160,96},{192,0},{224,... | collective-permute-start | bytes 786440 | tf_op jit(solution)/shard_map/ppermute | solution.py:542
  43.4 0.5 collective-permute-start.6
  43.9 0.3 collective-permute-start.5
  44.3 2.9 %shard_map.62 = (f32[8,64,128]{2,1,0:T(8,128)}, f32[8,64,128]{2,1,0:T(8,128)}, f32[8,32,128]{2,1,0:T(8,128)}, f32[8,16,128]{2,1,0:T(8,128)}) custom-call(s32[2,8]{1,0:T(2,128)} %bitcast.45), custom_call_target="tpu_custom_call" | custom-call | flops 100000000 | bytes 4194304 | tf_op jit(solution)/shard_map/pallas_call | solution.py:529
  47.2 8.2 %all-to-all-done = f32[800,1,128]{2,1,0:T(1,128)S(1)} async-done(((f32[800,1,128]{2,1,0:T(1,128)}), f32[800,1,128]{2,1,0:T(1,128)S(1)}, u32[]{:S(2)}, u32[]{:S(2)}) %all-to-all-start) | async-done | bytes 409632 | tf_op jit(solution)/shard_map/all_to_all | solution.py:625
  55.3 7.6 %shard_map.63 = f32[2048,128]{1,0:T(8,128)} custom-call(s32[1]{0:T(128)} %bitcast.mine_ref, s32[2,8]{1,0:T(2,128)} %bitcast.46, f32[800,128]{1,0:T(8,128)S(1)} %bitcast.32, f32[1024,128]{1,0:T(8,128)} %get-tuple-element.16.rim_hbm, f32[2048,128]{1,0:T(8,128)} %bitcast.39, f32[2048,128]{1,0:T(8,128)} %bitcast.41, f32[8,64,128]{2,1,0:T(8,128)} %get-tuple-element.21.col_hbm, ...), custom_call_target="tpu_custom_call" | custom-call | flops 100000000 | bytes 4194304 | tf_op jit(solution)/shard_map/pallas_call | solution.py:529
  62.9 0.0 collective-permute-done.7
  62.9 0.0 collective-permute-done.6
  62.9 0.0 collective-permute-done.5
  62.9 1.0 %shard_map.64 = f32[8,256,128]{2,1,0:T(8,128)} custom-call(s32[1]{0:T(128)} %bitcast.mine_ref, f32[32,32,128]{2,1,0:T(8,128)S(1)} %bitcast.33, f32[32,32,128]{2,1,0:T(8,128)S(1)} %bitcast.34, f32[16,32,128]{2,1,0:T(8,128)S(1)} %bitcast.37, f32[16,32,128]{2,1,0:T(8,128)S(1)} %bitcast.36, f32[16,32,128]{2,1,0:T(8,128)S(1)} %bitcast.35), custom_call_target="tpu_custom_call" | custom-call | flops 100000000 | bytes 4194304 | tf_op jit(solution)/shard_map/pallas_call | solution.py:529
  (14 shorter events, 0.2 us)
Async XLA Ops:
  5.9 4.8 %collective-permute-start = (f32[1024,128]{1,0:T(8,128)S(1)}, f32[1024,128]{1,0:T(8,128)S(1)}, u32[]{:S(2)}, u32[]{:S(2)}) collective-permute-start(f32[1024,128]{1,0:T(8,128)S(1)} %get-tuple-element.18), channel_id=1, source_target_pairs={{0,32},{32,0},{64,96},{96,64},{128,160},{160,128},{192,224},{224,1... | collective-permute-start | bytes 1572872 | tf_op jit(solution)/shard_map/ppermute | solution.py:542
  10.8 14.4 %collective-permute-start.3 = (f32[512,128]{1,0:T(8,128)S(1)}, f32[512,128]{1,0:T(8,128)S(1)}, u32[]{:S(2)}, u32[]{:S(2)}) collective-permute-start(f32[512,128]{1,0:T(8,128)S(1)} %pad_maximum_fusion.2), channel_id=1, source_target_pairs={{0,192},{32,224},{64,128},{96,160},{128,64},{160,96},{192,0},{224,... | collective-permute-start | bytes 786440 | tf_op jit(solution)/shard_map/ppermute | solution.py:542
  11.7 13.5 %collective-permute-start.2 = (f32[512,128]{1,0:T(8,128)S(1)}, f32[512,128]{1,0:T(8,128)S(1)}, u32[]{:S(2)}, u32[]{:S(2)}) collective-permute-start(f32[512,128]{1,0:T(8,128)S(1)} %pad_maximum_fusion.1), channel_id=1, source_target_pairs={{0,128},{32,160},{64,192},{96,224},{128,0},{160,32},{192,64},{224,... | collective-permute-start | bytes 786440 | tf_op jit(solution)/shard_map/ppermute | solution.py:542
  12.3 13.4 %collective-permute-start.1 = (f32[512,128]{1,0:T(8,128)S(1)}, f32[512,128]{1,0:T(8,128)S(1)}, u32[]{:S(2)}, u32[]{:S(2)}) collective-permute-start(f32[512,128]{1,0:T(8,128)S(1)} %pad_maximum_fusion), channel_id=1, source_target_pairs={{0,64},{32,96},{64,0},{96,32},{128,192},{160,224},{192,128},{224,1... | collective-permute-start | bytes 786440 | tf_op jit(solution)/shard_map/ppermute | solution.py:542
  27.0 13.7 %collective-permute-start.4 = (f32[1024,128]{1,0:T(8,128)S(1)}, f32[1024,128]{1,0:T(8,128)S(1)}, u32[]{:S(2)}, u32[]{:S(2)}) collective-permute-start(f32[1024,128]{1,0:T(8,128)S(1)} %get-tuple-element.25), channel_id=1, source_target_pairs={{0,32},{32,0},{64,96},{96,64},{128,160},{160,128},{192,224},{224,1... | collective-permute-start | bytes 1572872 | tf_op jit(solution)/shard_map/ppermute | solution.py:542
  31.1 24.2 %all-to-all-start = ((f32[800,1,128]{2,1,0:T(1,128)}), f32[800,1,128]{2,1,0:T(1,128)S(1)}, u32[]{:S(2)}, u32[]{:S(2)}) async-start(f32[800,1,128]{2,1,0:T(1,128)} %bitcast.7), calls=%async_computation | async-start | bytes 819200 | tf_op jit(solution)/shard_map/all_to_all | solution.py:625
  40.7 22.2 %collective-permute-start.7 = (f32[512,128]{1,0:T(8,128)S(1)}, f32[512,128]{1,0:T(8,128)S(1)}, u32[]{:S(2)}, u32[]{:S(2)}) collective-permute-start(f32[512,128]{1,0:T(8,128)S(1)} %pad_maximum_fusion.5), channel_id=1, source_target_pairs={{0,192},{32,224},{64,128},{96,160},{128,64},{160,96},{192,0},{224,... | collective-permute-start | bytes 786440 | tf_op jit(solution)/shard_map/ppermute | solution.py:542
  43.4 19.6 %collective-permute-start.6 = (f32[512,128]{1,0:T(8,128)S(1)}, f32[512,128]{1,0:T(8,128)S(1)}, u32[]{:S(2)}, u32[]{:S(2)}) collective-permute-start(f32[512,128]{1,0:T(8,128)S(1)} %pad_maximum_fusion.4), channel_id=1, source_target_pairs={{0,128},{32,160},{64,192},{96,224},{128,0},{160,32},{192,64},{224,... | collective-permute-start | bytes 786440 | tf_op jit(solution)/shard_map/ppermute | solution.py:542
  43.9 19.0 %collective-permute-start.5 = (f32[512,128]{1,0:T(8,128)S(1)}, f32[512,128]{1,0:T(8,128)S(1)}, u32[]{:S(2)}, u32[]{:S(2)}) collective-permute-start(f32[512,128]{1,0:T(8,128)S(1)} %pad_maximum_fusion.3), channel_id=1, source_target_pairs={{0,64},{32,96},{64,0},{96,32},{128,192},{160,224},{192,128},{224,1... | collective-permute-start | bytes 786440 | tf_op jit(solution)/shard_map/ppermute | solution.py:542

commit v3 on v2

--- a/solution.py
+++ b/solution.py
@@ -198,17 +198,19 @@
     odd = (odd_hi_ref, odd_lo_ref)
 
     def two(i, carry):
-        along_y(2 * i, *even)
-        along_x(jnp.maximum(2 * i - 1, 0), *odd, stage1_ref)
         along_y(2 * i + 1, *odd)
         along_x(2 * i, *even, stage0_ref)
+        along_y(jnp.minimum(2 * i + 2, holders - 1), *even)
+        along_x(2 * i + 1, *odd, stage1_ref)
         return carry
 
+    along_y(0, *even)
     lax.fori_loop(0, holders // 2, two, 0)
-    along_x(holders - 1, *odd, stage1_ref)
-
-
-def pack_kernel(planes, face_ref, rim_ref, pay_hbm, rim_hbm, used_ref, pay_ref, sems):
+
+
+def pack_kernel(planes, face_hbm, rim_ref, pay_hbm, rim_hbm, face_ref, used_ref, pay_ref, sems):
+    fetch = pltpu.make_async_copy(face_hbm, face_ref, sems.at[2])
+    fetch.start()
     keep = pltpu.make_async_copy(rim_ref, rim_hbm, sems.at[0])
     keep.start()
     pay_ref[...] = jnp.zeros_like(pay_ref)
@@ -218,7 +220,8 @@
         used_ref[t] = 0
         return carry
 
-    lax.fori_loop(0, targets, clear, 0)
+    lax.fori_loop(0, targets, clear, 0, unroll=8)
+    fetch.wait()
 
     lane = iota((planes, LANES), 1)
 
@@ -322,8 +325,6 @@
         pltpu.make_async_copy(now_hbm, now_ref, sems.at[5]),
         pltpu.make_async_copy(prev_hbm, prev_ref, sems.at[6]),
     ]
-    for copy in fetches:
-        copy.start()
     sources = got_ref.shape[0] // FACE_ROWS
     labels = got_ref[pl.ds(3 * planes, sources, stride=FACE_ROWS), :]
     place = iota((sources, LANES), 1)
@@ -332,38 +333,43 @@
     label_ref[...] = jnp.where(place == 0, first, second).astype(jnp.int32)
     to_scalars = pltpu.make_async_copy(label_ref, code_ref, sems.at[7])
     to_scalars.start()
+    for copy in fetches:
+        copy.start()
     sum_ref[...] = jnp.zeros_like(sum_ref)
     times_ref[...] = jnp.zeros_like(times_ref)
 
     to_scalars.wait()
 
-    def gather(k, carry):
-        code = code_ref[k >> 1, k & 1]
-
-        @pl.when(code > 0)
+    low = iota((RIM, LANES), 1) < B
+    row = iota((RIM, LANES), 0)
+
+    def gather(source, carry):
+        codes = (code_ref[source, 0], code_ref[source, 1])
+
+        @pl.when(codes[0] + codes[1] > 0)
         def _():
-            source = k >> 1
-            turn = (k & 1) * B
-            which = code - 1
-            tile = which >> 1
-            first = (which & 1) * 3
             base = source * FACE_ROWS
-            marks = got_ref[pl.ds(base + 3 * planes, 1), :]
-            marks = pltpu.roll(jnp.broadcast_to(marks, (RIM, LANES)), turn, 1)
-            here = (marks == code.astype(f32)) & (iota((RIM, LANES), 1) < B)
-            for j in range(3):
-                values = got_ref[pl.ds(base + j * planes, planes), :]
-                values = jnp.where(here, pltpu.roll(values, turn, 1), 0.0)
-                rows = pl.ds(tile * 64 + first + j, planes, stride=RIM)
-                sum_ref[rows, :] = sum_ref[rows, :] + values
-            row = iota((RIM, LANES), 0)
-            hit = here & (row >= first) & (row < first + 3)
-            rows = pl.ds(pl.multiple_of(tile * RIM, RIM), RIM)
-            times_ref[rows, :] = times_ref[rows, :] + jnp.where(hit, 1.0, 0.0)
+            marks = jnp.broadcast_to(got_ref[pl.ds(base + 3 * planes, 1), :], (RIM, LANES))
+            layers = [got_ref[pl.ds(base + j * planes, planes), :] for j in range(3)]
+            for slot in range(2):
+                code = codes[slot]
+                if slot == 1:
+                    marks = pltpu.roll(marks, B, 1)
+                    layers = [pltpu.roll(x, B, 1) for x in layers]
+                here = (marks == code.astype(f32)) & (marks > 0.0) & low
+                which = jnp.maximum(code - 1, 0)
+                tile = which >> 1
+                first = (which & 1) * 3
+                for j in range(3):
+                    rows = pl.ds(pl.multiple_of(tile * 64 + (first + j) * planes, 8), planes)
+                    sum_ref[rows, :] = sum_ref[rows, :] + jnp.where(here, layers[j], 0.0)
+                hit = here & (row >= first) & (row < first + 3)
+                rows = pl.ds(pl.multiple_of(tile * RIM, RIM), RIM)
+                times_ref[rows, :] = times_ref[rows, :] + jnp.where(hit, 1.0, 0.0)
 
         return carry
 
-    lax.fori_loop(0, 2 * sources, gather, 0)
+    lax.fori_loop(0, sources, gather, 0)
     first_plane = mine_ref[0] * planes
     lane = iota((32, LANES), 1)
     half = iota((RIM, LANES), 1) < B
@@ -374,7 +380,14 @@
             rows = pl.ds(pl.multiple_of((p * 2 + axis) * 64, 64), 64)
             times = times_ref[pl.ds(pl.multiple_of((p * 2 + axis) * RIM, RIM), RIM), :]
             times = jnp.concatenate([times] * planes, 0)
-            jumps.append(split(sum_ref[rows, :] - times * rim_ref[rows, :]))
+            came = jnp.concatenate(
+                [
+                    sum_ref[pl.ds((p * 2 + axis) * 64 + kz, RIM, stride=planes), :]
+                    for kz in range(planes)
+                ],
+                0,
+            )
+            jumps.append(split(came - times * rim_ref[rows, :]))
         j_hi, j_lo = jumps[0]
         c_hi, c_lo = split(jnp.concatenate([col_ref[p], jnp.zeros((B, LANES), f32)], 0))
         along_y = dot(
@@ -392,29 +405,35 @@
         for kz in range(planes):
             tile = along_y[kz * RIM : (kz + 1) * RIM]
             both = jnp.concatenate([jnp.where(half, tile, 0.0), jnp.where(half, 0.0, tile)], 0)
-            spot = slice(kz * 2 * RIM, (kz + 1) * 2 * RIM)
-            right_hi_ref[spot], right_lo_ref[spot] = split(both)
+            hi, lo = split(both)
+            right_hi_ref[:, kz * LANES : (kz + 1) * LANES] = hi
+            right_lo_ref[:, kz * LANES : (kz + 1) * LANES] = lo
 
     def finish(p, down_ref, right_hi_ref, right_lo_ref):
-        edge_hi, edge_lo = split(edge_row_ref[p])
-        down_hi, down_lo = split(down_ref[...])
+        edge = edge_row_ref[p]
+        edge_hi = edge.astype(bf16).astype(f32)
+        edge = jnp.where(lane < 4 * RIM, edge_hi, edge - edge_hi).astype(bf16)
+        right_hi = right_hi_ref[...]
+        across_x = dot(
+            edge[:, : 6 * RIM], jnp.concatenate([right_hi, right_lo_ref[...], right_hi], 0)
+        )
+        down = down_ref[...]
+        down_hi = down.astype(bf16).astype(f32)
+        down_lo = down - down_hi
         left_hi = []
         left_lo = []
         for kz in range(planes):
-            near = jnp.where(lane // 16 == kz, 1.0, 0.0).astype(bf16)
-            far = jnp.where((lane // RIM) % planes == kz, 1.0, 0.0).astype(bf16)
-            left_hi.append(jnp.concatenate([edge_hi * near, down_hi * far], 1))
-            left_lo.append(jnp.concatenate([edge_lo * near, down_lo * far], 1))
+            mine = (lane // RIM) % planes == kz
+            left_hi.append(jnp.where(mine, down_hi, 0.0).astype(bf16))
+            left_lo.append(jnp.where(mine, down_lo, 0.0).astype(bf16))
         left_hi = jnp.concatenate(left_hi, 0)
         left_lo = jnp.concatenate(left_lo, 0)
         edges = edge_col_ref[p]
         edges = jnp.concatenate([edges[:RIM]] * planes + [edges[RIM:]] * planes, 0)
         edges_hi, edges_lo = split(edges)
-        right_hi = jnp.concatenate([right_hi_ref[...], edges_hi], 0)
-        right_lo = jnp.concatenate([right_lo_ref[...], edges_lo], 0)
-        force = dot(
+        across_y = dot(
             jnp.concatenate([left_hi, left_hi, left_lo], 1),
-            jnp.concatenate([right_hi, right_lo, right_hi], 0),
+            jnp.concatenate([edges_hi, edges_lo, edges_hi], 0),
         )
         ex = box_ref[0, p]
         ey = box_ref[1, p]
@@ -433,24 +452,25 @@
                 s = s * u + f32(c)
             rows = pl.ds(kz * 256 + p, 32, stride=8)
             new = (2.0 - u * s) * now_ref[rows, :] - prev_ref[rows, :]
-            new = new + s * (force[kz * 32 : (kz + 1) * 32] * (TIME_STEP * TIME_STEP))
+            force = across_x[:, kz * LANES : (kz + 1) * LANES] + across_y[kz * 32 : (kz + 1) * 32]
+            new = new + s * (force * (TIME_STEP * TIME_STEP))
             out_ref[rows, :] = jnp.where(inside, new, 0.0)
 
     def two(i, carry):
-        faces(2 * i, *even)
-        finish(jnp.maximum(2 * i - 1, 0), *odd)
         faces(2 * i + 1, *odd)
         finish(2 * i, *even)
+        faces(jnp.minimum(2 * i + 2, holders - 1), *even)
+        finish(2 * i + 1, *odd)
         return carry
 
-    for copy in fetches:
-        copy.wait()
     even = (even_down_ref, even_hi_ref, even_lo_ref)
     odd = (odd_down_ref, odd_hi_ref, odd_lo_ref)
-    for ref in odd:
-        ref[...] = jnp.zeros_like(ref)
+    for copy in fetches[:5]:
+        copy.wait()
+    faces(0, *even)
+    for copy in fetches[5:]:
+        copy.wait()
     lax.fori_loop(0, holders // 2, two, 0)
-    finish(holders - 1, *odd)
 
 
 def tables_kernel(box_ref, *refs):
@@ -611,12 +631,13 @@
     pay, rim = call(
         functools.partial(pack_kernel, planes),
         (face_rows, rim),
-        [SM, VM],
+        [HB, VM],
         (rows(domains * FACE_ROWS), pltpu.HBM((holders * 128, LANES), f32)),
         [
+            pltpu.SMEM(face_rows.shape, jnp.int32),
             pltpu.SMEM((domains,), jnp.int32),
             pltpu.VMEM((domains * FACE_ROWS, LANES), f32),
-            pltpu.SemaphoreType.DMA((2,)),
+            pltpu.SemaphoreType.DMA((3,)),
         ],
         spot=HB,
     )
@@ -675,8 +696,8 @@
         ]
         + [
             pltpu.VMEM((32, LANES), f32),
-            pltpu.VMEM((LANES, LANES), bf16),
-            pltpu.VMEM((LANES, LANES), bf16),
+            pltpu.VMEM((2 * RIM, planes * LANES), bf16),
+            pltpu.VMEM((2 * RIM, planes * LANES), bf16),
         ]
         * 2
         + [pltpu.SemaphoreType.DMA((8,))],

time: 64.8 us -> 63.6 us (0.981)
  Pallas kernels: 20.6 us -> 19.4 us
    pallas_call x6, Pallas kernels: 20.6 us -> 19.4 us  [call(): pl.pallas_call(kernel, out_shape=outs, in_specs=spots, out_specs=tuple(sp...]
  transfers between devices with their start and end apart: 9 -> 9, of which waited for: 4 -> 4; matrix products, arithmetic and copies ran while one was open for 1% -> 1% of each run, Pallas kernels for 20% -> 19%
where the time goes in v3:
time: 63.6 us; the launch traced here: 62.8 us
  starting transfers between devices  21.4 us (34%)
  waiting for transfers between devices  20.6 us (32%)
  Pallas kernels  19.4 us (31%)
  between operations  0.79 us (1%)
    pallas_call x6, Pallas kernels, call(): pl.pallas_call(kernel, out_shape=outs, in_specs=spots, out_specs=tuple(sp...  19.4 us
    ppermute x8, waiting for transfers between devices, swap(): return lax.ppermute(block, 'height', [(i, i ^ step) for i in range(count)])  12.5 us
    ppermute x8, starting transfers between devices, swap(): return lax.ppermute(block, 'height', [(i, i ^ step) for i in range(count)])  11.9 us
    all_to_all x1, starting transfers between devices, step(): arrived = lax.all_to_all(pay.reshape(-1, 1, LANES), 'dom', 0, 0, tiled=True)  9.52 us
    all_to_all x1, waiting for transfers between devices, step(): arrived = lax.all_to_all(pay.reshape(-1, 1, LANES), 'dom', 0, 0, tiled=True)  8.16 us
  transfers between devices with their start and end apart: 9, of which 4 were waited for; matrix products, arithmetic and copies ran while one was open for 1% of the time, Pallas kernels for 19%

profile of v3, /device:TPU:1, one launch (start us, length us, event | category | flops | bytes accessed | tf_op | source)
XLA Modules:
  0.0 62.8 jit_solution(1543274512362109238)
XLA Ops:
  0.6 5.3 %shard_map.59 = (f32[1024,128]{1,0:T(8,128)S(1)}, f32[1024,128]{1,0:T(8,128)S(1)}, f32[1024,128]{1,0:T(8,128)S(1)}) custom-call(s32[1]{0:T(128)} %bitcast.mine_ref, s32[2,8]{1,0:T(2,128)} %bitcast.44, f32[2048,128]{1,0:T(8,128)} %bitcast.38), custom_call_target="tpu_custom_call" | custom-call | flops 100000000 | bytes 4194304 | tf_op jit(solution)/shard_map/pallas_call | solution.py:549
  6.0 3.3 %collective-permute-start = (f32[1024,128]{1,0:T(8,128)S(1)}, f32[1024,128]{1,0:T(8,128)S(1)}, u32[]{:S(2)}, u32[]{:S(2)}) collective-permute-start(f32[1024,128]{1,0:T(8,128)S(1)} %get-tuple-element.18), channel_id=1, source_target_pairs={{0,32},{32,0},{64,96},{96,64},{128,160},{160,128},{192,224},{224,1... | collective-permute-start | bytes 1572872 | tf_op jit(solution)/shard_map/ppermute | solution.py:562
  9.3 0.1 iota_add_fusion
  9.4 0.1 add.88
  9.5 1.3 %collective-permute-done.near_ref = f32[1024,128]{1,0:T(8,128)S(1)} collective-permute-done((f32[1024,128]{1,0:T(8,128)S(1)}, f32[1024,128]{1,0:T(8,128)S(1)}, u32[]{:S(2)}, u32[]{:S(2)}) %collective-permute-start) | collective-permute-done | bytes 524320 | tf_op jit(solution)/shard_map/ppermute | solution.py:562
  10.9 0.9 %collective-permute-start.3 = (f32[512,128]{1,0:T(8,128)S(1)}, f32[512,128]{1,0:T(8,128)S(1)}, u32[]{:S(2)}, u32[]{:S(2)}) collective-permute-start(f32[512,128]{1,0:T(8,128)S(1)} %pad_maximum_fusion.2), channel_id=1, source_target_pairs={{0,192},{32,224},{64,128},{96,160},{128,64},{160,96},{192,0},{224,... | collective-permute-start | bytes 786440 | tf_op jit(solution)/shard_map/ppermute | solution.py:562
  11.8 0.5 collective-permute-start.2
  12.4 2.0 %collective-permute-start.1 = (f32[512,128]{1,0:T(8,128)S(1)}, f32[512,128]{1,0:T(8,128)S(1)}, u32[]{:S(2)}, u32[]{:S(2)}) collective-permute-start(f32[512,128]{1,0:T(8,128)S(1)} %pad_maximum_fusion), channel_id=1, source_target_pairs={{0,64},{32,96},{64,0},{96,32},{128,192},{160,224},{192,128},{224,1... | collective-permute-start | bytes 786440 | tf_op jit(solution)/shard_map/ppermute | solution.py:562
  14.4 0.1 fusion.3
  14.5 0.1 pad_maximum_fusion.6.table_ref
  14.6 10.7 %collective-permute-done.3.refs_2_ = f32[512,128]{1,0:T(8,128)S(1)} collective-permute-done((f32[512,128]{1,0:T(8,128)S(1)}, f32[512,128]{1,0:T(8,128)S(1)}, u32[]{:S(2)}, u32[]{:S(2)}) %collective-permute-start.3) | collective-permute-done | bytes 262176 | tf_op jit(solution)/shard_map/ppermute | solution.py:562
  25.3 0.0 collective-permute-done.2.refs_1_
  25.3 0.5 collective-permute-done.1.refs_0_
  25.8 1.3 %shard_map.61 = (f32[1024,128]{1,0:T(8,128)S(1)}, f32[1024,128]{1,0:T(8,128)S(1)}) custom-call(f32[64,128]{1,0:T(8,128)S(1)} %pad_maximum_fusion.6.table_ref, f32[1024,128]{1,0:T(8,128)S(1)} %get-tuple-element.17.own_ref, f32[1024,128]{1,0:T(8,128)S(1)} %collective-permute-done.near_ref, f32[512,128]{1,0:T(8,128)S(1)} %collective-permute-done.1.refs_0_, ...), custom_call_target="tpu_custom_call" | custom-call | flops 100000000 | bytes 4194304 | tf_op jit(solution)/shard_map/pallas_call | solution.py:549
  27.1 1.6 %collective-permute-start.4 = (f32[1024,128]{1,0:T(8,128)S(1)}, f32[1024,128]{1,0:T(8,128)S(1)}, u32[]{:S(2)}, u32[]{:S(2)}) collective-permute-start(f32[1024,128]{1,0:T(8,128)S(1)} %get-tuple-element.25), channel_id=1, source_target_pairs={{0,32},{32,0},{64,96},{96,64},{128,160},{160,128},{192,224},{224,1... | collective-permute-start | bytes 1572872 | tf_op jit(solution)/shard_map/ppermute | solution.py:562
  28.6 2.3 %shard_map.60 = (f32[800,128]{1,0:T(8,128)}, f32[1024,128]{1,0:T(8,128)}) custom-call(s32[8,32]{1,0:T(8,128)} %bitcast.43, f32[1024,128]{1,0:T(8,128)S(1)} %get-tuple-element.14.rim_ref), custom_call_target="tpu_custom_call" | custom-call | flops 100000000 | bytes 4194304 | tf_op jit(solution)/shard_map/pallas_call | solution.py:549
  31.0 9.5 %all-to-all-start = ((f32[800,1,128]{2,1,0:T(1,128)}), f32[800,1,128]{2,1,0:T(1,128)S(1)}, u32[]{:S(2)}, u32[]{:S(2)}) async-start(f32[800,1,128]{2,1,0:T(1,128)} %bitcast.7), calls=%async_computation | async-start | bytes 819200 | tf_op jit(solution)/shard_map/all_to_all | solution.py:646
  40.5 0.0 collective-permute-done.4
  40.6 2.6 %collective-permute-start.7 = (f32[512,128]{1,0:T(8,128)S(1)}, f32[512,128]{1,0:T(8,128)S(1)}, u32[]{:S(2)}, u32[]{:S(2)}) collective-permute-start(f32[512,128]{1,0:T(8,128)S(1)} %pad_maximum_fusion.5), channel_id=1, source_target_pairs={{0,192},{32,224},{64,128},{96,160},{128,64},{160,96},{192,0},{224,... | collective-permute-start | bytes 786440 | tf_op jit(solution)/shard_map/ppermute | solution.py:562
  43.3 0.5 collective-permute-start.6
  43.8 0.3 collective-permute-start.5
  44.2 2.9 %shard_map.62 = (f32[8,64,128]{2,1,0:T(8,128)}, f32[8,64,128]{2,1,0:T(8,128)}, f32[8,32,128]{2,1,0:T(8,128)}, f32[8,16,128]{2,1,0:T(8,128)}) custom-call(s32[2,8]{1,0:T(2,128)} %bitcast.45), custom_call_target="tpu_custom_call" | custom-call | flops 100000000 | bytes 4194304 | tf_op jit(solution)/shard_map/pallas_call | solution.py:549
  47.1 8.2 %all-to-all-done = f32[800,1,128]{2,1,0:T(1,128)S(1)} async-done(((f32[800,1,128]{2,1,0:T(1,128)}), f32[800,1,128]{2,1,0:T(1,128)S(1)}, u32[]{:S(2)}, u32[]{:S(2)}) %all-to-all-start) | async-done | bytes 409632 | tf_op jit(solution)/shard_map/all_to_all | solution.py:646
  55.2 6.5 %shard_map.63 = f32[2048,128]{1,0:T(8,128)} custom-call(s32[1]{0:T(128)} %bitcast.mine_ref, s32[2,8]{1,0:T(2,128)} %bitcast.46, f32[800,128]{1,0:T(8,128)S(1)} %bitcast.32, f32[1024,128]{1,0:T(8,128)} %get-tuple-element.16.rim_hbm, f32[2048,128]{1,0:T(8,128)} %bitcast.39, f32[2048,128]{1,0:T(8,128)} %bitcast.41, f32[8,64,128]{2,1,0:T(8,128)} %get-tuple-element.21.col_hbm, ...), custom_call_target="tpu_custom_call" | custom-call | flops 100000000 | bytes 4194304 | tf_op jit(solution)/shard_map/pallas_call | solution.py:549
  61.8 0.0 collective-permute-done.7
  61.8 0.0 collective-permute-done.6
  61.8 0.0 collective-permute-done.5
  61.8 1.0 %shard_map.64 = f32[8,256,128]{2,1,0:T(8,128)} custom-call(s32[1]{0:T(128)} %bitcast.mine_ref, f32[32,32,128]{2,1,0:T(8,128)S(1)} %bitcast.33, f32[32,32,128]{2,1,0:T(8,128)S(1)} %bitcast.34, f32[16,32,128]{2,1,0:T(8,128)S(1)} %bitcast.37, f32[16,32,128]{2,1,0:T(8,128)S(1)} %bitcast.36, f32[16,32,128]{2,1,0:T(8,128)S(1)} %bitcast.35), custom_call_target="tpu_custom_call" | custom-call | flops 100000000 | bytes 4194304 | tf_op jit(solution)/shard_map/pallas_call | solution.py:549
  (14 shorter events, 0.2 us)
Async XLA Ops:
  6.0 4.8 %collective-permute-start = (f32[1024,128]{1,0:T(8,128)S(1)}, f32[1024,128]{1,0:T(8,128)S(1)}, u32[]{:S(2)}, u32[]{:S(2)}) collective-permute-start(f32[1024,128]{1,0:T(8,128)S(1)} %get-tuple-element.18), channel_id=1, source_target_pairs={{0,32},{32,0},{64,96},{96,64},{128,160},{160,128},{192,224},{224,1... | collective-permute-start | bytes 1572872 | tf_op jit(solution)/shard_map/ppermute | solution.py:562
  10.9 14.4 %collective-permute-start.3 = (f32[512,128]{1,0:T(8,128)S(1)}, f32[512,128]{1,0:T(8,128)S(1)}, u32[]{:S(2)}, u32[]{:S(2)}) collective-permute-start(f32[512,128]{1,0:T(8,128)S(1)} %pad_maximum_fusion.2), channel_id=1, source_target_pairs={{0,192},{32,224},{64,128},{96,160},{128,64},{160,96},{192,0},{224,... | collective-permute-start | bytes 786440 | tf_op jit(solution)/shard_map/ppermute | solution.py:562
  11.8 13.5 %collective-permute-start.2 = (f32[512,128]{1,0:T(8,128)S(1)}, f32[512,128]{1,0:T(8,128)S(1)}, u32[]{:S(2)}, u32[]{:S(2)}) collective-permute-start(f32[512,128]{1,0:T(8,128)S(1)} %pad_maximum_fusion.1), channel_id=1, source_target_pairs={{0,128},{32,160},{64,192},{96,224},{128,0},{160,32},{192,64},{224,... | collective-permute-start | bytes 786440 | tf_op jit(solution)/shard_map/ppermute | solution.py:562
  12.4 13.4 %collective-permute-start.1 = (f32[512,128]{1,0:T(8,128)S(1)}, f32[512,128]{1,0:T(8,128)S(1)}, u32[]{:S(2)}, u32[]{:S(2)}) collective-permute-start(f32[512,128]{1,0:T(8,128)S(1)} %pad_maximum_fusion), channel_id=1, source_target_pairs={{0,64},{32,96},{64,0},{96,32},{128,192},{160,224},{192,128},{224,1... | collective-permute-start | bytes 786440 | tf_op jit(solution)/shard_map/ppermute | solution.py:562
  27.1 13.5 %collective-permute-start.4 = (f32[1024,128]{1,0:T(8,128)S(1)}, f32[1024,128]{1,0:T(8,128)S(1)}, u32[]{:S(2)}, u32[]{:S(2)}) collective-permute-start(f32[1024,128]{1,0:T(8,128)S(1)} %get-tuple-element.25), channel_id=1, source_target_pairs={{0,32},{32,0},{64,96},{96,64},{128,160},{160,128},{192,224},{224,1... | collective-permute-start | bytes 1572872 | tf_op jit(solution)/shard_map/ppermute | solution.py:562
  31.0 24.2 %all-to-all-start = ((f32[800,1,128]{2,1,0:T(1,128)}), f32[800,1,128]{2,1,0:T(1,128)S(1)}, u32[]{:S(2)}, u32[]{:S(2)}) async-start(f32[800,1,128]{2,1,0:T(1,128)} %bitcast.7), calls=%async_computation | async-start | bytes 819200 | tf_op jit(solution)/shard_map/all_to_all | solution.py:646
  40.6 21.2 %collective-permute-start.7 = (f32[512,128]{1,0:T(8,128)S(1)}, f32[512,128]{1,0:T(8,128)S(1)}, u32[]{:S(2)}, u32[]{:S(2)}) collective-permute-start(f32[512,128]{1,0:T(8,128)S(1)} %pad_maximum_fusion.5), channel_id=1, source_target_pairs={{0,192},{32,224},{64,128},{96,160},{128,64},{160,96},{192,0},{224,... | collective-permute-start | bytes 786440 | tf_op jit(solution)/shard_map/ppermute | solution.py:562
  43.3 18.5 %collective-permute-start.6 = (f32[512,128]{1,0:T(8,128)S(1)}, f32[512,128]{1,0:T(8,128)S(1)}, u32[]{:S(2)}, u32[]{:S(2)}) collective-permute-start(f32[512,128]{1,0:T(8,128)S(1)} %pad_maximum_fusion.4), channel_id=1, source_target_pairs={{0,128},{32,160},{64,192},{96,224},{128,0},{160,32},{192,64},{224,... | collective-permute-start | bytes 786440 | tf_op jit(solution)/shard_map/ppermute | solution.py:562
  43.8 18.0 %collective-permute-start.5 = (f32[512,128]{1,0:T(8,128)S(1)}, f32[512,128]{1,0:T(8,128)S(1)}, u32[]{:S(2)}, u32[]{:S(2)}) collective-permute-start(f32[512,128]{1,0:T(8,128)S(1)} %pad_maximum_fusion.3), channel_id=1, source_target_pairs={{0,64},{32,96},{64,0},{96,32},{128,192},{160,224},{192,128},{224,1... | collective-permute-start | bytes 786440 | tf_op jit(solution)/shard_map/ppermute | solution.py:562

commit v4 on v3

--- a/solution.py
+++ b/solution.py
@@ -87,8 +87,10 @@
     mine_ref,
     box_ref,
     x_hbm,
-    even_ref,
-    odd_ref,
+    piece0_ref,
+    piece1_ref,
+    piece2_ref,
+    piece3_ref,
     rim_ref,
     x_ref,
     stage0_ref,
@@ -105,6 +107,7 @@
     sem,
 ):
     mine = mine_ref[0]
+    piece_refs = (piece0_ref, piece1_ref, piece2_ref, piece3_ref)
     holders = box_ref.shape[1]
     fetch = pltpu.make_async_copy(x_hbm, x_ref, sem)
     fetch.start()
@@ -183,8 +186,8 @@
             out = jnp.where(low32, tile[:32], tile[32:64])
             stage_ref[kz * 32 : (kz + 1) * 32, :] = out
             for s in range(8):
-                spot = (s // 2) * 256 + kz * 32 + p
-                (even_ref, odd_ref)[s % 2][pl.ds(spot, 4, stride=8), :] = stage_ref[
+                spot = (s % 2) * 256 + kz * 32 + p
+                piece_refs[s // 2][pl.ds(spot, 4, stride=8), :] = stage_ref[
                     pl.ds(kz * 32 + (mine ^ s) * 4, 4), :
                 ]
             rim_ref[pl.ds(pl.multiple_of(p * 128 + kz * RIM, RIM), RIM), :] = jnp.where(
@@ -253,11 +256,12 @@
     send.wait()
 
 
-def depth_kernel(planes, table_ref, own_ref, near_ref, *refs):
-    far, outs = refs[:-2], refs[-2:]
-    count = 2 + 2 * len(far)
+def depth_kernel(planes, table_ref, *refs):
+    ins, outs = refs[:-2], refs[-2:]
+    chips = len(ins) // 2
+    count = 2 * chips
     size = 32 * planes
-    blocks = [(own_ref, 0), (near_ref, 0)] + [(r, i * size) for r in far for i in range(2)]
+    blocks = [(ins[s // 2 + (s % 2) * chips], 0) for s in range(count)]
     total = count * planes
     t_hi, t_lo = split(table_ref[...])
     t_lo = jnp.where(iota((total, LANES), 1) < total, t_lo, jnp.zeros_like(t_lo))
@@ -607,11 +611,11 @@
         return jax.ShapeDtypeStruct((n, LANES), f32)
 
     half = 1024
-    even, odd, rim = call(
+    *pieces, rim = call(
         functools.partial(cells_kernel, planes),
         (mine_word, boxes, now),
         [SM, SM, HB],
-        (rows(half), rows(half), rows(holders * 128)),
+        (rows(half // 2),) * 4 + (rows(holders * 128),),
         [
             pltpu.VMEM((2048, LANES), f32),
             pltpu.VMEM((32 * planes, LANES), f32),
@@ -641,9 +645,10 @@
         ],
         spot=HB,
     )
-    near = swap(odd, 1)
-    far = across(even, near)
+    far = [swap(pieces[t], 2 * t) for t in range(1, 4)]
     arrived = lax.all_to_all(pay.reshape(-1, 1, LANES), "dom", 0, 0, tiled=True)
+
+    near = [swap(x[half // 4 :], 1) for x in (pieces[0], *far)]
 
     order = (mine ^ jnp.arange(count, dtype=jnp.int32))[:, None] * planes
     order = (order + jnp.arange(planes, dtype=jnp.int32)).reshape(-1)
@@ -651,8 +656,8 @@
     depth_table = jnp.concatenate([depth_table, depth_table], 1)
     mixed = call(
         functools.partial(depth_kernel, planes),
-        (depth_table, even, near, *far),
-        [VM] * (3 + len(far)),
+        (depth_table, pieces[0], *far, *near),
+        [VM] * (2 + len(far) + len(near)),
         (rows(half),) * 2,
     )
     back_near = swap(mixed[1], 1)

time: 63.6 us -> 65.1 us (1.024)
  starting transfers between devices: 21.4 us -> 31.1 us
  waiting for transfers between devices: 20.6 us -> 13 us
    ppermute x8 -> x11, starting transfers between devices: 11.9 us -> 19.9 us  [swap(): return lax.ppermute(block, 'height', [(i, i ^ step) for i in range(count)])]
    ppermute x8 -> x11, waiting for transfers between devices: 12.5 us -> 4.91 us  [swap(): return lax.ppermute(block, 'height', [(i, i ^ step) for i in range(count)])]
    all_to_all x1, starting transfers between devices: 9.52 us -> 11.2 us  [step(): arrived = lax.all_to_all(pay.reshape(-1, 1, LANES), 'dom', 0, 0, tiled=True)]
  transfers between devices with their start and end apart: 9 -> 12, of which waited for: 4 -> 4; matrix products, arithmetic and copies ran while one was open for 1% -> 1% of each run, Pallas kernels for 19% -> 18%
where the time goes in v4:
time: 65.1 us; the launch traced here: 64.8 us
  starting transfers between devices  31.1 us (48%)
  Pallas kernels  19.4 us (30%)
  waiting for transfers between devices  13 us (20%)
  between operations  0.81 us (1%)
    ppermute x11, starting transfers between devices, swap(): return lax.ppermute(block, 'height', [(i, i ^ step) for i in range(count)])  19.9 us
    pallas_call x6, Pallas kernels, call(): pl.pallas_call(kernel, out_shape=outs, in_specs=spots, out_specs=tuple(sp...  19.4 us
    all_to_all x1, starting transfers between devices, step(): arrived = lax.all_to_all(pay.reshape(-1, 1, LANES), 'dom', 0, 0, tiled=True)  11.2 us
    all_to_all x1, waiting for transfers between devices, step(): arrived = lax.all_to_all(pay.reshape(-1, 1, LANES), 'dom', 0, 0, tiled=True)  8.04 us
    ppermute x11, waiting for transfers between devices, swap(): return lax.ppermute(block, 'height', [(i, i ^ step) for i in range(count)])  4.91 us
  transfers between devices with their start and end apart: 12, of which 4 were waited for; matrix products, arithmetic and copies ran while one was open for 1% of the time, Pallas kernels for 18%

profile of v4, /device:TPU:1, one launch (start us, length us, event | category | flops | bytes accessed | tf_op | source)
XLA Modules:
  0.0 64.8 jit_solution(1659208326403971862)
XLA Ops:
  0.6 5.4 %shard_map.59 = (f32[512,128]{1,0:T(8,128)S(1)}, f32[512,128]{1,0:T(8,128)S(1)}, f32[512,128]{1,0:T(8,128)S(1)}, f32[512,128]{1,0:T(8,128)S(1)}, f32[1024,128]{1,0:T(8,128)S(1)}) custom-call(s32[1]{0:T(128)} %bitcast.mine_ref, s32[2,8]{1,0:T(2,128)} %bitcast.44, f32[2048,128]{1,0:T(8,128)} %bitcast.38), custom_call_target="tpu_custom_call" | custom-call | flops 100000000 | bytes 4194304 | tf_op jit(solution)/shard_map/pallas_call | solution.py:553
  6.0 2.1 %collective-permute-start = (f32[512,128]{1,0:T(8,128)S(1)}, f32[512,128]{1,0:T(8,128)S(1)}, u32[]{:S(2)}, u32[]{:S(2)}) collective-permute-start(f32[512,128]{1,0:T(8,128)S(1)} %get-tuple-element.20), channel_id=1, source_target_pairs={{0,64},{32,96},{64,0},{96,32},{128,192},{160,224},{192,128},{224,1... | collective-permute-start | bytes 786440 | tf_op jit(solution)/shard_map/ppermute | solution.py:566
  8.1 2.5 %collective-permute-start.1 = (f32[512,128]{1,0:T(8,128)S(1)}, f32[512,128]{1,0:T(8,128)S(1)}, u32[]{:S(2)}, u32[]{:S(2)}) collective-permute-start(f32[512,128]{1,0:T(8,128)S(1)} %get-tuple-element.21), channel_id=1, source_target_pairs={{0,128},{32,160},{64,192},{96,224},{128,0},{160,32},{192,64},{224,... | collective-permute-start | bytes 786440 | tf_op jit(solution)/shard_map/ppermute | solution.py:566
  10.6 0.0 collective-permute-start.2
  10.6 3.4 %collective-permute-start.3 = (f32[256,128]{1,0:T(8,128)S(1)}, f32[256,128]{1,0:T(8,128)S(1)}, u32[]{:S(2)}, u32[]{:S(2)}) collective-permute-start(f32[256,128]{1,0:T(8,128)S(1)} %slice.30), channel_id=1, source_target_pairs={{0,32},{32,0},{64,96},{96,64},{128,160},{160,128},{192,224},{224,1... | collective-permute-start | bytes 393224 | tf_op jit(solution)/shard_map/ppermute | solution.py:566
  14.1 0.1 iota_add_fusion
  14.2 0.1 add.88
  14.3 0.0 collective-permute-done.refs_1_
  14.3 4.0 %collective-permute-start.4 = (f32[256,128]{1,0:T(8,128)S(1)}, f32[256,128]{1,0:T(8,128)S(1)}, u32[]{:S(2)}, u32[]{:S(2)}) collective-permute-start(f32[256,128]{1,0:T(8,128)S(1)} %slice.40), channel_id=1, source_target_pairs={{0,32},{32,0},{64,96},{96,64},{128,160},{160,128},{192,224},{224,1... | collective-permute-start | bytes 393224 | tf_op jit(solution)/shard_map/ppermute | solution.py:566
  18.3 3.7 %collective-permute-done.1.refs_2_ = f32[512,128]{1,0:T(8,128)S(1)} collective-permute-done((f32[512,128]{1,0:T(8,128)S(1)}, f32[512,128]{1,0:T(8,128)S(1)}, u32[]{:S(2)}, u32[]{:S(2)}) %collective-permute-start.1) | collective-permute-done | bytes 262176 | tf_op jit(solution)/shard_map/ppermute | solution.py:566
  22.0 1.7 %collective-permute-start.5 = (f32[256,128]{1,0:T(8,128)S(1)}, f32[256,128]{1,0:T(8,128)S(1)}, u32[]{:S(2)}, u32[]{:S(2)}) collective-permute-start(f32[256,128]{1,0:T(8,128)S(1)} %slice.41), channel_id=1, source_target_pairs={{0,32},{32,0},{64,96},{96,64},{128,160},{160,128},{192,224},{224,1... | collective-permute-start | bytes 393224 | tf_op jit(solution)/shard_map/ppermute | solution.py:566
  23.7 0.4 collective-permute-done.2.refs_3_
  24.1 2.2 %collective-permute-start.6 = (f32[256,128]{1,0:T(8,128)S(1)}, f32[256,128]{1,0:T(8,128)S(1)}, u32[]{:S(2)}, u32[]{:S(2)}) collective-permute-start(f32[256,128]{1,0:T(8,128)S(1)} %slice.42), channel_id=1, source_target_pairs={{0,32},{32,0},{64,96},{96,64},{128,160},{160,128},{192,224},{224,1... | collective-permute-start | bytes 393224 | tf_op jit(solution)/shard_map/ppermute | solution.py:566
  26.3 0.1 fusion.3
  26.4 0.1 pad_maximum_fusion.3.table_ref
  26.5 0.0 collective-permute-done.3.refs_4_
  26.5 0.0 collective-permute-done.4.refs_5_
  26.5 0.0 collective-permute-done.5.refs_6_
  26.5 0.8 %collective-permute-done.6.refs_7_ = f32[256,128]{1,0:T(8,128)S(1)} collective-permute-done((f32[256,128]{1,0:T(8,128)S(1)}, f32[256,128]{1,0:T(8,128)S(1)}, u32[]{:S(2)}, u32[]{:S(2)}) %collective-permute-start.6) | collective-permute-done | bytes 131104 | tf_op jit(solution)/shard_map/ppermute | solution.py:566
  27.3 1.3 %shard_map.61 = (f32[1024,128]{1,0:T(8,128)S(1)}, f32[1024,128]{1,0:T(8,128)S(1)}) custom-call(f32[64,128]{1,0:T(8,128)S(1)} %pad_maximum_fusion.3.table_ref, f32[512,128]{1,0:T(8,128)S(1)} %get-tuple-element.19.refs_0_, f32[512,128]{1,0:T(8,128)S(1)} %collective-permute-done.refs_1_, f32[512,128]{1,0:T(8,128)S(1)} %collective-permute-done.1.refs_2_, ...), custom_call_target="tpu_custom_call" | custom-call | flops 100000000 | bytes 4194304 | tf_op jit(solution)/shard_map/pallas_call | solution.py:553
  28.6 0.4 collective-permute-start.7
  29.0 2.3 %shard_map.60 = (f32[800,128]{1,0:T(8,128)}, f32[1024,128]{1,0:T(8,128)}) custom-call(s32[8,32]{1,0:T(8,128)} %bitcast.43, f32[1024,128]{1,0:T(8,128)S(1)} %get-tuple-element.16.rim_ref), custom_call_target="tpu_custom_call" | custom-call | flops 100000000 | bytes 4194304 | tf_op jit(solution)/shard_map/pallas_call | solution.py:553
  31.4 11.2 %all-to-all-start = ((f32[800,1,128]{2,1,0:T(1,128)}), f32[800,1,128]{2,1,0:T(1,128)S(1)}, u32[]{:S(2)}, u32[]{:S(2)}) async-start(f32[800,1,128]{2,1,0:T(1,128)} %bitcast.7), calls=%async_computation | async-start | bytes 819200 | tf_op jit(solution)/shard_map/all_to_all | solution.py:649
  42.6 0.0 collective-permute-done.7
  42.7 0.2 collective-permute-start.10
  42.9 0.4 collective-permute-start.9
  43.4 2.9 %collective-permute-start.8 = (f32[512,128]{1,0:T(8,128)S(1)}, f32[512,128]{1,0:T(8,128)S(1)}, u32[]{:S(2)}, u32[]{:S(2)}) collective-permute-start(f32[512,128]{1,0:T(8,128)S(1)} %pad_maximum_fusion), channel_id=1, source_target_pairs={{0,64},{32,96},{64,0},{96,32},{128,192},{160,224},{192,128},{224,1... | collective-permute-start | bytes 786440 | tf_op jit(solution)/shard_map/ppermute | solution.py:566
  46.3 2.9 %shard_map.62 = (f32[8,64,128]{2,1,0:T(8,128)}, f32[8,64,128]{2,1,0:T(8,128)}, f32[8,32,128]{2,1,0:T(8,128)}, f32[8,16,128]{2,1,0:T(8,128)}) custom-call(s32[2,8]{1,0:T(2,128)} %bitcast.45), custom_call_target="tpu_custom_call" | custom-call | flops 100000000 | bytes 4194304 | tf_op jit(solution)/shard_map/pallas_call | solution.py:553
  49.1 8.0 %all-to-all-done = f32[800,1,128]{2,1,0:T(1,128)S(1)} async-done(((f32[800,1,128]{2,1,0:T(1,128)}), f32[800,1,128]{2,1,0:T(1,128)S(1)}, u32[]{:S(2)}, u32[]{:S(2)}) %all-to-all-start) | async-done | bytes 409632 | tf_op jit(solution)/shard_map/all_to_all | solution.py:649
  57.2 6.6 %shard_map.63 = f32[2048,128]{1,0:T(8,128)} custom-call(s32[1]{0:T(128)} %bitcast.mine_ref, s32[2,8]{1,0:T(2,128)} %bitcast.46, f32[800,128]{1,0:T(8,128)S(1)} %bitcast.32, f32[1024,128]{1,0:T(8,128)} %get-tuple-element.18.rim_hbm, f32[2048,128]{1,0:T(8,128)} %bitcast.39, f32[2048,128]{1,0:T(8,128)} %bitcast.41, f32[8,64,128]{2,1,0:T(8,128)} %get-tuple-element.25.col_hbm, ...), custom_call_target="tpu_custom_call" | custom-call | flops 100000000 | bytes 4194304 | tf_op jit(solution)/shard_map/pallas_call | solution.py:553
  63.7 0.0 collective-permute-done.10
  63.8 0.0 collective-permute-done.9
  63.8 0.0 collective-permute-done.8
  63.8 1.0 %shard_map.64 = f32[8,256,128]{2,1,0:T(8,128)} custom-call(s32[1]{0:T(128)} %bitcast.mine_ref, f32[32,32,128]{2,1,0:T(8,128)S(1)} %bitcast.33, f32[32,32,128]{2,1,0:T(8,128)S(1)} %bitcast.34, f32[16,32,128]{2,1,0:T(8,128)S(1)} %bitcast.37, f32[16,32,128]{2,1,0:T(8,128)S(1)} %bitcast.36, f32[16,32,128]{2,1,0:T(8,128)S(1)} %bitcast.35), custom_call_target="tpu_custom_call" | custom-call | flops 100000000 | bytes 4194304 | tf_op jit(solution)/shard_map/pallas_call | solution.py:553
  (13 shorter events, 0.2 us)
Async XLA Ops:
  6.0 8.3 %collective-permute-start = (f32[512,128]{1,0:T(8,128)S(1)}, f32[512,128]{1,0:T(8,128)S(1)}, u32[]{:S(2)}, u32[]{:S(2)}) collective-permute-start(f32[512,128]{1,0:T(8,128)S(1)} %get-tuple-element.20), channel_id=1, source_target_pairs={{0,64},{32,96},{64,0},{96,32},{128,192},{160,224},{192,128},{224,1... | collective-permute-start | bytes 786440 | tf_op jit(solution)/shard_map/ppermute | solution.py:566
  8.1 13.9 %collective-permute-start.1 = (f32[512,128]{1,0:T(8,128)S(1)}, f32[512,128]{1,0:T(8,128)S(1)}, u32[]{:S(2)}, u32[]{:S(2)}) collective-permute-start(f32[512,128]{1,0:T(8,128)S(1)} %get-tuple-element.21), channel_id=1, source_target_pairs={{0,128},{32,160},{64,192},{96,224},{128,0},{160,32},{192,64},{224,... | collective-permute-start | bytes 786440 | tf_op jit(solution)/shard_map/ppermute | solution.py:566
  10.6 13.5 %collective-permute-start.2 = (f32[512,128]{1,0:T(8,128)S(1)}, f32[512,128]{1,0:T(8,128)S(1)}, u32[]{:S(2)}, u32[]{:S(2)}) collective-permute-start(f32[512,128]{1,0:T(8,128)S(1)} %get-tuple-element.22), channel_id=1, source_target_pairs={{0,192},{32,224},{64,128},{96,160},{128,64},{160,96},{192,0},{224,... | collective-permute-start | bytes 786440 | tf_op jit(solution)/shard_map/ppermute | solution.py:566
  10.6 15.8 %collective-permute-start.3 = (f32[256,128]{1,0:T(8,128)S(1)}, f32[256,128]{1,0:T(8,128)S(1)}, u32[]{:S(2)}, u32[]{:S(2)}) collective-permute-start(f32[256,128]{1,0:T(8,128)S(1)} %slice.30), channel_id=1, source_target_pairs={{0,32},{32,0},{64,96},{96,64},{128,160},{160,128},{192,224},{224,1... | collective-permute-start | bytes 393224 | tf_op jit(solution)/shard_map/ppermute | solution.py:566
  14.3 12.2 %collective-permute-start.4 = (f32[256,128]{1,0:T(8,128)S(1)}, f32[256,128]{1,0:T(8,128)S(1)}, u32[]{:S(2)}, u32[]{:S(2)}) collective-permute-start(f32[256,128]{1,0:T(8,128)S(1)} %slice.40), channel_id=1, source_target_pairs={{0,32},{32,0},{64,96},{96,64},{128,160},{160,128},{192,224},{224,1... | collective-permute-start | bytes 393224 | tf_op jit(solution)/shard_map/ppermute | solution.py:566
  22.0 4.5 %collective-permute-start.5 = (f32[256,128]{1,0:T(8,128)S(1)}, f32[256,128]{1,0:T(8,128)S(1)}, u32[]{:S(2)}, u32[]{:S(2)}) collective-permute-start(f32[256,128]{1,0:T(8,128)S(1)} %slice.41), channel_id=1, source_target_pairs={{0,32},{32,0},{64,96},{96,64},{128,160},{160,128},{192,224},{224,1... | collective-permute-start | bytes 393224 | tf_op jit(solution)/shard_map/ppermute | solution.py:566
  24.1 3.2 %collective-permute-start.6 = (f32[256,128]{1,0:T(8,128)S(1)}, f32[256,128]{1,0:T(8,128)S(1)}, u32[]{:S(2)}, u32[]{:S(2)}) collective-permute-start(f32[256,128]{1,0:T(8,128)S(1)} %slice.42), channel_id=1, source_target_pairs={{0,32},{32,0},{64,96},{96,64},{128,160},{160,128},{192,224},{224,1... | collective-permute-start | bytes 393224 | tf_op jit(solution)/shard_map/ppermute | solution.py:566
  28.6 14.1 %collective-permute-start.7 = (f32[1024,128]{1,0:T(8,128)S(1)}, f32[1024,128]{1,0:T(8,128)S(1)}, u32[]{:S(2)}, u32[]{:S(2)}) collective-permute-start(f32[1024,128]{1,0:T(8,128)S(1)} %get-tuple-element.29), channel_id=1, source_target_pairs={{0,32},{32,0},{64,96},{96,64},{128,160},{160,128},{192,224},{224,1... | collective-permute-start | bytes 1572872 | tf_op jit(solution)/shard_map/ppermute | solution.py:566
  31.4 25.8 %all-to-all-start = ((f32[800,1,128]{2,1,0:T(1,128)}), f32[800,1,128]{2,1,0:T(1,128)S(1)}, u32[]{:S(2)}, u32[]{:S(2)}) async-start(f32[800,1,128]{2,1,0:T(1,128)} %bitcast.7), calls=%async_computation | async-start | bytes 819200 | tf_op jit(solution)/shard_map/all_to_all | solution.py:649
  42.7 21.1 %collective-permute-start.10 = (f32[512,128]{1,0:T(8,128)S(1)}, f32[512,128]{1,0:T(8,128)S(1)}, u32[]{:S(2)}, u32[]{:S(2)}) collective-permute-start(f32[512,128]{1,0:T(8,128)S(1)} %pad_maximum_fusion.2), channel_id=1, source_target_pairs={{0,192},{32,224},{64,128},{96,160},{128,64},{160,96},{192,0},{224,... | collective-permute-start | bytes 786440 | tf_op jit(solution)/shard_map/ppermute | solution.py:566
  42.9 20.8 %collective-permute-start.9 = (f32[512,128]{1,0:T(8,128)S(1)}, f32[512,128]{1,0:T(8,128)S(1)}, u32[]{:S(2)}, u32[]{:S(2)}) collective-permute-start(f32[512,128]{1,0:T(8,128)S(1)} %pad_maximum_fusion.1), channel_id=1, source_target_pairs={{0,128},{32,160},{64,192},{96,224},{128,0},{160,32},{192,64},{224,... | collective-permute-start | bytes 786440 | tf_op jit(solution)/shard_map/ppermute | solution.py:566
  43.4 20.4 %collective-permute-start.8 = (f32[512,128]{1,0:T(8,128)S(1)}, f32[512,128]{1,0:T(8,128)S(1)}, u32[]{:S(2)}, u32[]{:S(2)}) collective-permute-start(f32[512,128]{1,0:T(8,128)S(1)} %pad_maximum_fusion), channel_id=1, source_target_pairs={{0,64},{32,96},{64,0},{96,32},{128,192},{160,224},{192,128},{224,1... | collective-permute-start | bytes 786440 | tf_op jit(solution)/shard_map/ppermute | solution.py:566

commit v5 on v4

--- a/solution.py
+++ b/solution.py
@@ -566,19 +566,6 @@
     return lax.ppermute(block, "height", [(i, i ^ step) for i in range(count)])
 
 
-def across(blocks, near):
-    size = blocks.shape[0] // 4
-    return [
-        swap(
-            jnp.concatenate(
-                [blocks[t * size : (t + 1) * size], near[t * size : (t + 1) * size]], 0
-            ),
-            2 * t,
-        )
-        for t in range(1, 4)
-    ]
-
-
 def in_hbm(x):
     return pltpu.with_memory_space_constraint(x, pltpu.HBM)
 
@@ -660,8 +647,13 @@
         [VM] * (2 + len(far) + len(near)),
         (rows(half),) * 2,
     )
-    back_near = swap(mixed[1], 1)
-    back_far = across(mixed[0], back_near)
+    part = half // 4
+    cuts = [slice(t * part, (t + 1) * part) for t in range(4)]
+    back_near = [swap(mixed[1][cut], 1) for cut in cuts]
+    back_far = [
+        swap(jnp.concatenate([mixed[0][cuts[t]], back_near[t]], 0), 2 * t)
+        for t in range(1, 4)
+    ]
 
     later, _ = lax.optimization_barrier((boxes, mixed[0]))
     tables = call(
@@ -709,7 +701,7 @@
     )
     pressure = call(
         functools.partial(join_kernel, planes),
-        (mine_word, *[b.reshape(-1, 32, LANES) for b in (mixed[0], back_near, *back_far)]),
+        (mine_word, *[b.reshape(-1, 32, LANES) for b in (mixed[0], back_near[0], *back_far)]),
         [SM] + [VM] * (2 + len(back_far)),
         jax.ShapeDtypeStruct((planes, 256, LANES), f32),
         [pltpu.SemaphoreType.DMA((count,))],

time: 65.1 us -> 57.4 us (0.88)
  starting transfers between devices: 31.1 us -> 24.9 us
  waiting for transfers between devices: 13 us -> 11.4 us
    all_to_all x1, waiting for transfers between devices: 8.04 us -> 0.01 us  [step(): arrived = lax.all_to_all(pay.reshape(-1, 1, LANES), 'dom', 0, 0, tiled=True)]
    ppermute x11 -> x14, waiting for transfers between devices: 4.91 us -> 11.4 us  [swap(): return lax.ppermute(block, 'height', [(i, i ^ step) for i in range(count)])]
    ppermute x11 -> x14, starting transfers between devices: 19.9 us -> 15.4 us  [swap(): return lax.ppermute(block, 'height', [(i, i ^ step) for i in range(count)])]
    all_to_all x1, starting transfers between devices: 11.2 us -> 9.51 us  [step(): arrived = lax.all_to_all(pay.reshape(-1, 1, LANES), 'dom', 0, 0, tiled=True)]
  transfers between devices with their start and end apart: 12 -> 15, of which waited for: 4 -> 6; matrix products, arithmetic and copies ran while one was open for 1% -> 1% of each run, Pallas kernels for 18% -> 13%
where the time goes in v5:
time: 57.4 us; the launch traced here: 57.1 us
  starting transfers between devices  24.9 us (43%)
  Pallas kernels  19.4 us (34%)
  waiting for transfers between devices  11.4 us (20%)
  between operations  0.82 us (1%)
    pallas_call x6, Pallas kernels, call(): pl.pallas_call(kernel, out_shape=outs, in_specs=spots, out_specs=tuple(sp...  19.4 us
    ppermute x14, starting transfers between devices, swap(): return lax.ppermute(block, 'height', [(i, i ^ step) for i in range(count)])  15.4 us
    ppermute x14, waiting for transfers between devices, swap(): return lax.ppermute(block, 'height', [(i, i ^ step) for i in range(count)])  11.4 us
    all_to_all x1, starting transfers between devices, step(): arrived = lax.all_to_all(pay.reshape(-1, 1, LANES), 'dom', 0, 0, tiled=True)  9.51 us
  transfers between devices with their start and end apart: 15, of which 6 were waited for; matrix products, arithmetic and copies ran while one was open for 1% of the time, Pallas kernels for 13%

profile of v5, /device:TPU:1, one launch (start us, length us, event | category | flops | bytes accessed | tf_op | source)
XLA Modules:
  0.0 57.1 jit_solution(16492711088954664160)
XLA Ops:
  0.6 5.4 %shard_map.59 = (f32[512,128]{1,0:T(8,128)S(1)}, f32[512,128]{1,0:T(8,128)S(1)}, f32[512,128]{1,0:T(8,128)S(1)}, f32[512,128]{1,0:T(8,128)S(1)}, f32[1024,128]{1,0:T(8,128)S(1)}) custom-call(s32[1]{0:T(128)} %bitcast.mine_ref, s32[2,8]{1,0:T(2,128)} %bitcast.44, f32[2048,128]{1,0:T(8,128)} %bitcast.38), custom_call_target="tpu_custom_call" | custom-call | flops 100000000 | bytes 4194304 | tf_op jit(solution)/shard_map/pallas_call | solution.py:553
  6.0 3.3 %collective-permute-start.3 = (f32[256,128]{1,0:T(8,128)S(1)}, f32[256,128]{1,0:T(8,128)S(1)}, u32[]{:S(2)}, u32[]{:S(2)}) collective-permute-start(f32[256,128]{1,0:T(8,128)S(1)} %slice.33), channel_id=1, source_target_pairs={{0,32},{32,0},{64,96},{96,64},{128,160},{160,128},{192,224},{224,1... | collective-permute-start | bytes 393224 | tf_op jit(solution)/shard_map/ppermute | solution.py:566
  9.3 0.0 collective-permute-start
  9.3 2.0 %collective-permute-start.1 = (f32[512,128]{1,0:T(8,128)S(1)}, f32[512,128]{1,0:T(8,128)S(1)}, u32[]{:S(2)}, u32[]{:S(2)}) collective-permute-start(f32[512,128]{1,0:T(8,128)S(1)} %get-tuple-element.21), channel_id=1, source_target_pairs={{0,128},{32,160},{64,192},{96,224},{128,0},{160,32},{192,64},{224,... | collective-permute-start | bytes 786440 | tf_op jit(solution)/shard_map/ppermute | solution.py:566
  11.3 1.8 %collective-permute-start.2 = (f32[512,128]{1,0:T(8,128)S(1)}, f32[512,128]{1,0:T(8,128)S(1)}, u32[]{:S(2)}, u32[]{:S(2)}) collective-permute-start(f32[512,128]{1,0:T(8,128)S(1)} %get-tuple-element.22), channel_id=1, source_target_pairs={{0,192},{32,224},{64,128},{96,160},{128,64},{160,96},{192,0},{224,... | collective-permute-start | bytes 786440 | tf_op jit(solution)/shard_map/ppermute | solution.py:566
  13.2 2.3 %shard_map.60 = (f32[800,128]{1,0:T(8,128)}, f32[1024,128]{1,0:T(8,128)}) custom-call(s32[8,32]{1,0:T(8,128)} %bitcast.43, f32[1024,128]{1,0:T(8,128)S(1)} %get-tuple-element.16.rim_ref), custom_call_target="tpu_custom_call" | custom-call | flops 100000000 | bytes 4194304 | tf_op jit(solution)/shard_map/pallas_call | solution.py:553
  15.5 9.5 %all-to-all-start = ((f32[800,1,128]{2,1,0:T(1,128)}), f32[800,1,128]{2,1,0:T(1,128)S(1)}, u32[]{:S(2)}, u32[]{:S(2)}) async-start(f32[800,1,128]{2,1,0:T(1,128)} %bitcast.7), calls=%async_computation | async-start | bytes 819200 | tf_op jit(solution)/shard_map/all_to_all | solution.py:636
  25.0 0.1 iota_add_fusion
  25.1 0.1 add.88
  25.2 0.0 collective-permute-done.refs_1_
  25.3 1.3 %collective-permute-start.4 = (f32[256,128]{1,0:T(8,128)S(1)}, f32[256,128]{1,0:T(8,128)S(1)}, u32[]{:S(2)}, u32[]{:S(2)}) collective-permute-start(f32[256,128]{1,0:T(8,128)S(1)} %slice.44), channel_id=1, source_target_pairs={{0,32},{32,0},{64,96},{96,64},{128,160},{160,128},{192,224},{224,1... | collective-permute-start | bytes 393224 | tf_op jit(solution)/shard_map/ppermute | solution.py:566
  26.6 0.0 collective-permute-done.1.refs_2_
  26.6 0.1 collective-permute-start.5
  26.7 0.0 collective-permute-done.2.refs_3_
  26.7 0.6 %collective-permute-start.6 = (f32[256,128]{1,0:T(8,128)S(1)}, f32[256,128]{1,0:T(8,128)S(1)}, u32[]{:S(2)}, u32[]{:S(2)}) collective-permute-start(f32[256,128]{1,0:T(8,128)S(1)} %slice.46), channel_id=1, source_target_pairs={{0,32},{32,0},{64,96},{96,64},{128,160},{160,128},{192,224},{224,1... | collective-permute-start | bytes 393224 | tf_op jit(solution)/shard_map/ppermute | solution.py:566
  27.3 0.1 fusion.3
  27.4 0.1 pad_maximum_fusion.3.table_ref
  27.5 0.0 collective-permute-done.3.refs_4_
  27.5 0.1 collective-permute-done.4.refs_5_
  27.6 0.5 collective-permute-done.5.refs_6_
  28.0 0.3 collective-permute-done.6.refs_7_
  28.3 1.3 %shard_map.61 = (f32[1024,128]{1,0:T(8,128)S(1)}, f32[1024,128]{1,0:T(8,128)S(1)}) custom-call(f32[64,128]{1,0:T(8,128)S(1)} %pad_maximum_fusion.3.table_ref, f32[512,128]{1,0:T(8,128)S(1)} %get-tuple-element.19.refs_0_, f32[512,128]{1,0:T(8,128)S(1)} %collective-permute-done.refs_1_, f32[512,128]{1,0:T(8,128)S(1)} %collective-permute-done.1.refs_2_, ...), custom_call_target="tpu_custom_call" | custom-call | flops 100000000 | bytes 4194304 | tf_op jit(solution)/shard_map/pallas_call | solution.py:553
  29.6 0.4 collective-permute-start.12
  30.1 0.1 collective-permute-start.10
  30.2 0.4 collective-permute-start.8
  30.6 1.0 %collective-permute-done.8 = f32[256,128]{1,0:T(8,128)S(1)} collective-permute-done((f32[256,128]{1,0:T(8,128)S(1)}, f32[256,128]{1,0:T(8,128)S(1)}, u32[]{:S(2)}, u32[]{:S(2)}) %collective-permute-start.8) | collective-permute-done | bytes 131104 | tf_op jit(solution)/shard_map/ppermute | solution.py:566
  31.6 0.1 collective-permute-start.9
  31.7 0.0 collective-permute-done.10
  31.7 3.8 %collective-permute-start.11 = (f32[512,128]{1,0:T(8,128)S(1)}, f32[512,128]{1,0:T(8,128)S(1)}, u32[]{:S(2)}, u32[]{:S(2)}) collective-permute-start(f32[512,128]{1,0:T(8,128)S(1)} %pad_maximum_fusion.1), channel_id=1, source_target_pairs={{0,128},{32,160},{64,192},{96,224},{128,0},{160,32},{192,64},{224,... | collective-permute-start | bytes 786440 | tf_op jit(solution)/shard_map/ppermute | solution.py:566
  35.5 0.0 collective-permute-done.12
  35.6 0.2 collective-permute-start.13
  35.8 1.2 %collective-permute-start.7 = (f32[256,128]{1,0:T(8,128)S(1)}, f32[256,128]{1,0:T(8,128)S(1)}, u32[]{:S(2)}, u32[]{:S(2)}) collective-permute-start(f32[256,128]{1,0:T(8,128)S(1)} %get-tuple-element.36), channel_id=1, source_target_pairs={{0,32},{32,0},{64,96},{96,64},{128,160},{160,128},{192,224},{224,1... | collective-permute-start | bytes 393224 | tf_op jit(solution)/shard_map/ppermute | solution.py:566
  36.9 2.9 %shard_map.62 = (f32[8,64,128]{2,1,0:T(8,128)}, f32[8,64,128]{2,1,0:T(8,128)}, f32[8,32,128]{2,1,0:T(8,128)}, f32[8,16,128]{2,1,0:T(8,128)}) custom-call(s32[2,8]{1,0:T(2,128)} %bitcast.45), custom_call_target="tpu_custom_call" | custom-call | flops 100000000 | bytes 4194304 | tf_op jit(solution)/shard_map/pallas_call | solution.py:553
  39.8 0.0 collective-permute-done.7
  39.8 0.0 collective-permute-done.9
  39.8 7.3 %collective-permute-done.11 = f32[512,128]{1,0:T(8,128)S(1)} collective-permute-done((f32[512,128]{1,0:T(8,128)S(1)}, f32[512,128]{1,0:T(8,128)S(1)}, u32[]{:S(2)}, u32[]{:S(2)}) %collective-permute-start.11) | collective-permute-done | bytes 262176 | tf_op jit(solution)/shard_map/ppermute | solution.py:566
  47.2 2.3 %collective-permute-done.13 = f32[512,128]{1,0:T(8,128)S(1)} collective-permute-done((f32[512,128]{1,0:T(8,128)S(1)}, f32[512,128]{1,0:T(8,128)S(1)}, u32[]{:S(2)}, u32[]{:S(2)}) %collective-permute-start.13) | collective-permute-done | bytes 262176 | tf_op jit(solution)/shard_map/ppermute | solution.py:566
  49.5 1.0 %shard_map.64 = f32[8,256,128]{2,1,0:T(8,128)} custom-call(s32[1]{0:T(128)} %bitcast.mine_ref, f32[32,32,128]{2,1,0:T(8,128)S(1)} %bitcast.33, f32[8,32,128]{2,1,0:T(8,128)S(1)} %bitcast.37, f32[16,32,128]{2,1,0:T(8,128)S(1)} %bitcast.34, f32[16,32,128]{2,1,0:T(8,128)S(1)} %bitcast.35, f32[16,32,128]{2,1,0:T(8,128)S(1)} %bitcast.36), custom_call_target="tpu_custom_call" | custom-call | flops 100000000 | bytes 4194304 | tf_op jit(solution)/shard_map/pallas_call | solution.py:553
  50.5 0.0 all-to-all-done
  50.5 6.6 %shard_map.63 = f32[2048,128]{1,0:T(8,128)} custom-call(s32[1]{0:T(128)} %bitcast.mine_ref, s32[2,8]{1,0:T(2,128)} %bitcast.46, f32[800,128]{1,0:T(8,128)S(1)} %bitcast.32, f32[1024,128]{1,0:T(8,128)} %get-tuple-element.18.rim_hbm, f32[2048,128]{1,0:T(8,128)} %bitcast.39, f32[2048,128]{1,0:T(8,128)} %bitcast.41, f32[8,64,128]{2,1,0:T(8,128)} %get-tuple-element.25.col_hbm, ...), custom_call_target="tpu_custom_call" | custom-call | flops 100000000 | bytes 4194304 | tf_op jit(solution)/shard_map/pallas_call | solution.py:553
  (13 shorter events, 0.2 us)
Async XLA Ops:
  6.0 21.5 %collective-permute-start.3 = (f32[256,128]{1,0:T(8,128)S(1)}, f32[256,128]{1,0:T(8,128)S(1)}, u32[]{:S(2)}, u32[]{:S(2)}) collective-permute-start(f32[256,128]{1,0:T(8,128)S(1)} %slice.33), channel_id=1, source_target_pairs={{0,32},{32,0},{64,96},{96,64},{128,160},{160,128},{192,224},{224,1... | collective-permute-start | bytes 393224 | tf_op jit(solution)/shard_map/ppermute | solution.py:566
  9.3 15.9 %collective-permute-start = (f32[512,128]{1,0:T(8,128)S(1)}, f32[512,128]{1,0:T(8,128)S(1)}, u32[]{:S(2)}, u32[]{:S(2)}) collective-permute-start(f32[512,128]{1,0:T(8,128)S(1)} %get-tuple-element.20), channel_id=1, source_target_pairs={{0,64},{32,96},{64,0},{96,32},{128,192},{160,224},{192,128},{224,1... | collective-permute-start | bytes 786440 | tf_op jit(solution)/shard_map/ppermute | solution.py:566
  9.3 17.3 %collective-permute-start.1 = (f32[512,128]{1,0:T(8,128)S(1)}, f32[512,128]{1,0:T(8,128)S(1)}, u32[]{:S(2)}, u32[]{:S(2)}) collective-permute-start(f32[512,128]{1,0:T(8,128)S(1)} %get-tuple-element.21), channel_id=1, source_target_pairs={{0,128},{32,160},{64,192},{96,224},{128,0},{160,32},{192,64},{224,... | collective-permute-start | bytes 786440 | tf_op jit(solution)/shard_map/ppermute | solution.py:566
  11.3 15.4 %collective-permute-start.2 = (f32[512,128]{1,0:T(8,128)S(1)}, f32[512,128]{1,0:T(8,128)S(1)}, u32[]{:S(2)}, u32[]{:S(2)}) collective-permute-start(f32[512,128]{1,0:T(8,128)S(1)} %get-tuple-element.22), channel_id=1, source_target_pairs={{0,192},{32,224},{64,128},{96,160},{128,64},{160,96},{192,0},{224,... | collective-permute-start | bytes 786440 | tf_op jit(solution)/shard_map/ppermute | solution.py:566
  15.5 35.0 %all-to-all-start = ((f32[800,1,128]{2,1,0:T(1,128)}), f32[800,1,128]{2,1,0:T(1,128)S(1)}, u32[]{:S(2)}, u32[]{:S(2)}) async-start(f32[800,1,128]{2,1,0:T(1,128)} %bitcast.7), calls=%async_computation | async-start | bytes 819200 | tf_op jit(solution)/shard_map/all_to_all | solution.py:636
  25.3 2.3 %collective-permute-start.4 = (f32[256,128]{1,0:T(8,128)S(1)}, f32[256,128]{1,0:T(8,128)S(1)}, u32[]{:S(2)}, u32[]{:S(2)}) collective-permute-start(f32[256,128]{1,0:T(8,128)S(1)} %slice.44), channel_id=1, source_target_pairs={{0,32},{32,0},{64,96},{96,64},{128,160},{160,128},{192,224},{224,1... | collective-permute-start | bytes 393224 | tf_op jit(solution)/shard_map/ppermute | solution.py:566
  26.6 1.4 %collective-permute-start.5 = (f32[256,128]{1,0:T(8,128)S(1)}, f32[256,128]{1,0:T(8,128)S(1)}, u32[]{:S(2)}, u32[]{:S(2)}) collective-permute-start(f32[256,128]{1,0:T(8,128)S(1)} %slice.45), channel_id=1, source_target_pairs={{0,32},{32,0},{64,96},{96,64},{128,160},{160,128},{192,224},{224,1... | collective-permute-start | bytes 393224 | tf_op jit(solution)/shard_map/ppermute | solution.py:566
  26.7 1.6 %collective-permute-start.6 = (f32[256,128]{1,0:T(8,128)S(1)}, f32[256,128]{1,0:T(8,128)S(1)}, u32[]{:S(2)}, u32[]{:S(2)}) collective-permute-start(f32[256,128]{1,0:T(8,128)S(1)} %slice.46), channel_id=1, source_target_pairs={{0,32},{32,0},{64,96},{96,64},{128,160},{160,128},{192,224},{224,1... | collective-permute-start | bytes 393224 | tf_op jit(solution)/shard_map/ppermute | solution.py:566
  29.6 6.0 %collective-permute-start.12 = (f32[256,128]{1,0:T(8,128)S(1)}, f32[256,128]{1,0:T(8,128)S(1)}, u32[]{:S(2)}, u32[]{:S(2)}) collective-permute-start(f32[256,128]{1,0:T(8,128)S(1)} %get-tuple-element.33), channel_id=1, source_target_pairs={{0,32},{32,0},{64,96},{96,64},{128,160},{160,128},{192,224},{224,1... | collective-permute-start | bytes 393224 | tf_op jit(solution)/shard_map/ppermute | solution.py:566
  30.1 1.7 %collective-permute-start.10 = (f32[256,128]{1,0:T(8,128)S(1)}, f32[256,128]{1,0:T(8,128)S(1)}, u32[]{:S(2)}, u32[]{:S(2)}) collective-permute-start(f32[256,128]{1,0:T(8,128)S(1)} %get-tuple-element.34), channel_id=1, source_target_pairs={{0,32},{32,0},{64,96},{96,64},{128,160},{160,128},{192,224},{224,1... | collective-permute-start | bytes 393224 | tf_op jit(solution)/shard_map/ppermute | solution.py:566
  30.2 1.4 %collective-permute-start.8 = (f32[256,128]{1,0:T(8,128)S(1)}, f32[256,128]{1,0:T(8,128)S(1)}, u32[]{:S(2)}, u32[]{:S(2)}) collective-permute-start(f32[256,128]{1,0:T(8,128)S(1)} %get-tuple-element.35), channel_id=1, source_target_pairs={{0,32},{32,0},{64,96},{96,64},{128,160},{160,128},{192,224},{224,1... | collective-permute-start | bytes 393224 | tf_op jit(solution)/shard_map/ppermute | solution.py:566
  31.6 8.2 %collective-permute-start.9 = (f32[512,128]{1,0:T(8,128)S(1)}, f32[512,128]{1,0:T(8,128)S(1)}, u32[]{:S(2)}, u32[]{:S(2)}) collective-permute-start(f32[512,128]{1,0:T(8,128)S(1)} %pad_maximum_fusion), channel_id=1, source_target_pairs={{0,64},{32,96},{64,0},{96,32},{128,192},{160,224},{192,128},{224,1... | collective-permute-start | bytes 786440 | tf_op jit(solution)/shard_map/ppermute | solution.py:566
  31.7 15.4 %collective-permute-start.11 = (f32[512,128]{1,0:T(8,128)S(1)}, f32[512,128]{1,0:T(8,128)S(1)}, u32[]{:S(2)}, u32[]{:S(2)}) collective-permute-start(f32[512,128]{1,0:T(8,128)S(1)} %pad_maximum_fusion.1), channel_id=1, source_target_pairs={{0,128},{32,160},{64,192},{96,224},{128,0},{160,32},{192,64},{224,... | collective-permute-start | bytes 786440 | tf_op jit(solution)/shard_map/ppermute | solution.py:566
  35.6 13.9 %collective-permute-start.13 = (f32[512,128]{1,0:T(8,128)S(1)}, f32[512,128]{1,0:T(8,128)S(1)}, u32[]{:S(2)}, u32[]{:S(2)}) collective-permute-start(f32[512,128]{1,0:T(8,128)S(1)} %pad_maximum_fusion.2), channel_id=1, source_target_pairs={{0,192},{32,224},{64,128},{96,160},{128,64},{160,96},{192,0},{224,... | collective-permute-start | bytes 786440 | tf_op jit(solution)/shard_map/ppermute | solution.py:566
  35.8 4.0 %collective-permute-start.7 = (f32[256,128]{1,0:T(8,128)S(1)}, f32[256,128]{1,0:T(8,128)S(1)}, u32[]{:S(2)}, u32[]{:S(2)}) collective-permute-start(f32[256,128]{1,0:T(8,128)S(1)} %get-tuple-element.36), channel_id=1, source_target_pairs={{0,32},{32,0},{64,96},{96,64},{128,160},{160,128},{192,224},{224,1... | collective-permute-start | bytes 393224 | tf_op jit(solution)/shard_map/ppermute | solution.py:566
